TPU v7x, 32 devices: a whole 2x2x4 slice. The times are simulated.
32 devices in a mesh: cells: 16 (over z, y, core), waves: 2 (over x).
Axes of the slice: x: 2, y: 2, z: 4, core: 2. Of those that a mesh axis runs over, the one named last changes fastest.
Arguments:
- features: bfloat16 [32768, 512], P('cells', 'waves'), may hold values from -6 to 6
- positions: float32 [3, 32768], P(None, 'cells'), may hold values from 0 to 256, as said below
- occupancy: int32 [256], P('cells'), may hold values from 1 to 128, as said below
- neighbours: int32 [256, 3], P('cells'), may hold values from -2 to 2, as said below
- wavevectors: float32 [3, 4096], P(None, 'waves'), may hold values from -1 to 1
- filters: float32 [4096, 512], P('waves'), may hold values from -6 to 6
- falloffs: float32 [4], replicated, may hold values from 0.05 to 2
- mixing: float32 [4, 512], replicated, may hold values from -2 to 2
- norm_gain: float32 [512], replicated, may hold values from 0.5 to 1.5
- in_weight: bfloat16 [512, 1024], P(None, 'waves'), may hold values from -0.25 to 0.25
- out_weight: bfloat16 [1024, 512], P('waves'), may hold values from -0.1875 to 0.1875
Outputs:
- result: bfloat16 [32768, 512], P('cells', 'waves')
Inputs may be any that keep to these rules, and one draw needn't show every extreme that they name: `occupancy`: the atoms of a cell fill its first slots; the last cell is full. `neighbours`: each row holds 3 distinct offsets; cell c interacts with cells c + offset modulo 256. `positions`: the first coordinate of an atom in cell c lies in [c, c + 1]; the other two lie in [0, 3].
All inputs are finite; a program needn't handle non-finite values.
Results may differ from a plain program's by a relative error of at most 0.009.
Values may be sent and summed in bfloat16 or wider, within the bound.
No kernel may reach another device: no remote copies, remote signals or barrier semaphores. Data moves between devices by JAX's collectives and lax.ppermute only.
A program may use at most 128 MiB of HBM per device.

v0:
```python
import math

import jax
import jax.numpy as jnp
from jax import lax
from jax.sharding import PartitionSpec as P

K = 4096
HW = 2


EPS = 1e-06


def extended(cells, sides, width):
    for axis, dim in sides:
        count = lax.axis_size(axis)
        head = lax.slice_in_dim(cells, 0, width, axis=dim)
        tail = lax.slice_in_dim(cells, cells.shape[dim] - width, cells.shape[dim], axis=dim)
        cells = jnp.concatenate(
            [
                lax.ppermute(tail, axis, [(i, (i + 1) % count) for i in range(count)]),
                cells,
                lax.ppermute(head, axis, [((i + 1) % count, i) for i in range(count)]),
            ],
            axis=dim,
        )
    return cells


def wrap_long(along_x, length):
    return jnp.where(
        along_x > 0.5 * length,
        along_x - length,
        jnp.where(along_x < -0.5 * length, along_x + length, along_x),
    )


def phases_of(block_waves, positions):
    return (
        block_waves[0][:, None] * positions[0][None, :]
        + block_waves[1][:, None] * positions[1][None, :]
        + block_waves[2][:, None] * positions[2][None, :]
    )


def trig_blocks(block_waves, positions):
    phases = phases_of(block_waves, positions)
    return (jnp.cos(phases).astype(jnp.bfloat16), jnp.sin(phases).astype(jnp.bfloat16))


def near_messages(wide_feats, wide_pos, cell_pos, neighbours, falloffs, coefs, length):
    cell_count = cell_pos.shape[0]
    partner_rows = jnp.arange(cell_count, dtype=jnp.int32)[:, None] + HW + neighbours
    partner_pos = wide_pos[partner_rows]
    partner_feats = wide_feats[partner_rows]
    displace = cell_pos[:, None, :, :, None] - partner_pos[:, :, :, None, :]
    along_x = wrap_long(displace[:, :, 0], length)
    squared = (
        along_x * along_x
        + displace[:, :, 1] * displace[:, :, 1]
        + displace[:, :, 2] * displace[:, :, 2]
    )
    kernel = jnp.exp(-falloffs[:, None, None, None, None] * squared[None]).astype(jnp.bfloat16)
    messages = jnp.einsum(
        "gcnij,cnjf->gcif", kernel, partner_feats, preferred_element_type=jnp.float32
    )
    near = jnp.sum(messages * coefs[:, None, None, :], axis=0)
    return near.reshape(cell_count * cell_pos.shape[2], coefs.shape[1])


def shards(
    features,
    positions,
    occupancy,
    neighbours,
    wavevectors,
    filters,
    falloffs,
    mixing,
    norm_gain,
    in_weight,
    out_weight,
):
    cell_count = occupancy.shape[0]
    atom_rows = features.shape[0]
    capacity = atom_rows // cell_count
    part_width = features.shape[1]
    full_width = mixing.shape[1]
    length = jnp.float32(lax.axis_size("cells") * cell_count)
    count = lax.psum(jnp.sum(occupancy).astype(jnp.float32), "cells")
    is_live = (jnp.arange(capacity, dtype=jnp.int32)[None, :] < occupancy[:, None]).reshape(
        atom_rows, 1
    )
    whole = lax.all_gather(features, "waves", axis=1, tiled=True)
    masked_whole = jnp.where(is_live, whole, jnp.zeros_like(whole))
    cell_pos = positions.reshape(3, cell_count, capacity).transpose(1, 0, 2)
    wide_pos = extended(cell_pos, (("cells", 0),), HW)
    wave_rows = wavevectors.shape[1]
    block_rows = math.gcd(wave_rows, 512)
    stacked = wavevectors.reshape(3, wave_rows // block_rows, block_rows).transpose(1, 0, 2)

    def forward(block_waves):
        cosine_block, sine_block = trig_blocks(block_waves, positions)
        return (
            jnp.dot(cosine_block, masked_whole, preferred_element_type=jnp.float32),
            jnp.dot(sine_block, masked_whole, preferred_element_type=jnp.float32),
        )

    cos_sum, sin_sum = lax.map(forward, stacked)
    cos_sum = cos_sum.reshape(wave_rows, full_width)
    sin_sum = sin_sum.reshape(wave_rows, full_width)
    empty = jnp.zeros((atom_rows, full_width), jnp.float32)
    count_root = jnp.sqrt(count)
    cos_total, sin_total = lax.psum((cos_sum, sin_sum), "cells")
    cos_filtered = (filters * (cos_total / count_root)).astype(jnp.bfloat16)
    sin_filtered = (filters * (sin_total / count_root)).astype(jnp.bfloat16)
    piece_rows = cos_filtered.shape[0]
    inner_rows = math.gcd(piece_rows, 512)
    contract = (((0,), (0,)), ((), ()))

    def add_block(block_number, total_far):
        begin = block_number * inner_rows
        block_waves = lax.dynamic_slice_in_dim(wavevectors, 0 + begin, inner_rows, 1)
        cosine_block, sine_block = trig_blocks(block_waves, positions)
        cos_part = lax.dynamic_slice_in_dim(cos_filtered, begin, inner_rows, 0)
        sin_part = lax.dynamic_slice_in_dim(sin_filtered, begin, inner_rows, 0)
        total_far = total_far + lax.dot_general(
            cosine_block, cos_part, contract, preferred_element_type=jnp.float32
        )
        return total_far + lax.dot_general(
            sine_block, sin_part, contract, preferred_element_type=jnp.float32
        )

    far_sum = lax.fori_loop(0, piece_rows // inner_rows, add_block, empty)
    column = lax.axis_index("waves") * part_width
    masked_part = jnp.where(is_live, features, jnp.zeros_like(features))
    wide_feats = extended(
        masked_part.reshape(cell_count, capacity, part_width), (("cells", 0),), HW
    )
    coefs = lax.dynamic_slice_in_dim(mixing, column, part_width, 1)
    near = near_messages(wide_feats, wide_pos, cell_pos, neighbours, falloffs, coefs, length)
    far_part = lax.psum_scatter(
        far_sum.astype(jnp.bfloat16), "waves", scatter_dimension=1, tiled=True
    ).astype(jnp.float32) / math.sqrt(K)
    merged_part = features.astype(jnp.float32) + near + far_part
    merged = lax.all_gather(merged_part.astype(jnp.bfloat16), "waves", axis=1, tiled=True).astype(
        merged_part.dtype
    )
    normed = (
        merged * lax.rsqrt(jnp.mean(merged * merged, axis=-1, keepdims=True) + EPS) * norm_gain
    ).astype(jnp.bfloat16)
    hidden = jax.nn.silu(jnp.dot(normed, in_weight, preferred_element_type=jnp.float32)).astype(
        jnp.bfloat16
    )
    mlp_terms = jnp.dot(hidden, out_weight, preferred_element_type=jnp.float32)
    mlp_part = lax.psum_scatter(
        mlp_terms.astype(jnp.bfloat16), "waves", scatter_dimension=1, tiled=True
    ).astype(jnp.float32)
    return (merged_part + mlp_part).astype(jnp.bfloat16)


def solution(mesh):
    placed = (
        P("cells", "waves"),
        P(None, "cells"),
        P("cells"),
        P("cells", None),
        P(None, "waves"),
        P("waves", None),
        P(),
        P(),
        P(),
        P(None, "waves"),
        P("waves", None),
    )
    return jax.shard_map(
        shards, mesh=mesh, in_specs=placed, out_specs=P("cells", "waves"), check_vma=False
    )
```

profile of v0, /device:TPU:0, one launch (start us, length us, event | category | flops | bytes accessed | tf_op | source)
XLA Modules:
  0.0 636.2 jit_solution(1382222038693318387)
XLA Ops:
  6.5 0.7 all-gather.3.cloned.1.call-update
  7.3 0.0 all-reduce.3.cloned.1.call-start
  7.3 0.7 fusion.59
  8.1 36.6 %all-gather.3.cloned.1.call-done = bf16[2048,512]{1,0:T(8,128)(2,1)} async-done(((bf16[2048,256]{1,0:T(8,128)(2,1)}), bf16[2048,512]{1,0:T(8,128)(2,1)}) %all-gather.3.cloned.1.call-update) | async-done | bytes 2097168 | tf_op jit(solution)/shard_map/all_gather | solution.py:95
  44.7 1.8 broadcast_select_fusion
  46.5 125.5 %while.26 = (s32[]{:T(128)}, f32[4,512,512]{2,1,0:T(8,128)}, f32[4,512,512]{2,1,0:T(8,128)}, f32[4,3,512]{2,1,0:T(4,128)}, f32[3,2048]{1,0:T(4,128)S(1)}, /*inde...) while((s32[]{:T(128)}, f32[4,512,512]{2,1,0:T(8,128)}, f32[4,512,512]{2,1,0:T(8,128)}, ...), condition=%wide.region_2.3_spmd, body=%wide.region_1.0_spmd.sunk | while | flops 2160066560 | bytes 6415497 | solution.py:110
  46.5 0.8 constant_dynamic-slice_fusion.7
  47.3 15.4 %fusion.84 = f32[4,512,512]{2,1,0:T(8,128)} fusion(f32[4,512,512]{2,1,0:T(8,128)} %get-tuple-element.325, s32[]{:T(128)} %get-tuple-element.323, bf16[2048,512]{1,0:T(8,128)(2,1)S(1)} %get-tuple-element.338, f32[2048]{0:T(1024)S(1)} %bitcast.119, f32[512]{0:T(512)S(1)} %bitcast.137, f32[2048]{0:T(1024)S(1)} %bitcast.121, f32[512]{0:T(512)S(1)} %bitcast.135, ...), kind=kOutput, calls=%fused_computation.20.clone.1 | convolution fusion | flops 1080033280 | bytes 3176960 | tf_op jit(solution)/shard_map/while/body/eval_jaxpr/dot_general | solution.py:107
  62.7 15.2 %fusion.83 = f32[4,512,512]{2,1,0:T(8,128)} fusion(f32[4,512,512]{2,1,0:T(8,128)} %get-tuple-element.324, s32[]{:T(128)} %get-tuple-element.323, bf16[2048,512]{1,0:T(8,128)(2,1)S(1)} %get-tuple-element.338, f32[2048]{0:T(1024)S(1)} %bitcast.120, f32[512]{0:T(512)S(1)} %bitcast.138, f32[2048]{0:T(1024)S(1)} %bitcast.122, f32[512]{0:T(512)S(1)} %bitcast.136, ...), kind=kOutput, calls=%fused_computation.22.clone.1 | convolution fusion | flops 1080033280 | bytes 3176960 | tf_op jit(solution)/shard_map/while/body/eval_jaxpr/dot_general | solution.py:106
  77.8 0.8 constant_dynamic-slice_fusion.7
  78.7 15.4 %fusion.84 = f32[4,512,512]{2,1,0:T(8,128)} fusion(f32[4,512,512]{2,1,0:T(8,128)} %get-tuple-element.325, s32[]{:T(128)} %get-tuple-element.323, bf16[2048,512]{1,0:T(8,128)(2,1)S(1)} %get-tuple-element.338, f32[2048]{0:T(1024)S(1)} %bitcast.119, f32[512]{0:T(512)S(1)} %bitcast.137, f32[2048]{0:T(1024)S(1)} %bitcast.121, f32[512]{0:T(512)S(1)} %bitcast.135, ...), kind=kOutput, calls=%fused_computation.20.clone.1 | convolution fusion | flops 1080033280 | bytes 3176960 | tf_op jit(solution)/shard_map/while/body/eval_jaxpr/dot_general | solution.py:107
  94.0 15.2 %fusion.83 = f32[4,512,512]{2,1,0:T(8,128)} fusion(f32[4,512,512]{2,1,0:T(8,128)} %get-tuple-element.324, s32[]{:T(128)} %get-tuple-element.323, bf16[2048,512]{1,0:T(8,128)(2,1)S(1)} %get-tuple-element.338, f32[2048]{0:T(1024)S(1)} %bitcast.120, f32[512]{0:T(512)S(1)} %bitcast.138, f32[2048]{0:T(1024)S(1)} %bitcast.122, f32[512]{0:T(512)S(1)} %bitcast.136, ...), kind=kOutput, calls=%fused_computation.22.clone.1 | convolution fusion | flops 1080033280 | bytes 3176960 | tf_op jit(solution)/shard_map/while/body/eval_jaxpr/dot_general | solution.py:106
  109.2 0.8 constant_dynamic-slice_fusion.7
  110.0 15.3 %fusion.84 = f32[4,512,512]{2,1,0:T(8,128)} fusion(f32[4,512,512]{2,1,0:T(8,128)} %get-tuple-element.325, s32[]{:T(128)} %get-tuple-element.323, bf16[2048,512]{1,0:T(8,128)(2,1)S(1)} %get-tuple-element.338, f32[2048]{0:T(1024)S(1)} %bitcast.119, f32[512]{0:T(512)S(1)} %bitcast.137, f32[2048]{0:T(1024)S(1)} %bitcast.121, f32[512]{0:T(512)S(1)} %bitcast.135, ...), kind=kOutput, calls=%fused_computation.20.clone.1 | convolution fusion | flops 1080033280 | bytes 3176960 | tf_op jit(solution)/shard_map/while/body/eval_jaxpr/dot_general | solution.py:107
  125.4 15.2 %fusion.83 = f32[4,512,512]{2,1,0:T(8,128)} fusion(f32[4,512,512]{2,1,0:T(8,128)} %get-tuple-element.324, s32[]{:T(128)} %get-tuple-element.323, bf16[2048,512]{1,0:T(8,128)(2,1)S(1)} %get-tuple-element.338, f32[2048]{0:T(1024)S(1)} %bitcast.120, f32[512]{0:T(512)S(1)} %bitcast.138, f32[2048]{0:T(1024)S(1)} %bitcast.122, f32[512]{0:T(512)S(1)} %bitcast.136, ...), kind=kOutput, calls=%fused_computation.22.clone.1 | convolution fusion | flops 1080033280 | bytes 3176960 | tf_op jit(solution)/shard_map/while/body/eval_jaxpr/dot_general | solution.py:106
  140.6 0.8 constant_dynamic-slice_fusion.7
  141.4 15.3 %fusion.84 = f32[4,512,512]{2,1,0:T(8,128)} fusion(f32[4,512,512]{2,1,0:T(8,128)} %get-tuple-element.325, s32[]{:T(128)} %get-tuple-element.323, bf16[2048,512]{1,0:T(8,128)(2,1)S(1)} %get-tuple-element.338, f32[2048]{0:T(1024)S(1)} %bitcast.119, f32[512]{0:T(512)S(1)} %bitcast.137, f32[2048]{0:T(1024)S(1)} %bitcast.121, f32[512]{0:T(512)S(1)} %bitcast.135, ...), kind=kOutput, calls=%fused_computation.20.clone.1 | convolution fusion | flops 1080033280 | bytes 3176960 | tf_op jit(solution)/shard_map/while/body/eval_jaxpr/dot_general | solution.py:107
  156.8 15.2 %fusion.83 = f32[4,512,512]{2,1,0:T(8,128)} fusion(f32[4,512,512]{2,1,0:T(8,128)} %get-tuple-element.324, s32[]{:T(128)} %get-tuple-element.323, bf16[2048,512]{1,0:T(8,128)(2,1)S(1)} %get-tuple-element.338, f32[2048]{0:T(1024)S(1)} %bitcast.120, f32[512]{0:T(512)S(1)} %bitcast.138, f32[2048]{0:T(1024)S(1)} %bitcast.122, f32[512]{0:T(512)S(1)} %bitcast.136, ...), kind=kOutput, calls=%fused_computation.22.clone.1 | convolution fusion | flops 1080033280 | bytes 3176960 | tf_op jit(solution)/shard_map/while/body/eval_jaxpr/dot_general | solution.py:106
  171.9 0.0 all-reduce.3.cloned.1.call-update
  172.0 0.0 reduce-scatter.3.cloned.1.call-start
  172.0 0.6 copy-done.5
  172.6 0.6 reduce_sum.28
  173.9 35.3 %psum.22 = f32[]{:T(128)} all-reduce(f32[]{:T(128)S(6)} %convert_element_type.64), channel_id=1, replica_groups=mesh['cells'=16,'waves'=2] {'cells'}, use_global_device_ids=true, to_apply=%region_5.6 | all-reduce | flops 1 | bytes 8 | tf_op jit(solution)/shard_map/psum | solution.py:91
  209.9 132.7 %all-reduce.3.cloned.1.call-done = (f32[2048,512]{1,0:T(8,128)}, f32[2048,512]{1,0:T(8,128)}) async-done(((f32[2048,512]{1,0:T(8,128)}, f32[2048,512]{1,0:T(8,128)}), (f32[2048,512]{1,0:T(8,128)}, f32[2048,512]{1,0:T(8,128)})) %all-reduce.3.cloned.1.call-update) | async-done | bytes 8388624 | tf_op jit(solution)/shard_map/psum | solution.py:115
  342.5 7.7 %multiply_convert_fusion.1 = (bf16[2048,512]{1,0:T(8,128)(2,1)S(1)}, bf16[2048,512]{1,0:T(8,128)(2,1)}) fusion(f32[2048,512]{1,0:T(8,128)} %param.20, f32[2048,512]{1,0:T(8,128)} %get-tuple-element.196, f32[]{:T(128)S(6)} %sqrt.3, f32[2048,512]{1,0:T(8,128)} %get-tuple-element.195), kind=kLoop, calls=%fused_computation.63 | loop fusion | flops 6291456 | bytes 16777220 | tf_op jit(solution)/shard_map/convert_element_type | solution.py:117
  350.3 163.6 %while.27 = (s32[]{:T(128)}, f32[2048,512]{1,0:T(8,128)}, f32[3,2048]{1,0:T(4,128)}, f32[3,2048]{1,0:T(4,128)S(1)}, bf16[2048,512]{1,0:T(8,128)(2,1)}, /*index=5...) while((s32[]{:T(128)}, f32[2048,512]{1,0:T(8,128)}, ...), condition=%wide.region_8.9_spmd.clone, body=%wide.region_7.8_spmd.clone.sunk | while | flops 2163212288 | bytes 17948888 | solution.py:135
  365.8 0.9 constant_dynamic-slice_fusion.8
  366.7 17.6 %fusion.88 = f32[2048,512]{1,0:T(8,128)} fusion(f32[2048]{0:T(1024)S(1)} %bitcast.113, f32[512]{0:T(512)S(1)} %bitcast.131, f32[2048]{0:T(1024)S(1)} %bitcast.115, f32[512]{0:T(512)S(1)} %bitcast.129, f32[2048]{0:T(1024)S(1)} %bitcast.111, f32[512]{0:T(512)S(1)} %bitcast.127, bf16[2048,512]{1,0:T(8,128)(2,1)} %get-tuple-element.371, s32[]{:T(128)S(6)} %select_n.66), kind=kOutput, calls=%fused_computation.31.clone.1 | convolution fusion | flops 1080033280 | bytes 4749316 | tf_op jit(solution)/shard_map/while/body/eval_jaxpr/dot_general | solution.py:128
  384.3 18.0 %fusion.89 = f32[2048,512]{1,0:T(8,128)} fusion(f32[2048,512]{1,0:T(8,128)} %fusion.88, f32[2048,512]{1,0:T(8,128)} %get-tuple-element.356, f32[2048]{0:T(1024)S(1)} %bitcast.114, f32[512]{0:T(512)S(1)} %bitcast.132, f32[2048]{0:T(1024)S(1)} %bitcast.116, f32[512]{0:T(512)S(1)} %bitcast.130, f32[2048]{0:T(1024)S(1)} %bitcast.112, ...), kind=kOutput, calls=%fused_computation.27.clone.1 | convolution fusion | flops 1083179008 | bytes 13137925 | tf_op jit(solution)/shard_map/while/body/eval_jaxpr/dot_general | solution.py:131
  402.3 0.9 constant_dynamic-slice_fusion.8
  403.2 17.6 %fusion.88 = f32[2048,512]{1,0:T(8,128)} fusion(f32[2048]{0:T(1024)S(1)} %bitcast.113, f32[512]{0:T(512)S(1)} %bitcast.131, f32[2048]{0:T(1024)S(1)} %bitcast.115, f32[512]{0:T(512)S(1)} %bitcast.129, f32[2048]{0:T(1024)S(1)} %bitcast.111, f32[512]{0:T(512)S(1)} %bitcast.127, bf16[2048,512]{1,0:T(8,128)(2,1)} %get-tuple-element.371, s32[]{:T(128)S(6)} %select_n.66), kind=kOutput, calls=%fused_computation.31.clone.1 | convolution fusion | flops 1080033280 | bytes 4749316 | tf_op jit(solution)/shard_map/while/body/eval_jaxpr/dot_general | solution.py:128
  420.8 18.6 %fusion.89 = f32[2048,512]{1,0:T(8,128)} fusion(f32[2048,512]{1,0:T(8,128)} %fusion.88, f32[2048,512]{1,0:T(8,128)} %get-tuple-element.356, f32[2048]{0:T(1024)S(1)} %bitcast.114, f32[512]{0:T(512)S(1)} %bitcast.132, f32[2048]{0:T(1024)S(1)} %bitcast.116, f32[512]{0:T(512)S(1)} %bitcast.130, f32[2048]{0:T(1024)S(1)} %bitcast.112, ...), kind=kOutput, calls=%fused_computation.27.clone.1 | convolution fusion | flops 1083179008 | bytes 13137925 | tf_op jit(solution)/shard_map/while/body/eval_jaxpr/dot_general | solution.py:131
  439.4 0.9 constant_dynamic-slice_fusion.8
  440.3 17.6 %fusion.88 = f32[2048,512]{1,0:T(8,128)} fusion(f32[2048]{0:T(1024)S(1)} %bitcast.113, f32[512]{0:T(512)S(1)} %bitcast.131, f32[2048]{0:T(1024)S(1)} %bitcast.115, f32[512]{0:T(512)S(1)} %bitcast.129, f32[2048]{0:T(1024)S(1)} %bitcast.111, f32[512]{0:T(512)S(1)} %bitcast.127, bf16[2048,512]{1,0:T(8,128)(2,1)} %get-tuple-element.371, s32[]{:T(128)S(6)} %select_n.66), kind=kOutput, calls=%fused_computation.31.clone.1 | convolution fusion | flops 1080033280 | bytes 4749316 | tf_op jit(solution)/shard_map/while/body/eval_jaxpr/dot_general | solution.py:128
  457.9 18.6 %fusion.89 = f32[2048,512]{1,0:T(8,128)} fusion(f32[2048,512]{1,0:T(8,128)} %fusion.88, f32[2048,512]{1,0:T(8,128)} %get-tuple-element.356, f32[2048]{0:T(1024)S(1)} %bitcast.114, f32[512]{0:T(512)S(1)} %bitcast.132, f32[2048]{0:T(1024)S(1)} %bitcast.116, f32[512]{0:T(512)S(1)} %bitcast.130, f32[2048]{0:T(1024)S(1)} %bitcast.112, ...), kind=kOutput, calls=%fused_computation.27.clone.1 | convolution fusion | flops 1083179008 | bytes 13137925 | tf_op jit(solution)/shard_map/while/body/eval_jaxpr/dot_general | solution.py:131
  476.6 0.9 constant_dynamic-slice_fusion.8
  477.5 17.6 %fusion.88 = f32[2048,512]{1,0:T(8,128)} fusion(f32[2048]{0:T(1024)S(1)} %bitcast.113, f32[512]{0:T(512)S(1)} %bitcast.131, f32[2048]{0:T(1024)S(1)} %bitcast.115, f32[512]{0:T(512)S(1)} %bitcast.129, f32[2048]{0:T(1024)S(1)} %bitcast.111, f32[512]{0:T(512)S(1)} %bitcast.127, bf16[2048,512]{1,0:T(8,128)(2,1)} %get-tuple-element.371, s32[]{:T(128)S(6)} %select_n.66), kind=kOutput, calls=%fused_computation.31.clone.1 | convolution fusion | flops 1080033280 | bytes 4749316 | tf_op jit(solution)/shard_map/while/body/eval_jaxpr/dot_general | solution.py:128
  495.1 18.6 %fusion.89 = f32[2048,512]{1,0:T(8,128)} fusion(f32[2048,512]{1,0:T(8,128)} %fusion.88, f32[2048,512]{1,0:T(8,128)} %get-tuple-element.356, f32[2048]{0:T(1024)S(1)} %bitcast.114, f32[512]{0:T(512)S(1)} %bitcast.132, f32[2048]{0:T(1024)S(1)} %bitcast.116, f32[512]{0:T(512)S(1)} %bitcast.130, f32[2048]{0:T(1024)S(1)} %bitcast.112, ...), kind=kOutput, calls=%fused_computation.27.clone.1 | convolution fusion | flops 1083179008 | bytes 13137925 | tf_op jit(solution)/shard_map/while/body/eval_jaxpr/dot_general | solution.py:131
  513.9 3.9 convert_element_type.67
  517.8 0.0 reduce-scatter.3.cloned.1.call-update
  517.9 0.0 all-gather.5.cloned.1.call-start
  517.9 0.1 collective-permute-start.2
  518.0 4.4 collective-permute-start.3
  522.4 0.4 broadcast_select_fusion.1
  522.9 0.1 collective-permute-start
  522.9 4.4 collective-permute-start.1
  527.4 0.1 copy.18
  527.5 0.1 reshape.112
  527.7 0.6 gather_fusion.1
  528.3 1.4 broadcast_subtract_fusion
  529.8 2.8 fusion.46
  532.6 0.2 pad_maximum_fusion
  532.8 2.5 gather_fusion
  535.3 8.1 %fusion.36 = f32[16,128,256]{1,2,0:T(8,128)} fusion(f32[4,256]{1,0:T(4,128)S(1)} %constant_dynamic-slice_fusion.4, bf16[16,3,128,256,1]{3,2,1,4,0:T(8,128)(2,1)} %bitcast.106, f32[16,3,128,128]{3,2,1,0:T(8,128)} %fusion.46, f32[4]{0:T(128)S(1)} %neg.8), kind=kOutput, calls=%fused_computation.52 | convolution fusion | flops 1620574208 | bytes 8392720 | tf_op jit(solution)/shard_map/gcnij,cnjf->gcif/dot_general | solution.py:65
  543.4 2.0 copy.22
  545.4 4.4 reduce-scatter.3.cloned.1.call-done
  549.7 3.0 fusion.58
  552.7 0.0 all-gather.5.cloned.1.call-update
  552.7 0.0 reduce-scatter.5.cloned.1.call-start
  552.8 33.2 %all-gather.5.cloned.1.call-done = bf16[2048,512]{1,0:T(8,128)(2,1)} async-done(((bf16[2048,256]{1,0:T(8,128)(2,1)}), bf16[2048,512]{1,0:T(8,128)(2,1)}) %all-gather.5.cloned.1.call-update) | async-done | bytes 2097168 | tf_op jit(solution)/shard_map/all_gather | solution.py:147
  585.9 2.1 fusion.40
  588.1 5.8 convolution_convert_fusion
  593.8 32.1 %reduce-scatter.5.cloned.1.call-done = bf16[2048,256]{1,0:T(8,128)(2,1)} async-done(((bf16[2048,512]{1,0:T(8,128)(2,1)}), bf16[2048,256]{1,0:T(8,128)(2,1)}) %reduce-scatter.5.cloned.1.call-update) | async-done | bytes 1048592 | tf_op jit(solution)/shard_map/reduce_scatter | solution.py:157
  625.9 3.4 add_convert_fusion
  (45 shorter events, 0.3 us)
Async XLA Ops:
  6.5 581.5 %copy-start = (bf16[512,512]{1,0:T(8,128)(2,1)S(1)}, bf16[512,512]{1,0:T(8,128)(2,1)}, u32[]{:S(2)}) copy-start(bf16[512,512]{1,0:T(8,128)(2,1)} %param.25) | copy-start | bytes 1572868
  6.5 39.9 %copy-start.2 = (f32[3,2048]{1,0:T(4,128)S(1)}, f32[3,2048]{1,0:T(4,128)}, u32[]{:S(2)}) copy-start(f32[3,2048]{1,0:T(4,128)} %param.16) | copy-start | bytes 73732
  6.5 38.1 %all-gather.3.cloned.1.call-start = ((), (), s32[]{:S(2)}) async-start(), calls=%async_computation.2 | async-start | bytes 3145728 | tf_op jit(solution)/shard_map/all_gather | solution.py:95
  7.3 335.3 %all-reduce.3.cloned.1.call-start = ((), (), s32[]{:S(2)}) async-start(), calls=%async_computation.6 | async-start | bytes 16777216 | tf_op jit(solution)/shard_map/psum | solution.py:115
  171.9 0.7 copy-start.5
  172.0 377.8 %reduce-scatter.3.cloned.1.call-start = ((), (), s32[]{:S(2)}) async-start(), calls=%async_computation.3 | async-start | bytes 3145728 | tf_op jit(solution)/shard_map/reduce_scatter | solution.py:143
  513.9 8.5 %copy-start.1 = (bf16[2048,256]{1,0:T(8,128)(2,1)S(1)}, bf16[2048,256]{1,0:T(8,128)(2,1)}, u32[]{:S(2)}) copy-start(bf16[2048,256]{1,0:T(8,128)(2,1)} %param.15) | copy-start | bytes 3145732
  513.9 13.5 %copy-start.4 = (s32[16,3]{0,1:T(4,128)S(1)}, s32[16,3]{0,1:T(4,128)}, u32[]{:S(2)}) copy-start(s32[16,3]{0,1:T(4,128)} %param.18) | copy-start | bytes 580
  513.9 13.7 %copy-start.3 = (f32[4,512]{1,0:T(4,128)S(1)}, f32[4,512]{1,0:T(4,128)}, u32[]{:S(2)}) copy-start(f32[4,512]{1,0:T(4,128)} %param.22) | copy-start | bytes 24580
  513.9 13.7 %copy-start.8 = (f32[4]{0:T(128)S(1)}, f32[4]{0:T(128)}, u32[]{:S(2)}) copy-start(f32[4]{0:T(128)} %param.21) | copy-start | bytes 52
  517.9 68.1 %all-gather.5.cloned.1.call-start = ((), (), s32[]{:S(2)}) async-start(), calls=%async_computation.4 | async-start | bytes 3145728 | tf_op jit(solution)/shard_map/all_gather | solution.py:147
  517.9 9.7 %collective-permute-start.2 = (f32[2,3,128]{2,1,0:T(4,128)S(1)}, f32[2,3,128]{2,1,0:T(4,128)S(1)}, u32[]{:S(2)}, u32[]{:S(2)}) collective-permute-start(f32[2,3,128]{2,1,0:T(4,128)S(1)} %get-tuple-element.213), channel_id=1, source_target_pairs={{0,2},{2,4},{4,6},{6,8},{8,10},{10,12},{12,14},{14,16},{16,18},{18... | collective-permute-start | bytes 9224 | tf_op jit(solution)/shard_map/ppermute | solution.py:22
  518.0 9.7 %collective-permute-start.3 = (f32[2,3,128]{2,1,0:T(4,128)S(1)}, f32[2,3,128]{2,1,0:T(4,128)S(1)}, u32[]{:S(2)}, u32[]{:S(2)}) collective-permute-start(f32[2,3,128]{2,1,0:T(4,128)S(1)} %get-tuple-element.214), channel_id=1, source_target_pairs={{2,0},{4,2},{6,4},{8,6},{10,8},{12,10},{14,12},{16,14},{18,16},{20... | collective-permute-start | bytes 9224 | tf_op jit(solution)/shard_map/ppermute | solution.py:24
  522.9 9.7 %collective-permute-start = (bf16[2,128,256]{2,1,0:T(8,128)(2,1)S(1)}, bf16[2,128,256]{2,1,0:T(8,128)(2,1)S(1)}, u32[]{:S(2)}, u32[]{:S(2)}) collective-permute-start(bf16[2,128,256]{2,1,0:T(8,128)(2,1)S(1)} %bitcast.124), channel_id=1, source_target_pairs={{0,2},{2,4},{4,6},{6,8},{8,10},{10,12},{12,14},{14,16},{16,18},{18... | collective-permute-start | bytes 393224 | tf_op jit(solution)/shard_map/ppermute | solution.py:22
  522.9 9.6 %collective-permute-start.1 = (bf16[2,128,256]{2,1,0:T(8,128)(2,1)S(1)}, bf16[2,128,256]{2,1,0:T(8,128)(2,1)S(1)}, u32[]{:S(2)}, u32[]{:S(2)}) collective-permute-start(bf16[2,128,256]{2,1,0:T(8,128)(2,1)S(1)} %bitcast.123), channel_id=1, source_target_pairs={{2,0},{4,2},{6,4},{8,6},{10,8},{12,10},{14,12},{16,14},{18,16},{20... | collective-permute-start | bytes 393224 | tf_op jit(solution)/shard_map/ppermute | solution.py:24
  545.4 42.7 %copy-start.6 = (bf16[512,512]{1,0:T(8,128)(2,1)S(1)}, bf16[512,512]{1,0:T(8,128)(2,1)}, u32[]{:S(2)}) copy-start(bf16[512,512]{1,0:T(8,128)(2,1)} %param.24) | copy-start | bytes 1572868
  545.4 42.7 %copy-start.7 = (f32[512]{0:T(512)S(1)}, f32[512]{0:T(512)}, u32[]{:S(2)}) copy-start(f32[512]{0:T(512)} %param.23) | copy-start | bytes 6148
  552.7 73.2 %reduce-scatter.5.cloned.1.call-start = ((), (), s32[]{:S(2)}) async-start(), calls=%async_computation.5 | async-start | bytes 3145728 | tf_op jit(solution)/shard_map/reduce_scatter | solution.py:157
Sparse Core Ops, SparseCore 0:
  8.9 35.7 all-gather.2
  172.1 170.4 all-reduce.2
  518.0 31.7 reduce-scatter.2
  552.9 33.0 all-gather.4
  594.0 31.8 reduce-scatter.4
where the time goes:
time: 649 us; the launch traced here: 636 us
  matrix products  280 us (43%)
  waiting for transfers between devices  240 us (37%)
  blocking collectives  35.3 us (5%)
  other arithmetic  28.1 us (4%)
  loops' own time  15.7 us (2%)
  between operations  15.1 us (2%)
  local copies, waits for them, and re-layouts  12.9 us (2%)
  starting transfers between devices  9.14 us (1%)
    psum x1, waiting for transfers between devices, shards(): cos_total, sin_total = lax.psum((cos_sum, sin_sum), 'cells')  133 us
    dot_general x4, matrix products, add_block(): lax.dot_general(sine_block, sin_part, contract, preferred_element_type=jn...  73.9 us
    dot_general x4, matrix products, add_block(): lax.dot_general(cosine_block, cos_part, contract, preferred_element_type=...  70.4 us
    dot_general x4, matrix products, forward(): jnp.dot(sine_block, masked_whole, preferred_element_type=jnp.float32)  61.4 us
    dot_general x4, matrix products, forward(): jnp.dot(cosine_block, masked_whole, preferred_element_type=jnp.float32)  60.7 us
    all_gather x1, waiting for transfers between devices, shards(): whole = lax.all_gather(features, 'waves', axis=1, tiled=True)  36.6 us
    psum x1, blocking collectives, shards(): count = lax.psum(jnp.sum(occupancy).astype(jnp.float32), 'cells')  35.3 us
    all_gather x1, waiting for transfers between devices, shards(): lax.all_gather(merged_part.astype(jnp.bfloat16), 'waves', axis=1, tiled=T...  33.2 us
  transfers between devices with their start and end apart: 9, of which 5 were waited for; matrix products, arithmetic and copies ran while one was open for 3% of the time, Pallas kernels for 0%

commit v1 on v0

v1 whole, which is shorter than its diff:
```python
import functools
import math

import jax
import jax.numpy as jnp
from jax import lax
from jax.experimental import pallas as pl
from jax.experimental.pallas import tpu as pltpu
from jax.sharding import PartitionSpec as P

EPS = 1e-06
HW = 2
CHUNKS = 2
TILE = 256

SCALE = 8.0**0.25
SIN_QUARTER = [SCALE * c for c in (1.5707884677838282, -0.6457119641929367, 0.07766728844449011)]
COS_QUARTER = [
    SCALE * c for c in (0.9999999724196053, -1.2336970139164884, 0.2535986397412255, -0.02040833859268099)
]


def horner(x, coefs):
    value = jnp.float32(coefs[-1])
    for coef in coefs[-2::-1]:
        value = value * x + jnp.float32(coef)
    return value


def cos_sin_turns(turns):
    rest = turns - jnp.round(turns)
    square = rest * rest
    sin_quarter = horner(square, SIN_QUARTER) * rest
    cos_quarter = horner(square, COS_QUARTER)
    sin_half = sin_quarter * cos_quarter
    cos_half = jnp.float32(math.sqrt(2.0)) - sin_quarter * sin_quarter
    return jnp.float32(1.0) - sin_half * sin_half, sin_half * cos_half


def forward_body(base, block_rows, reverse, waves_ref, atoms_ref, feats_ref, cos_ref, sin_ref, sum_ref, lhs, rhs, turns):
    rows = lhs.shape[0]
    blocks = feats_ref.shape[0] // TILE
    step = pl.program_id(0)
    sums = [None, None]

    @pl.when(step == 0)
    def _():
        high, middle, low = thirds(atoms_ref[...])
        rhs[...] = jnp.concatenate([high, middle, high, low, high, middle], axis=0).astype(jnp.bfloat16)

    start, first = base
    for part in range(rows // block_rows):
        number = (first + step * (rows // block_rows) + part) ^ reverse[0]
        at = pl.multiple_of(start + number * block_rows, block_rows)
        lhs[part * block_rows : (part + 1) * block_rows, :] = waves_ref[pl.ds(at, block_rows), :]

    def phase(block):
        turns[block % 3] = jnp.dot(
            lhs[...], rhs[:, block * TILE : (block + 1) * TILE], preferred_element_type=jnp.float32
        )

    def fill(block):
        for strip in range(rows // 16):
            at = slice(strip * 16, strip * 16 + 16)
            cos_part, sin_part = cos_sin_turns(turns[block % 3, at, :])
            cos_ref[at, block * TILE : (block + 1) * TILE] = cos_part.astype(jnp.bfloat16)
            sin_ref[at, block * TILE : (block + 1) * TILE] = sin_part.astype(jnp.bfloat16)

    def multiply(block):
        at = slice(block * TILE, (block + 1) * TILE)
        for which, ref in enumerate((cos_ref, sin_ref)):
            term = jnp.dot(ref[:, at], feats_ref[at, :], preferred_element_type=jnp.float32)
            sums[which] = term if sums[which] is None else sums[which] + term

    phase(0)
    for block in range(blocks):
        if block + 1 < blocks:
            phase(block + 1)
        fill(block)
        if block > 0:
            multiply(block - 1)
    multiply(blocks - 1)
    for which in range(2):
        sum_ref[which] = sums[which].astype(sum_ref.dtype)


def forward(reverse, waves, atoms, feats, start, position, count, block_rows, dtype):
    depth = waves.shape[1]
    atom_rows, width = feats.shape
    tile = min(TILE, count)
    trig = jax.ShapeDtypeStruct((count, atom_rows), jnp.bfloat16)
    return pl.pallas_call(
        functools.partial(forward_body, (start, position // block_rows), block_rows),
        grid_spec=pltpu.PrefetchScalarGridSpec(
            num_scalar_prefetch=1,
            grid=(count // tile,),
            in_specs=[
                pl.BlockSpec(waves.shape, lambda k, *_: (0, 0)),
                pl.BlockSpec(atoms.shape, lambda k, *_: (0, 0)),
                pl.BlockSpec(feats.shape, lambda k, *_: (0, 0)),
            ],
            out_specs=[
                pl.BlockSpec((tile, atom_rows), lambda k, *_: (k, 0)),
                pl.BlockSpec((tile, atom_rows), lambda k, *_: (k, 0)),
                pl.BlockSpec((2, tile, width), lambda k, *_: (0, k, 0)),
            ],
            scratch_shapes=[
                pltpu.VMEM((tile, depth), jnp.bfloat16),
                pltpu.VMEM((depth, atom_rows), jnp.bfloat16),
                pltpu.VMEM((3, tile, TILE), jnp.float32),
            ],
        ),
        out_shape=[trig, trig, jax.ShapeDtypeStruct((2, count, width), dtype)],
        cost_estimate=pl.CostEstimate(
            flops=9 * count * atom_rows * width,
            transcendentals=0,
            bytes_accessed=4 * count * atom_rows,
        ),
        name="structure",
    )(reverse, waves, atoms, feats)


def near_body(places, scales, row_ref, left_ref, masked_ref, right_ref, feats_ref, mix_ref, out_ref, wide, kernels, partners):
    cells_per_step = kernels.shape[0]
    cap = wide.shape[1]
    step = pl.program_id(0)
    kinds = mix_ref.shape[0]
    count = places.shape[1]
    halo = left_ref.shape[0]
    inner = masked_ref.shape[0]

    @pl.when(step == 0)
    def _():
        wide[0:halo] = left_ref[...]
        wide[halo : halo + inner] = masked_ref[...]
        wide[halo + inner :] = right_ref[...]

    for part in range(cells_per_step):
        cell = step * cells_per_step + part
        col = jnp.transpose(row_ref[cell + halo])
        for which in range(count):
            place = places[cell, which]
            row = row_ref[place]
            squared = None
            for axis in range(3):
                gap = col[:, axis : axis + 1] - row[axis : axis + 1, :]
                squared = gap * gap if squared is None else squared + gap * gap
            for kind in range(kinds):
                kernels[part, kind * cap : (kind + 1) * cap, which * cap : (which + 1) * cap] = (
                    jnp.exp2(scales[kind] * squared).astype(jnp.bfloat16)
                )
            partners[part, which * cap : (which + 1) * cap, :] = wide[place]
        total = jnp.dot(kernels[part], partners[part], preferred_element_type=jnp.float32)
        at = slice(part * cap, (part + 1) * cap)
        near = feats_ref[at, :].astype(jnp.float32)
        for kind in range(kinds):
            near = near + total[kind * cap : (kind + 1) * cap, :] * mix_ref[kind : kind + 1, :]
        out_ref[at, :] = near


def near_part(places, scales, rows, left, masked, right, feats, mix):
    cells, count = places.shape
    cap, width = masked.shape[1:]
    kinds = mix.shape[0]
    per = 2
    whole3 = lambda a: pl.BlockSpec(a.shape, lambda c, *_: (0, 0, 0))
    return pl.pallas_call(
        near_body,
        grid_spec=pltpu.PrefetchScalarGridSpec(
            num_scalar_prefetch=2,
            grid=(cells // per,),
            in_specs=[
                whole3(rows),
                whole3(left),
                whole3(masked),
                whole3(right),
                pl.BlockSpec((per * cap, width), lambda c, *_: (c, 0)),
                pl.BlockSpec(mix.shape, lambda c, *_: (0, 0)),
            ],
            out_specs=pl.BlockSpec((per * cap, width), lambda c, *_: (c, 0)),
            scratch_shapes=[
                pltpu.VMEM((rows.shape[0], cap, width), jnp.bfloat16),
                pltpu.VMEM((per, kinds * cap, count * cap), jnp.bfloat16),
                pltpu.VMEM((per, count * cap, width), jnp.bfloat16),
            ],
        ),
        out_shape=jax.ShapeDtypeStruct(feats.shape, jnp.float32),
        cost_estimate=pl.CostEstimate(
            flops=8 * cells * cap * cap * count * width * kinds,
            transcendentals=0,
            bytes_accessed=8 * cells * cap * width,
        ),
        name="near",
    )(places, scales, rows, left, masked, right, feats, mix)


def backward_body(pieces, *refs):
    trig = refs[:4]
    filts = refs[4:6]
    acc_ref = refs[6]
    outs = refs[7:]
    contract = (((0,), (0,)), ((), ()))
    total = acc_ref[...]
    for half in range(2):
        for which in range(2):
            total = total + lax.dot_general(
                trig[2 * half + which][...],
                filts[half][which],
                contract,
                preferred_element_type=jnp.float32,
            )
    outs[0][...] = total
    for piece in range(pieces):

        @pl.when(pl.program_id(0) == piece)
        def _(piece=piece):
            outs[1 + piece][...] = total.astype(jnp.bfloat16)


def backward(trig, filts, acc, first, tiles, tile, pieces):
    count = trig[0].shape[0]
    width = acc.shape[1]
    acc_offset = first if acc.shape[0] > tiles * tile else 0
    shapes = [jax.ShapeDtypeStruct((tiles * tile, width), jnp.float32)]
    specs = [pl.BlockSpec((tile, width), lambda i: (i, 0))]
    for _ in range(pieces):
        shapes.append(jax.ShapeDtypeStruct((tile, width), jnp.bfloat16))
        specs.append(pl.BlockSpec((tile, width), lambda i: (0, 0)))
    return pl.pallas_call(
        functools.partial(backward_body, pieces),
        grid=(tiles,),
        in_specs=[pl.BlockSpec((count, tile), lambda i: (0, i + first))] * 4
        + [pl.BlockSpec(filts[0].shape, lambda i: (0, 0, 0))] * 2
        + [pl.BlockSpec((tile, width), lambda i: (i + acc_offset, 0))],
        out_specs=specs,
        out_shape=shapes,
        cost_estimate=pl.CostEstimate(
            flops=16 * count * tiles * tile * width,
            transcendentals=0,
            bytes_accessed=8 * count * tiles * tile + 8 * tiles * tile * width,
        ),
        name="messages",
    )(*trig, *filts, acc)


def mlp_body(side, own_ref, other_ref, gain_ref, in0_ref, in1_ref, out0_ref, out1_ref, result_ref):
    width = own_ref.shape[1]
    mine = side[0]
    own = own_ref[...]
    own_wide = own.astype(jnp.bfloat16).astype(jnp.float32)
    other = other_ref[...].astype(jnp.float32)
    mean = (
        jnp.sum(own_wide * own_wide, axis=1, keepdims=True)
        + jnp.sum(other * other, axis=1, keepdims=True)
    ) / (2 * width)
    scale = lax.rsqrt(mean + EPS)
    normed_own = (own_wide * scale * gain_ref[pl.ds(mine, 1), :]).astype(jnp.bfloat16)
    normed_other = (other * scale * gain_ref[pl.ds(1 - mine, 1), :]).astype(jnp.bfloat16)
    at_own = pl.ds(pl.multiple_of(mine * width, width), width)
    at_other = pl.ds(pl.multiple_of((1 - mine) * width, width), width)
    total = own
    for in_ref, out_ref in ((in0_ref, out0_ref), (in1_ref, out1_ref)):
        value = jnp.dot(normed_own, in_ref[at_own, :], preferred_element_type=jnp.float32)
        value = value + jnp.dot(
            normed_other, in_ref[at_other, :], preferred_element_type=jnp.float32
        )
        half = jnp.float32(0.5) * value
        hidden = (half * jnp.tanh(half) + half).astype(jnp.bfloat16)
        total = total + jnp.dot(hidden, out_ref[...], preferred_element_type=jnp.float32)
    result_ref[...] = total.astype(jnp.bfloat16)


def mlp(side, own, other, piece, gains, weights):
    rows, width = other.shape
    tile = min(256, rows)
    offset = piece * (rows // tile)
    return pl.pallas_call(
        mlp_body,
        grid_spec=pltpu.PrefetchScalarGridSpec(
            num_scalar_prefetch=1,
            grid=(rows // tile,),
            in_specs=[
                pl.BlockSpec((tile, width), lambda i, *_: (i + offset, 0)),
                pl.BlockSpec((tile, width), lambda i, *_: (i, 0)),
                pl.BlockSpec(gains.shape, lambda i, *_: (0, 0)),
            ]
            + [pl.BlockSpec(weight.shape, lambda i, *_: (0, 0)) for weight in weights],
            out_specs=pl.BlockSpec((tile, width), lambda i, *_: (i, 0)),
        ),
        out_shape=jax.ShapeDtypeStruct((rows, width), jnp.bfloat16),
        cost_estimate=pl.CostEstimate(
            flops=2 * rows * width * weights[0].shape[1] * 12,
            transcendentals=0,
            bytes_accessed=8 * rows * width,
        ),
        name="mlp",
    )(side, own, other, gains, *weights)


def thirds(values):
    def rounded(v):
        return v.astype(jnp.bfloat16).astype(jnp.float32)

    high = rounded(values)
    middle = rounded(values - high)
    return high, middle, values - high - middle


def swap(value):
    return lax.ppermute(value, "waves", [(0, 1), (1, 0)])


def across(value, bit):
    count = lax.axis_size("cells")
    return lax.ppermute(value, "cells", [(i, i ^ bit) for i in range(count)])


def shards(
    features,
    positions,
    occupancy,
    neighbours,
    wavevectors,
    filters,
    falloffs,
    mixing,
    norm_gain,
    in_weight,
    out_weight,
):
    devices = lax.axis_size("cells")
    bits = [1 << b for b in range(devices.bit_length() - 1)]
    cell_count = occupancy.shape[0]
    atom_rows, width = features.shape
    capacity = atom_rows // cell_count
    wave_rows = wavevectors.shape[1]
    all_waves = 2 * wave_rows
    chunk_rows = wave_rows // CHUNKS
    block_rows = chunk_rows // devices
    length = jnp.float32(devices * cell_count)
    place = lax.axis_index("cells").astype(jnp.int32)
    side = lax.axis_index("waves").astype(jnp.int32)

    live = (jnp.arange(capacity, dtype=jnp.int32)[None, :] < occupancy[:, None]).reshape(atom_rows, 1)
    masked = jnp.where(live, features, jnp.zeros_like(features))

    reverse = jnp.int32(0)
    for index, bit in enumerate(reversed(bits)):
        reverse = reverse | jnp.where((place & bit) != 0, bits[index], 0).astype(jnp.int32)
    reverse_scalar = reverse.reshape(1)

    def wave_operand(waves):
        padded = jnp.pad(waves * jnp.float32(1.0 / (2.0 * math.pi)), ((0, 5), (0, 0)))
        high = lax.reduce_precision(padded, 8, 7)
        middle = lax.reduce_precision(padded - high, 8, 7)
        low = padded - high - middle
        return jnp.concatenate([high, high, middle, high, low, middle], axis=0).T.astype(jnp.bfloat16)

    atoms = jnp.pad(positions, ((0, 5), (0, 0)))
    other_waves = swap(wavevectors)

    to_right = [(i, (i + 1) % devices) for i in range(devices)]
    to_left = [((i + 1) % devices, i) for i in range(devices)]
    edge = HW * capacity
    left_feats = lax.ppermute(masked[atom_rows - edge :], "cells", to_right)
    right_feats = lax.ppermute(masked[:edge], "cells", to_left)
    left_pos = lax.ppermute(positions[:, atom_rows - edge :], "cells", to_right)
    right_pos = lax.ppermute(positions[:, :edge], "cells", to_left)
    count = jnp.full((8, 128), jnp.sum(occupancy).astype(jnp.float32))
    for bit in bits:
        count = count + across(count, bit)
    count = count[0:1, 0:1]

    def filter_part(chunk, whose):
        return lax.dynamic_slice(
            filters, (chunk * chunk_rows + reverse * block_rows, whose * width), (block_rows, width)
        )

    own_filters = [filter_part(chunk, side) for chunk in range(CHUNKS)]
    sent_filters = jnp.stack([filter_part(chunk, 1 - side) for chunk in range(CHUNKS)])
    other_filters = swap(sent_filters)

    in_other = swap(in_weight)
    hidden_rows = out_weight.shape[0]
    out_own = lax.dynamic_slice(out_weight, (0, side * width), (hidden_rows, width))
    out_other = swap(lax.dynamic_slice(out_weight, (0, (1 - side) * width), (hidden_rows, width)))

    factor = lax.rsqrt(count) * jnp.float32(1.0 / math.sqrt(all_waves))

    trig, totals = [], []
    number = 0
    for waves, rows_of_filter in ((wavevectors, own_filters), (other_waves, other_filters)):
        operand = wave_operand(waves)
        for chunk in range(CHUNKS):
            half = chunk_rows // 2
            cos_far, sin_far, send = forward(
                reverse_scalar, operand, atoms, masked, chunk * chunk_rows, half, half, block_rows, jnp.bfloat16
            )
            cos_near, sin_near, keep = forward(
                reverse_scalar, operand, atoms, masked, chunk * chunk_rows, 0, half, block_rows, jnp.float32
            )
            trig.append((cos_near, sin_near, cos_far, sin_far))
            for index, bit in enumerate(bits):
                summed = keep + across(send, bit).astype(jnp.float32)
                if index + 1 < len(bits):
                    half = summed.shape[1] // 2
                    keep, send = summed[:, :half], summed[:, half:].astype(jnp.bfloat16)
            filt = (summed * rows_of_filter[chunk][None] * factor[None]).astype(jnp.bfloat16)
            for index, bit in enumerate(reversed(bits)):
                came = across(filt, bit)
                if index + 1 < len(bits):
                    filt = jnp.concatenate([filt, came], axis=1)
            totals.append((filt, came))
            number += 1

    shift_left = jnp.where(place == 0, length, 0.0).astype(jnp.float32)
    shift_right = jnp.where(place == devices - 1, length, 0.0).astype(jnp.float32)
    first = jnp.array([[1.0], [0.0], [0.0]], jnp.float32)
    wide_pos = jnp.concatenate(
        [left_pos - first * shift_left, positions, right_pos + first * shift_right], axis=1
    )
    rows = jnp.pad(wide_pos, ((0, 5), (0, 0))).reshape(8, cell_count + 2 * HW, capacity).transpose(1, 0, 2)
    places = jnp.arange(cell_count, dtype=jnp.int32)[:, None] + HW + neighbours
    mix = lax.dynamic_slice(mixing, (0, side * width), (mixing.shape[0], width))
    merged = near_part(
        places,
        falloffs * jnp.float32(-1.0 / math.log(2.0)),
        rows,
        left_feats.reshape(HW, capacity, width),
        masked.reshape(cell_count, capacity, width),
        right_feats.reshape(HW, capacity, width),
        features,
        mix,
    )
    pieces = 4
    tile = atom_rows // pieces
    for number in range(len(trig) - 1):
        (merged,) = backward(trig[number], totals[number], merged, 0, pieces, tile, 0)

    gains = norm_gain.reshape(2, width)
    outs = []
    for call in range(2):
        part, *sends = backward(trig[-1], totals[-1], merged, call * 2, 2, tile, 2)
        for piece in range(2):
            came = swap(sends[piece])
            outs.append(
                mlp(side.reshape(1), part, came, piece, gains, (in_weight, in_other, out_own, out_other))
            )
    return jnp.concatenate(outs, axis=0)


def solution(mesh):
    placed = (
        P("cells", "waves"),
        P(None, "cells"),
        P("cells"),
        P("cells", None),
        P(None, "waves"),
        P("waves", None),
        P(),
        P(),
        P(),
        P(None, "waves"),
        P("waves", None),
    )

    return jax.shard_map(shards, mesh=mesh, in_specs=placed, out_specs=P("cells", "waves"), check_vma=False)
```

time: 649 us -> 240 us (0.37); the launches traced: 636 us -> 239 us
  matrix products: 280 us -> 0 us
  waiting for transfers between devices: 240 us -> 62.1 us
  Pallas kernels: 0 us -> 113 us
  blocking collectives: 35.3 us -> 0 us
  starting transfers between devices: 9.14 us -> 39.2 us
  other arithmetic: 28.1 us -> 10.7 us
  loops' own time: 15.7 us -> 0 us
  between operations: 15.1 us -> 2.01 us
    dot_general x18 -> x0, matrix products: 280 us -> none  [the longest x4 73.9 us: add_block(): lax.dot_general(sine_block, sin_part, contract, preferred_element_type=jn...]
    psum x1 -> x0, waiting for transfers between devices: 133 us -> none  [shards(): cos_total, sin_total = lax.psum((cos_sum, sin_sum), 'cells')]
    pallas_call x0 -> x18, Pallas kernels: none -> 113 us  [the longest x8 54.4 us: forward(): pl.pallas_call(functools.partial(forward_body, (start, position // block_...]
    all_gather x2 -> x0, waiting for transfers between devices: 69.8 us -> none  [the longest x1 36.6 us: shards(): whole = lax.all_gather(features, 'waves', axis=1, tiled=True)]
    ppermute x4 -> x48, waiting for transfers between devices: 0.01 us -> 62.1 us  [the longest x36 59.7 us: across(): return lax.ppermute(value, 'cells', [(i, i ^ bit) for i in range(count)])]
    reduce_scatter x2 -> x0, waiting for transfers between devices: 36.4 us -> none  [the longest x1 32.1 us: shards(): lax.psum_scatter(mlp_terms.astype(jnp.bfloat16), 'waves', scatter_dimensi...]
    psum x1 -> x0, blocking collectives: 35.3 us -> none  [shards(): count = lax.psum(jnp.sum(occupancy).astype(jnp.float32), 'cells')]
    ppermute x4 -> x48, starting transfers between devices: 8.97 us -> 39.2 us  [the longest x36 20.8 us: across(): return lax.ppermute(value, 'cells', [(i, i ^ bit) for i in range(count)])]
  transfers between devices with their start and end apart: 9 -> 48, of which waited for: 5 -> 25; matrix products, arithmetic and copies ran while one was open for 3% -> 7% of each run, Pallas kernels for 0% -> 46%
where the time goes in v1:
time: 240 us; the launch traced here: 239 us
  Pallas kernels  113 us (47%)
  waiting for transfers between devices  62.1 us (26%)
  starting transfers between devices  39.2 us (16%)
  local copies, waits for them, and re-layouts  12 us (5%)
  other arithmetic  10.7 us (4%)
    ppermute x36, waiting for transfers between devices, across(): return lax.ppermute(value, 'cells', [(i, i ^ bit) for i in range(count)])  59.7 us
    pallas_call x8, Pallas kernels, forward(): pl.pallas_call(functools.partial(forward_body, (start, position // block_...  54.4 us
    pallas_call x5, Pallas kernels, backward(): pl.pallas_call(functools.partial(backward_body, pieces), grid=(tiles,), i...  32.8 us
    ppermute x36, starting transfers between devices, across(): return lax.ppermute(value, 'cells', [(i, i ^ bit) for i in range(count)])  20.8 us
    pallas_call x4, Pallas kernels, mlp(): pl.pallas_call(mlp_body, grid_spec=pltpu.PrefetchScalarGridSpec(num_scala...  15.4 us
    ppermute x8, starting transfers between devices, swap(): return lax.ppermute(value, 'waves', [(0, 1), (1, 0)])  10.8 us
    pallas_call x1, Pallas kernels, near_part(): pl.pallas_call(near_body, grid_spec=pltpu.PrefetchScalarGridSpec(num_scal...  10.8 us
  transfers between devices with their start and end apart: 48, of which 25 were waited for; matrix products, arithmetic and copies ran while one was open for 7% of the time, Pallas kernels for 46%

profile of v1, /device:TPU:0, one launch (start us, length us, event | category | flops | bytes accessed | tf_op | source)
XLA Modules:
  0.0 239.4 jit_solution(8136498181433806813)
XLA Ops:
  0.0 3.0 %collective-permute-start = (f32[3,2048]{1,0:T(4,128)}, f32[3,2048]{1,0:T(4,128)S(1)}, u32[]{:S(2)}, u32[]{:S(2)}) collective-permute-start(f32[3,2048]{1,0:T(4,128)} %param.16), channel_id=1, source_target_pairs={{0,1},{1,0},{2,3},{3,2},{4,5},{5,4},{6,7},{7,6},{8,9},{9,8},{10,11... | collective-permute-start | bytes 73736 | tf_op jit(solution)/shard_map/ppermute | solution.py:310
  3.9 1.0 copy.20
  5.6 2.3 broadcast_select_fusion.feats_ref
  8.5 6.7 %structure.15 = (bf16[512,2048]{1,0:T(8,128)(2,1)}, bf16[512,2048]{1,0:T(8,128)(2,1)}, bf16[2,512,256]{2,1,0:T(8,128)(2,1)}) custom-call(s32[1]{0:T(128)} %bitcast.1.reverse, bf16[2048,48]{1,0:T(8,128)(2,1)} %bitcast.27, f32[8,2048]{1,0:T(8,128)} %pad.15.atoms_ref, bf16[2048,256]{1,0:T(8,128)(2,1)} %broadcast_select_fusion.feats_ref), custom_call_target="tpu_custom_call" | custom-call | flops 2415919104 | bytes 4194304 | tf_op jit(solution)/shard_map/structure/pallas_call | solution.py:92
  17.1 4.2 %collective-permute-start.39 = (f32[3,256]{1,0:T(4,128)S(1)}, f32[3,256]{1,0:T(4,128)S(1)}, u32[]{:S(2)}, u32[]{:S(2)}) collective-permute-start(f32[3,256]{1,0:T(4,128)S(1)} %get-tuple-element.76), channel_id=1, source_target_pairs={{2,0},{4,2},{6,4},{8,6},{10,8},{12,10},{14,12},{16,14},{18,16},{20... | collective-permute-start | bytes 9224 | tf_op jit(solution)/shard_map/ppermute | solution.py:368
  21.4 6.8 %structure.14 = (bf16[512,2048]{1,0:T(8,128)(2,1)}, bf16[512,2048]{1,0:T(8,128)(2,1)}, f32[2,512,256]{2,1,0:T(8,128)}) custom-call(s32[1]{0:T(128)} %bitcast.1.reverse, bf16[2048,48]{1,0:T(8,128)(2,1)} %bitcast.28, f32[8,2048]{1,0:T(8,128)} %pad.15.atoms_ref, bf16[2048,256]{1,0:T(8,128)(2,1)} %broadcast_select_fusion.feats_ref), custom_call_target="tpu_custom_call" | custom-call | flops 2415919104 | bytes 4194304 | tf_op jit(solution)/shard_map/structure/pallas_call | solution.py:92
  28.1 1.0 fusion.19
  29.1 6.8 %structure.13 = (bf16[512,2048]{1,0:T(8,128)(2,1)}, bf16[512,2048]{1,0:T(8,128)(2,1)}, bf16[2,512,256]{2,1,0:T(8,128)(2,1)}) custom-call(s32[1]{0:T(128)} %bitcast.1.reverse, bf16[2048,48]{1,0:T(8,128)(2,1)} %bitcast.29, f32[8,2048]{1,0:T(8,128)} %pad.15.atoms_ref, bf16[2048,256]{1,0:T(8,128)(2,1)} %broadcast_select_fusion.feats_ref), custom_call_target="tpu_custom_call" | custom-call | flops 2415919104 | bytes 4194304 | tf_op jit(solution)/shard_map/structure/pallas_call | solution.py:92
  36.0 6.9 %structure.12 = (bf16[512,2048]{1,0:T(8,128)(2,1)}, bf16[512,2048]{1,0:T(8,128)(2,1)}, f32[2,512,256]{2,1,0:T(8,128)}) custom-call(s32[1]{0:T(128)} %bitcast.1.reverse, bf16[2048,48]{1,0:T(8,128)(2,1)} %bitcast.30, f32[8,2048]{1,0:T(8,128)} %pad.15.atoms_ref, bf16[2048,256]{1,0:T(8,128)(2,1)} %broadcast_select_fusion.feats_ref), custom_call_target="tpu_custom_call" | custom-call | flops 2415919104 | bytes 4194304 | tf_op jit(solution)/shard_map/structure/pallas_call | solution.py:92
  45.0 1.0 fusion.18
  46.8 3.5 %collective-permute-done.7 = f32[8,128]{1,0:T(8,128)S(1)} collective-permute-done((f32[8,128]{1,0:T(8,128)S(1)}, f32[8,128]{1,0:T(8,128)S(1)}, u32[]{:S(2)}, u32[]{:S(2)}) %collective-permute-start.7) | collective-permute-done | bytes 4128 | tf_op jit(solution)/shard_map/ppermute | solution.py:315
  50.3 3.3 %collective-permute-start.41 = (bf16[256,256]{1,0:T(8,128)(2,1)S(1)}, bf16[256,256]{1,0:T(8,128)(2,1)S(1)}, u32[]{:S(2)}, u32[]{:S(2)}) collective-permute-start(bf16[256,256]{1,0:T(8,128)(2,1)S(1)} %get-tuple-element.69), channel_id=1, source_target_pairs={{2,0},{4,2},{6,4},{8,6},{10,8},{12,10},{14,12},{16,14},{18,16},{20... | collective-permute-start | bytes 393224 | tf_op jit(solution)/shard_map/ppermute | solution.py:366
  53.7 3.5 %collective-permute-done.8 = f32[8,128]{1,0:T(8,128)S(1)} collective-permute-done((f32[8,128]{1,0:T(8,128)S(1)}, f32[8,128]{1,0:T(8,128)S(1)}, u32[]{:S(2)}, u32[]{:S(2)}) %collective-permute-start.8) | collective-permute-done | bytes 4128 | tf_op jit(solution)/shard_map/ppermute | solution.py:315
  57.8 3.9 %collective-permute-done.9 = f32[8,128]{1,0:T(8,128)S(1)} collective-permute-done((f32[8,128]{1,0:T(8,128)S(1)}, f32[8,128]{1,0:T(8,128)S(1)}, u32[]{:S(2)}, u32[]{:S(2)}) %collective-permute-start.9) | collective-permute-done | bytes 4128 | tf_op jit(solution)/shard_map/ppermute | solution.py:315
  63.6 1.0 copy.19
  64.6 6.7 %structure.11 = (bf16[512,2048]{1,0:T(8,128)(2,1)}, bf16[512,2048]{1,0:T(8,128)(2,1)}, bf16[2,512,256]{2,1,0:T(8,128)(2,1)}) custom-call(s32[1]{0:T(128)} %bitcast.1.reverse, bf16[2048,48]{1,0:T(8,128)(2,1)} %bitcast.31, f32[8,2048]{1,0:T(8,128)} %pad.15.atoms_ref, bf16[2048,256]{1,0:T(8,128)(2,1)} %broadcast_select_fusion.feats_ref), custom_call_target="tpu_custom_call" | custom-call | flops 2415919104 | bytes 4194304 | tf_op jit(solution)/shard_map/structure/pallas_call | solution.py:92
  71.3 6.8 %structure.10 = (bf16[512,2048]{1,0:T(8,128)(2,1)}, bf16[512,2048]{1,0:T(8,128)(2,1)}, f32[2,512,256]{2,1,0:T(8,128)}) custom-call(s32[1]{0:T(128)} %bitcast.1.reverse, bf16[2048,48]{1,0:T(8,128)(2,1)} %bitcast.32, f32[8,2048]{1,0:T(8,128)} %pad.15.atoms_ref, bf16[2048,256]{1,0:T(8,128)(2,1)} %broadcast_select_fusion.feats_ref), custom_call_target="tpu_custom_call" | custom-call | flops 2415919104 | bytes 4194304 | tf_op jit(solution)/shard_map/structure/pallas_call | solution.py:92
  78.2 6.8 %structure.9 = (bf16[512,2048]{1,0:T(8,128)(2,1)}, bf16[512,2048]{1,0:T(8,128)(2,1)}, bf16[2,512,256]{2,1,0:T(8,128)(2,1)}) custom-call(s32[1]{0:T(128)} %bitcast.1.reverse, bf16[2048,48]{1,0:T(8,128)(2,1)} %bitcast.33, f32[8,2048]{1,0:T(8,128)} %pad.15.atoms_ref, bf16[2048,256]{1,0:T(8,128)(2,1)} %broadcast_select_fusion.feats_ref), custom_call_target="tpu_custom_call" | custom-call | flops 2415919104 | bytes 4194304 | tf_op jit(solution)/shard_map/structure/pallas_call | solution.py:92
  85.0 6.9 %structure.8 = (bf16[512,2048]{1,0:T(8,128)(2,1)}, bf16[512,2048]{1,0:T(8,128)(2,1)}, f32[2,512,256]{2,1,0:T(8,128)}) custom-call(s32[1]{0:T(128)} %bitcast.1.reverse, bf16[2048,48]{1,0:T(8,128)(2,1)} %bitcast.34, f32[8,2048]{1,0:T(8,128)} %pad.15.atoms_ref, bf16[2048,256]{1,0:T(8,128)(2,1)} %broadcast_select_fusion.feats_ref), custom_call_target="tpu_custom_call" | custom-call | flops 2415919104 | bytes 4194304 | tf_op jit(solution)/shard_map/structure/pallas_call | solution.py:92
  94.1 1.0 collective-permute-start.23
  95.2 1.1 collective-permute-start.15
  96.5 5.5 %collective-permute-done.31 = bf16[2,256,256]{2,1,0:T(8,128)(2,1)S(1)} collective-permute-done((bf16[2,256,256]{2,1,0:T(8,128)(2,1)S(1)}, bf16[2,256,256]{2,1,0:T(8,128)(2,1)S(1)}, u32[]{:S(2)}, u32[]{:S(2)}) %collective-permute-start.31) | collective-permute-done | bytes 262176 | tf_op jit(solution)/shard_map/ppermute | solution.py:315
  102.0 5.5 %collective-permute-done.23 = bf16[2,256,256]{2,1,0:T(8,128)(2,1)S(1)} collective-permute-done((bf16[2,256,256]{2,1,0:T(8,128)(2,1)S(1)}, bf16[2,256,256]{2,1,0:T(8,128)(2,1)S(1)}, u32[]{:S(2)}, u32[]{:S(2)}) %collective-permute-start.23) | collective-permute-done | bytes 262176 | tf_op jit(solution)/shard_map/ppermute | solution.py:315
  107.6 1.4 collective-permute-start.32
  109.1 4.1 %collective-permute-done.15 = bf16[2,256,256]{2,1,0:T(8,128)(2,1)S(1)} collective-permute-done((bf16[2,256,256]{2,1,0:T(8,128)(2,1)S(1)}, bf16[2,256,256]{2,1,0:T(8,128)(2,1)S(1)}, u32[]{:S(2)}, u32[]{:S(2)}) %collective-permute-start.15) | collective-permute-done | bytes 262176 | tf_op jit(solution)/shard_map/ppermute | solution.py:315
  113.2 1.4 collective-permute-start.24
  114.7 3.4 %collective-permute-done.2 = bf16[2,256,256]{2,1,0:T(8,128)(2,1)S(1)} collective-permute-done((bf16[2,256,256]{2,1,0:T(8,128)(2,1)S(1)}, bf16[2,256,256]{2,1,0:T(8,128)(2,1)S(1)}, u32[]{:S(2)}, u32[]{:S(2)}) %collective-permute-start.2) | collective-permute-done | bytes 262176 | tf_op jit(solution)/shard_map/ppermute | solution.py:315
  118.1 1.4 collective-permute-start.16
  120.4 4.6 %collective-permute-done.16 = bf16[2,128,256]{2,1,0:T(8,128)(2,1)S(1)} collective-permute-done((bf16[2,128,256]{2,1,0:T(8,128)(2,1)S(1)}, bf16[2,128,256]{2,1,0:T(8,128)(2,1)S(1)}, u32[]{:S(2)}, u32[]{:S(2)}) %collective-permute-start.16) | collective-permute-done | bytes 131104 | tf_op jit(solution)/shard_map/ppermute | solution.py:315
  125.1 2.3 collective-permute-done.3
  128.2 2.7 %collective-permute-start.4 = (bf16[2,64,256]{2,1,0:T(8,128)(2,1)S(1)}, bf16[2,64,256]{2,1,0:T(8,128)(2,1)S(1)}, u32[]{:S(2)}, u32[]{:S(2)}) collective-permute-start(bf16[2,64,256]{2,1,0:T(8,128)(2,1)S(1)} %slice.225), channel_id=1, source_target_pairs={{0,16},{2,18},{4,20},{6,22},{8,24},{10,26},{12,28},{14,30},{16,0},... | collective-permute-start | bytes 196616 | tf_op jit(solution)/shard_map/ppermute | solution.py:315
  130.9 3.3 %collective-permute-done.25 = bf16[2,64,256]{2,1,0:T(8,128)(2,1)S(1)} collective-permute-done((bf16[2,64,256]{2,1,0:T(8,128)(2,1)S(1)}, bf16[2,64,256]{2,1,0:T(8,128)(2,1)S(1)}, u32[]{:S(2)}, u32[]{:S(2)}) %collective-permute-start.25) | collective-permute-done | bytes 65568 | tf_op jit(solution)/shard_map/ppermute | solution.py:315
  134.3 2.1 collective-permute-done.17
  136.3 0.9 collective-permute-start.26
  137.3 1.9 collective-permute-done.4
  139.4 2.6 %collective-permute-done.34 = bf16[2,64,256]{2,1,0:T(8,128)(2,1)S(1)} collective-permute-done((bf16[2,64,256]{2,1,0:T(8,128)(2,1)S(1)}, bf16[2,64,256]{2,1,0:T(8,128)(2,1)S(1)}, u32[]{:S(2)}, u32[]{:S(2)}) %collective-permute-start.34) | collective-permute-done | bytes 65568 | tf_op jit(solution)/shard_map/ppermute | solution.py:315
  142.2 1.7 collective-permute-done.26
  143.9 1.0 collective-permute-start.35
  146.0 1.7 collective-permute-done.10
  148.0 2.5 %collective-permute-done.35 = bf16[2,128,256]{2,1,0:T(8,128)(2,1)S(1)} collective-permute-done((bf16[2,128,256]{2,1,0:T(8,128)(2,1)S(1)}, bf16[2,128,256]{2,1,0:T(8,128)(2,1)S(1)}, u32[]{:S(2)}, u32[]{:S(2)}) %collective-permute-start.35) | collective-permute-done | bytes 131104 | tf_op jit(solution)/shard_map/ppermute | solution.py:315
  151.3 2.0 collective-permute-done.27
  153.3 0.9 collective-permute-start.36
  154.2 1.5 collective-permute-done.19
  155.7 1.5 collective-permute-start.44
  157.3 1.1 collective-permute-start.28
  158.4 2.8 %collective-permute-done.36 = bf16[2,256,256]{2,1,0:T(8,128)(2,1)S(1)} collective-permute-done((bf16[2,256,256]{2,1,0:T(8,128)(2,1)S(1)}, bf16[2,256,256]{2,1,0:T(8,128)(2,1)S(1)}, u32[]{:S(2)}, u32[]{:S(2)}) %collective-permute-start.36) | collective-permute-done | bytes 262176 | tf_op jit(solution)/shard_map/ppermute | solution.py:315
  161.2 0.8 collective-permute-start.20
  162.1 1.3 collective-permute-start.12
  164.0 10.8 %near.1.refs_6_ = f32[2048,256]{1,0:T(8,128)} custom-call(s32[16,3]{1,0:T(8,128)} %broadcast_add_fusion.places, f32[4]{0:T(128)} %broadcast_multiply_fusion.2.scales, f32[20,8,128]{2,1,0:T(8,128)} %fusion.12.row_ref, bf16[2,128,256]{2,1,0:T(8,128)(2,1)} %bitcast.35, bf16[16,128,256]{2,1,0:T(8,128)(2,1)} %bitcast.26, bf16[2,128,256]{2,1,0:T(8,128)(2,1)} %bitcast.36, ...), custom_call_target="tpu_custom_call" | custom-call | flops 6442450944 | bytes 4194304 | tf_op jit(solution)/shard_map/near/pallas_call | solution.py:167
  174.8 1.6 collective-permute-start.43
  177.1 1.0 pad_maximum_fusion.1.refs_4_
  178.3 7.7 %messages.5.refs_6_ = f32[2048,256]{1,0:T(8,128)} custom-call(bf16[512,2048]{1,0:T(8,128)(2,1)} %get-tuple-element.53.refs_0_, bf16[512,2048]{1,0:T(8,128)(2,1)} %get-tuple-element.54.refs_1_, bf16[512,2048]{1,0:T(8,128)(2,1)} %get-tuple-element.55.refs_2_, bf16[512,2048]{1,0:T(8,128)(2,1)} %get-tuple-element.56.refs_3_, bf16[2,512,256]{2,1,0:T(8,128)(2,1)} %copy-done.9, ...), custom_call_target="tpu_custom_call" | custom-call | flops 4294967296 | bytes 12582912 | tf_op jit(solution)/shard_map/messages/pallas_call | solution.py:229
  186.0 7.7 %messages.6.refs_6_ = f32[2048,256]{1,0:T(8,128)} custom-call(bf16[512,2048]{1,0:T(8,128)(2,1)} %get-tuple-element.47.refs_0_, bf16[512,2048]{1,0:T(8,128)(2,1)} %get-tuple-element.48.refs_1_, bf16[512,2048]{1,0:T(8,128)(2,1)} %get-tuple-element.49.refs_2_, bf16[512,2048]{1,0:T(8,128)(2,1)} %get-tuple-element.50.refs_3_, bf16[2,512,256]{2,1,0:T(8,128)(2,1)} %copy-done.10, ...), custom_call_target="tpu_custom_call" | custom-call | flops 4294967296 | bytes 12582912 | tf_op jit(solution)/shard_map/messages/pallas_call | solution.py:229
  193.7 7.7 %messages.7.refs_6_ = f32[2048,256]{1,0:T(8,128)} custom-call(bf16[512,2048]{1,0:T(8,128)(2,1)} %get-tuple-element.41.refs_0_, bf16[512,2048]{1,0:T(8,128)(2,1)} %get-tuple-element.42.refs_1_, bf16[512,2048]{1,0:T(8,128)(2,1)} %get-tuple-element.43.refs_2_, bf16[512,2048]{1,0:T(8,128)(2,1)} %get-tuple-element.44.refs_3_, bf16[2,512,256]{2,1,0:T(8,128)(2,1)} %copy-done.11, ...), custom_call_target="tpu_custom_call" | custom-call | flops 4294967296 | bytes 12582912 | tf_op jit(solution)/shard_map/messages/pallas_call | solution.py:229
  202.2 4.9 %messages.8 = (f32[1024,256]{1,0:T(8,128)}, bf16[512,256]{1,0:T(8,128)(2,1)}, bf16[512,256]{1,0:T(8,128)(2,1)}) custom-call(bf16[512,2048]{1,0:T(8,128)(2,1)} %get-tuple-element.35.refs_0_, bf16[512,2048]{1,0:T(8,128)(2,1)} %get-tuple-element.36.refs_1_, bf16[512,2048]{1,0:T(8,128)(2,1)} %get-tuple-element.37.refs_2_, ...), custom_call_target="tpu_custom_call" | custom-call | flops 2147483648 | bytes 6291456 | tf_op jit(solution)/shard_map/messages/pallas_call | solution.py:229
  207.1 1.4 collective-permute-start.42
  209.8 4.9 %messages.9 = (f32[1024,256]{1,0:T(8,128)}, bf16[512,256]{1,0:T(8,128)(2,1)}, bf16[512,256]{1,0:T(8,128)(2,1)}) custom-call(bf16[512,2048]{1,0:T(8,128)(2,1)} %get-tuple-element.35.refs_0_, bf16[512,2048]{1,0:T(8,128)(2,1)} %get-tuple-element.36.refs_1_, bf16[512,2048]{1,0:T(8,128)(2,1)} %get-tuple-element.37.refs_2_, ...), custom_call_target="tpu_custom_call" | custom-call | flops 2147483648 | bytes 6291456 | tf_op jit(solution)/shard_map/messages/pallas_call | solution.py:229
  214.7 1.4 collective-permute-start.46
  217.5 3.8 %mlp.4 = bf16[512,256]{1,0:T(8,128)(2,1)} custom-call(s32[1]{0:T(128)} %bitcast.side, f32[1024,256]{1,0:T(8,128)} %get-tuple-element.59.own_ref, bf16[512,256]{1,0:T(8,128)(2,1)} %copy-done.21, f32[2,256]{1,0:T(2,128)} %reshape.54.gain_ref, bf16[512,512]{1,0:T(8,128)(2,1)} %in0_ref.7, bf16[512,512]{1,0:T(8,128)(2,1)} %collective-permute-done.43.in1_ref, ...), custom_call_target="tpu_custom_call" | custom-call | flops 1610612736 | bytes 1048576 | tf_op jit(solution)/shard_map/mlp/pallas_call | solution.py:277
  222.8 3.9 %mlp.5 = bf16[512,256]{1,0:T(8,128)(2,1)} custom-call(s32[1]{0:T(128)} %bitcast.side, f32[1024,256]{1,0:T(8,128)} %get-tuple-element.59.own_ref, bf16[512,256]{1,0:T(8,128)(2,1)} %copy-done.20, f32[2,256]{1,0:T(2,128)} %reshape.54.gain_ref, bf16[512,512]{1,0:T(8,128)(2,1)} %in0_ref.7, bf16[512,512]{1,0:T(8,128)(2,1)} %collective-permute-done.43.in1_ref, ...), custom_call_target="tpu_custom_call" | custom-call | flops 1610612736 | bytes 1048576 | tf_op jit(solution)/shard_map/mlp/pallas_call | solution.py:277
  226.7 1.1 collective-permute-done.46.other_ref
  228.5 3.8 %mlp.6 = bf16[512,256]{1,0:T(8,128)(2,1)} custom-call(s32[1]{0:T(128)} %bitcast.side, f32[1024,256]{1,0:T(8,128)} %get-tuple-element.62.own_ref, bf16[512,256]{1,0:T(8,128)(2,1)} %copy-done.23, f32[2,256]{1,0:T(2,128)} %reshape.54.gain_ref, bf16[512,512]{1,0:T(8,128)(2,1)} %in0_ref.7, bf16[512,512]{1,0:T(8,128)(2,1)} %collective-permute-done.43.in1_ref, ...), custom_call_target="tpu_custom_call" | custom-call | flops 1610612736 | bytes 1048576 | tf_op jit(solution)/shard_map/mlp/pallas_call | solution.py:277
  233.5 3.9 %mlp.7 = bf16[512,256]{1,0:T(8,128)(2,1)} custom-call(s32[1]{0:T(128)} %bitcast.side, f32[1024,256]{1,0:T(8,128)} %get-tuple-element.62.own_ref, bf16[512,256]{1,0:T(8,128)(2,1)} %copy-done.22, f32[2,256]{1,0:T(2,128)} %reshape.54.gain_ref, bf16[512,512]{1,0:T(8,128)(2,1)} %in0_ref.7, bf16[512,512]{1,0:T(8,128)(2,1)} %collective-permute-done.43.in1_ref, ...), custom_call_target="tpu_custom_call" | custom-call | flops 1610612736 | bytes 1048576 | tf_op jit(solution)/shard_map/mlp/pallas_call | solution.py:277
  237.4 2.0 pad_maximum_fusion
  (187 shorter events, 23.8 us)
Async XLA Ops:
  0.0 46.0 %copy-start = (f32[4,512]{1,0:T(4,128)S(1)}, f32[4,512]{1,0:T(4,128)}, u32[]{:S(2)}) copy-start(f32[4,512]{1,0:T(4,128)} %param.19) | copy-start | bytes 24580
  0.0 7.9 %copy-start.15 = (f32[3,2048]{1,0:T(4,128)S(1)}, f32[3,2048]{1,0:T(4,128)}, u32[]{:S(2)}) copy-start(f32[3,2048]{1,0:T(4,128)} %param.13) | copy-start | bytes 73732
  0.0 62.9 %collective-permute-start = (f32[3,2048]{1,0:T(4,128)}, f32[3,2048]{1,0:T(4,128)S(1)}, u32[]{:S(2)}, u32[]{:S(2)}) collective-permute-start(f32[3,2048]{1,0:T(4,128)} %param.16), channel_id=1, source_target_pairs={{0,1},{1,0},{2,3},{3,2},{4,5},{5,4},{6,7},{7,6},{8,9},{9,8},{10,11... | collective-permute-start | bytes 73736 | tf_op jit(solution)/shard_map/ppermute | solution.py:310
  8.5 6.7 %copy-start.18 = (s32[16]{0:T(128)S(1)}, s32[16]{0:T(128)}, u32[]{:S(2)}) copy-start(s32[16]{0:T(128)} %param.14) | copy-start | bytes 196
  15.2 76.9 %collective-permute-start.30 = (bf16[2,512,256]{2,1,0:T(8,128)(2,1)}, bf16[2,512,256]{2,1,0:T(8,128)(2,1)S(1)}, u32[]{:S(2)}, u32[]{:S(2)}) collective-permute-start(bf16[2,512,256]{2,1,0:T(8,128)(2,1)} %get-tuple-element.58), channel_id=1, source_target_pairs={{0,2},{2,0},{4,6},{6,4},{8,10},{10,8},{12,14},{14,12},{16,18},{18,... | collective-permute-start | bytes 1572872 | tf_op jit(solution)/shard_map/ppermute | solution.py:315
  16.6 30.0 %collective-permute-start.6 = (f32[8,128]{1,0:T(8,128)S(1)}, f32[8,128]{1,0:T(8,128)S(1)}, u32[]{:S(2)}, u32[]{:S(2)}) collective-permute-start(f32[8,128]{1,0:T(8,128)S(1)} %broadcast_in_dim.14), channel_id=1, source_target_pairs={{0,2},{2,0},{4,6},{6,4},{8,10},{10,8},{12,14},{14,12},{16,18},{18,... | collective-permute-start | bytes 12296 | tf_op jit(solution)/shard_map/ppermute | solution.py:315
  17.1 29.5 %collective-permute-start.39 = (f32[3,256]{1,0:T(4,128)S(1)}, f32[3,256]{1,0:T(4,128)S(1)}, u32[]{:S(2)}, u32[]{:S(2)}) collective-permute-start(f32[3,256]{1,0:T(4,128)S(1)} %get-tuple-element.76), channel_id=1, source_target_pairs={{2,0},{4,2},{6,4},{8,6},{10,8},{12,10},{14,12},{16,14},{18,16},{20... | collective-permute-start | bytes 9224 | tf_op jit(solution)/shard_map/ppermute | solution.py:368
  21.4 32.2 %collective-permute-start.38 = (f32[3,256]{1,0:T(4,128)S(1)}, f32[3,256]{1,0:T(4,128)S(1)}, u32[]{:S(2)}, u32[]{:S(2)}) collective-permute-start(f32[3,256]{1,0:T(4,128)S(1)} %get-tuple-element.75), channel_id=1, source_target_pairs={{0,2},{2,4},{4,6},{6,8},{8,10},{10,12},{12,14},{14,16},{16,18},{18... | collective-permute-start | bytes 9224 | tf_op jit(solution)/shard_map/ppermute | solution.py:367
  36.0 6.9 %copy-start.16 = (s32[16,3]{0,1:T(4,128)S(1)}, s32[16,3]{0,1:T(4,128)}, u32[]{:S(2)}) copy-start(s32[16,3]{0,1:T(4,128)} %param.15) | copy-start | bytes 580
  36.0 7.0 %copy-start.26 = (f32[4]{0:T(128)S(1)}, f32[4]{0:T(128)}, u32[]{:S(2)}) copy-start(f32[4]{0:T(128)} %param.18) | copy-start | bytes 52
  36.0 8.2 %copy-start.8 = (bf16[512,512]{1,0:T(8,128)(2,1)S(1)}, bf16[512,512]{1,0:T(8,128)(2,1)}, u32[]{:S(2)}) copy-start(bf16[512,512]{1,0:T(8,128)(2,1)} %param.22) | copy-start | bytes 1572868
  36.0 10.0 %copy-start.19 = (f32[3,1]{0,1:T(1,128)S(1)}, f32[3,1]{0,1:T(1,128)}, u32[]{:S(2)}) copy-start(f32[3,1]{0,1:T(1,128)} %constant.48.clone) | copy-start | bytes 40
  46.6 115.5 %collective-permute-start.40 = (bf16[256,256]{1,0:T(8,128)(2,1)S(1)}, bf16[256,256]{1,0:T(8,128)(2,1)S(1)}, u32[]{:S(2)}, u32[]{:S(2)}) collective-permute-start(bf16[256,256]{1,0:T(8,128)(2,1)S(1)} %get-tuple-element.70), channel_id=1, source_target_pairs={{0,2},{2,4},{4,6},{6,8},{8,10},{10,12},{12,14},{14,16},{16,18},{18... | collective-permute-start | bytes 393224 | tf_op jit(solution)/shard_map/ppermute | solution.py:365
  46.6 3.7 %collective-permute-start.7 = (f32[8,128]{1,0:T(8,128)S(1)}, f32[8,128]{1,0:T(8,128)S(1)}, u32[]{:S(2)}, u32[]{:S(2)}) collective-permute-start(f32[8,128]{1,0:T(8,128)S(1)} %broadcast_add_fusion.2), channel_id=1, source_target_pairs={{0,4},{2,6},{4,0},{6,2},{8,12},{10,14},{12,8},{14,10},{16,20},{18,... | collective-permute-start | bytes 12296 | tf_op jit(solution)/shard_map/ppermute | solution.py:315
  50.3 113.1 %collective-permute-start.41 = (bf16[256,256]{1,0:T(8,128)(2,1)S(1)}, bf16[256,256]{1,0:T(8,128)(2,1)S(1)}, u32[]{:S(2)}, u32[]{:S(2)}) collective-permute-start(bf16[256,256]{1,0:T(8,128)(2,1)S(1)} %get-tuple-element.69), channel_id=1, source_target_pairs={{2,0},{4,2},{6,4},{8,6},{10,8},{12,10},{14,12},{16,14},{18,16},{20... | collective-permute-start | bytes 393224 | tf_op jit(solution)/shard_map/ppermute | solution.py:366
  53.6 3.6 %collective-permute-start.8 = (f32[8,128]{1,0:T(8,128)S(1)}, f32[8,128]{1,0:T(8,128)S(1)}, u32[]{:S(2)}, u32[]{:S(2)}) collective-permute-start(f32[8,128]{1,0:T(8,128)S(1)} %fusion.21), channel_id=1, source_target_pairs={{0,8},{2,10},{4,12},{6,14},{8,0},{10,2},{12,4},{14,6},{16,24},{18,... | collective-permute-start | bytes 12296 | tf_op jit(solution)/shard_map/ppermute | solution.py:315
  57.2 4.5 %collective-permute-start.9 = (f32[8,128]{1,0:T(8,128)S(1)}, f32[8,128]{1,0:T(8,128)S(1)}, u32[]{:S(2)}, u32[]{:S(2)}) collective-permute-start(f32[8,128]{1,0:T(8,128)S(1)} %add.129), channel_id=1, source_target_pairs={{0,16},{2,18},{4,20},{6,22},{8,24},{10,26},{12,28},{14,30},{16,0},... | collective-permute-start | bytes 12296 | tf_op jit(solution)/shard_map/ppermute | solution.py:315
  61.7 31.0 %collective-permute-start.22 = (bf16[2,512,256]{2,1,0:T(8,128)(2,1)}, bf16[2,512,256]{2,1,0:T(8,128)(2,1)S(1)}, u32[]{:S(2)}, u32[]{:S(2)}) collective-permute-start(bf16[2,512,256]{2,1,0:T(8,128)(2,1)} %get-tuple-element.52), channel_id=1, source_target_pairs={{0,2},{2,0},{4,6},{6,4},{8,10},{10,8},{12,14},{14,12},{16,18},{18,... | collective-permute-start | bytes 1572872 | tf_op jit(solution)/shard_map/ppermute | solution.py:315
  62.9 29.0 %collective-permute-start.5 = (f32[2,64,256]{2,1,0:T(8,128)S(1)}, f32[2,64,256]{2,1,0:T(8,128)S(1)}, u32[]{:S(2)}, u32[]{:S(2)}) collective-permute-start(f32[2,64,256]{2,1,0:T(8,128)S(1)} %pad_maximum_fusion.9), channel_id=1, source_target_pairs={{0,1},{1,0},{2,3},{3,2},{4,5},{5,4},{6,7},{7,6},{8,9},{9,8},{10,11... | collective-permute-start | bytes 393224 | tf_op jit(solution)/shard_map/ppermute | solution.py:310
  85.0 7.6 %copy-start.4 = (f32[2,512,256]{2,1,0:T(8,128)S(1)}, f32[2,512,256]{2,1,0:T(8,128)}, u32[]{:S(2)}) copy-start(f32[2,512,256]{2,1,0:T(8,128)} %get-tuple-element.57) | copy-start | bytes 3145732
  91.9 2.2 collective-permute-start.14
  92.2 3.0 %collective-permute-start.1 = (bf16[2,512,256]{2,1,0:T(8,128)(2,1)}, bf16[2,512,256]{2,1,0:T(8,128)(2,1)S(1)}, u32[]{:S(2)}, u32[]{:S(2)}) collective-permute-start(bf16[2,512,256]{2,1,0:T(8,128)(2,1)} %get-tuple-element.40), channel_id=1, source_target_pairs={{0,2},{2,0},{4,6},{6,4},{8,10},{10,8},{12,14},{14,12},{16,18},{18,... | collective-permute-start | bytes 1572872 | tf_op jit(solution)/shard_map/ppermute | solution.py:315
  92.7 9.2 %collective-permute-start.31 = (bf16[2,256,256]{2,1,0:T(8,128)(2,1)S(1)}, bf16[2,256,256]{2,1,0:T(8,128)(2,1)S(1)}, u32[]{:S(2)}, u32[]{:S(2)}) collective-permute-start(bf16[2,256,256]{2,1,0:T(8,128)(2,1)S(1)} %slice.214), channel_id=1, source_target_pairs={{0,4},{2,6},{4,0},{6,2},{8,12},{10,14},{12,8},{14,10},{16,20},{18,... | collective-permute-start | bytes 786440 | tf_op jit(solution)/shard_map/ppermute | solution.py:315
  94.1 13.5 %collective-permute-start.23 = (bf16[2,256,256]{2,1,0:T(8,128)(2,1)S(1)}, bf16[2,256,256]{2,1,0:T(8,128)(2,1)S(1)}, u32[]{:S(2)}, u32[]{:S(2)}) collective-permute-start(bf16[2,256,256]{2,1,0:T(8,128)(2,1)S(1)} %slice.215), channel_id=1, source_target_pairs={{0,4},{2,6},{4,0},{6,2},{8,12},{10,14},{12,8},{14,10},{16,20},{18,... | collective-permute-start | bytes 786440 | tf_op jit(solution)/shard_map/ppermute | solution.py:315
  95.2 18.0 %collective-permute-start.15 = (bf16[2,256,256]{2,1,0:T(8,128)(2,1)S(1)}, bf16[2,256,256]{2,1,0:T(8,128)(2,1)S(1)}, u32[]{:S(2)}, u32[]{:S(2)}) collective-permute-start(bf16[2,256,256]{2,1,0:T(8,128)(2,1)S(1)} %slice.216), channel_id=1, source_target_pairs={{0,4},{2,6},{4,0},{6,2},{8,12},{10,14},{12,8},{14,10},{16,20},{18,... | collective-permute-start | bytes 786440 | tf_op jit(solution)/shard_map/ppermute | solution.py:315
  101.9 16.1 %collective-permute-start.2 = (bf16[2,256,256]{2,1,0:T(8,128)(2,1)S(1)}, bf16[2,256,256]{2,1,0:T(8,128)(2,1)S(1)}, u32[]{:S(2)}, u32[]{:S(2)}) collective-permute-start(bf16[2,256,256]{2,1,0:T(8,128)(2,1)S(1)} %slice.217), channel_id=1, source_target_pairs={{0,4},{2,6},{4,0},{6,2},{8,12},{10,14},{12,8},{14,10},{16,20},{18,... | collective-permute-start | bytes 786440 | tf_op jit(solution)/shard_map/ppermute | solution.py:315
  107.6 12.0 %collective-permute-start.32 = (bf16[2,128,256]{2,1,0:T(8,128)(2,1)S(1)}, bf16[2,128,256]{2,1,0:T(8,128)(2,1)S(1)}, u32[]{:S(2)}, u32[]{:S(2)}) collective-permute-start(bf16[2,128,256]{2,1,0:T(8,128)(2,1)S(1)} %slice.218), channel_id=1, source_target_pairs={{0,8},{2,10},{4,12},{6,14},{8,0},{10,2},{12,4},{14,6},{16,24},{18,... | collective-permute-start | bytes 393224 | tf_op jit(solution)/shard_map/ppermute | solution.py:315
  113.2 7.1 %collective-permute-start.24 = (bf16[2,128,256]{2,1,0:T(8,128)(2,1)S(1)}, bf16[2,128,256]{2,1,0:T(8,128)(2,1)S(1)}, u32[]{:S(2)}, u32[]{:S(2)}) collective-permute-start(bf16[2,128,256]{2,1,0:T(8,128)(2,1)S(1)} %slice.219), channel_id=1, source_target_pairs={{0,8},{2,10},{4,12},{6,14},{8,0},{10,2},{12,4},{14,6},{16,24},{18,... | collective-permute-start | bytes 393224 | tf_op jit(solution)/shard_map/ppermute | solution.py:315
  118.1 7.0 %collective-permute-start.16 = (bf16[2,128,256]{2,1,0:T(8,128)(2,1)S(1)}, bf16[2,128,256]{2,1,0:T(8,128)(2,1)S(1)}, u32[]{:S(2)}, u32[]{:S(2)}) collective-permute-start(bf16[2,128,256]{2,1,0:T(8,128)(2,1)S(1)} %slice.220), channel_id=1, source_target_pairs={{0,8},{2,10},{4,12},{6,14},{8,0},{10,2},{12,4},{14,6},{16,24},{18,... | collective-permute-start | bytes 393224 | tf_op jit(solution)/shard_map/ppermute | solution.py:315
  119.6 7.8 %collective-permute-start.3 = (bf16[2,128,256]{2,1,0:T(8,128)(2,1)S(1)}, bf16[2,128,256]{2,1,0:T(8,128)(2,1)S(1)}, u32[]{:S(2)}, u32[]{:S(2)}) collective-permute-start(bf16[2,128,256]{2,1,0:T(8,128)(2,1)S(1)} %slice.221), channel_id=1, source_target_pairs={{0,8},{2,10},{4,12},{6,14},{8,0},{10,2},{12,4},{14,6},{16,24},{18,... | collective-permute-start | bytes 393224 | tf_op jit(solution)/shard_map/ppermute | solution.py:315
  120.3 7.8 %collective-permute-start.33 = (bf16[2,64,256]{2,1,0:T(8,128)(2,1)S(1)}, bf16[2,64,256]{2,1,0:T(8,128)(2,1)S(1)}, u32[]{:S(2)}, u32[]{:S(2)}) collective-permute-start(bf16[2,64,256]{2,1,0:T(8,128)(2,1)S(1)} %slice.222), channel_id=1, source_target_pairs={{0,16},{2,18},{4,20},{6,22},{8,24},{10,26},{12,28},{14,30},{16,0},... | collective-permute-start | bytes 196616 | tf_op jit(solution)/shard_map/ppermute | solution.py:315
  125.1 9.2 %collective-permute-start.25 = (bf16[2,64,256]{2,1,0:T(8,128)(2,1)S(1)}, bf16[2,64,256]{2,1,0:T(8,128)(2,1)S(1)}, u32[]{:S(2)}, u32[]{:S(2)}) collective-permute-start(bf16[2,64,256]{2,1,0:T(8,128)(2,1)S(1)} %slice.223), channel_id=1, source_target_pairs={{0,16},{2,18},{4,20},{6,22},{8,24},{10,26},{12,28},{14,30},{16,0},... | collective-permute-start | bytes 196616 | tf_op jit(solution)/shard_map/ppermute | solution.py:315
  127.4 8.9 %collective-permute-start.17 = (bf16[2,64,256]{2,1,0:T(8,128)(2,1)S(1)}, bf16[2,64,256]{2,1,0:T(8,128)(2,1)S(1)}, u32[]{:S(2)}, u32[]{:S(2)}) collective-permute-start(bf16[2,64,256]{2,1,0:T(8,128)(2,1)S(1)} %slice.224), channel_id=1, source_target_pairs={{0,16},{2,18},{4,20},{6,22},{8,24},{10,26},{12,28},{14,30},{16,0},... | collective-permute-start | bytes 196616 | tf_op jit(solution)/shard_map/ppermute | solution.py:315
  128.2 11.0 %collective-permute-start.4 = (bf16[2,64,256]{2,1,0:T(8,128)(2,1)S(1)}, bf16[2,64,256]{2,1,0:T(8,128)(2,1)S(1)}, u32[]{:S(2)}, u32[]{:S(2)}) collective-permute-start(bf16[2,64,256]{2,1,0:T(8,128)(2,1)S(1)} %slice.225), channel_id=1, source_target_pairs={{0,16},{2,18},{4,20},{6,22},{8,24},{10,26},{12,28},{14,30},{16,0},... | collective-permute-start | bytes 196616 | tf_op jit(solution)/shard_map/ppermute | solution.py:315
  134.2 7.7 %collective-permute-start.34 = (bf16[2,64,256]{2,1,0:T(8,128)(2,1)S(1)}, bf16[2,64,256]{2,1,0:T(8,128)(2,1)S(1)}, u32[]{:S(2)}, u32[]{:S(2)}) collective-permute-start(bf16[2,64,256]{2,1,0:T(8,128)(2,1)S(1)} %fusion.2), channel_id=1, source_target_pairs={{0,16},{2,18},{4,20},{6,22},{8,24},{10,26},{12,28},{14,30},{16,0},... | collective-permute-start | bytes 196616 | tf_op jit(solution)/shard_map/ppermute | solution.py:315
  136.3 7.6 %collective-permute-start.26 = (bf16[2,64,256]{2,1,0:T(8,128)(2,1)S(1)}, bf16[2,64,256]{2,1,0:T(8,128)(2,1)S(1)}, u32[]{:S(2)}, u32[]{:S(2)}) collective-permute-start(bf16[2,64,256]{2,1,0:T(8,128)(2,1)S(1)} %fusion.5), channel_id=1, source_target_pairs={{0,16},{2,18},{4,20},{6,22},{8,24},{10,26},{12,28},{14,30},{16,0},... | collective-permute-start | bytes 196616 | tf_op jit(solution)/shard_map/ppermute | solution.py:315
  139.1 6.2 %collective-permute-start.18 = (bf16[2,64,256]{2,1,0:T(8,128)(2,1)S(1)}, bf16[2,64,256]{2,1,0:T(8,128)(2,1)S(1)}, u32[]{:S(2)}, u32[]{:S(2)}) collective-permute-start(bf16[2,64,256]{2,1,0:T(8,128)(2,1)S(1)} %fusion.8), channel_id=1, source_target_pairs={{0,16},{2,18},{4,20},{6,22},{8,24},{10,26},{12,28},{14,30},{16,0},... | collective-permute-start | bytes 196616 | tf_op jit(solution)/shard_map/ppermute | solution.py:315
  141.9 5.8 %collective-permute-start.10 = (bf16[2,64,256]{2,1,0:T(8,128)(2,1)S(1)}, bf16[2,64,256]{2,1,0:T(8,128)(2,1)S(1)}, u32[]{:S(2)}, u32[]{:S(2)}) collective-permute-start(bf16[2,64,256]{2,1,0:T(8,128)(2,1)S(1)} %fusion.11), channel_id=1, source_target_pairs={{0,16},{2,18},{4,20},{6,22},{8,24},{10,26},{12,28},{14,30},{16,0},... | collective-permute-start | bytes 196616 | tf_op jit(solution)/shard_map/ppermute | solution.py:315
  143.9 6.6 %collective-permute-start.35 = (bf16[2,128,256]{2,1,0:T(8,128)(2,1)S(1)}, bf16[2,128,256]{2,1,0:T(8,128)(2,1)S(1)}, u32[]{:S(2)}, u32[]{:S(2)}) collective-permute-start(bf16[2,128,256]{2,1,0:T(8,128)(2,1)S(1)} %pad_maximum_fusion.13), channel_id=1, source_target_pairs={{0,8},{2,10},{4,12},{6,14},{8,0},{10,2},{12,4},{14,6},{16,24},{18,... | collective-permute-start | bytes 393224 | tf_op jit(solution)/shard_map/ppermute | solution.py:315
  145.3 7.9 %collective-permute-start.27 = (bf16[2,128,256]{2,1,0:T(8,128)(2,1)S(1)}, bf16[2,128,256]{2,1,0:T(8,128)(2,1)S(1)}, u32[]{:S(2)}, u32[]{:S(2)}) collective-permute-start(bf16[2,128,256]{2,1,0:T(8,128)(2,1)S(1)} %pad_maximum_fusion.12), channel_id=1, source_target_pairs={{0,8},{2,10},{4,12},{6,14},{8,0},{10,2},{12,4},{14,6},{16,24},{18,... | collective-permute-start | bytes 393224 | tf_op jit(solution)/shard_map/ppermute | solution.py:315
  147.7 8.0 %collective-permute-start.19 = (bf16[2,128,256]{2,1,0:T(8,128)(2,1)S(1)}, bf16[2,128,256]{2,1,0:T(8,128)(2,1)S(1)}, u32[]{:S(2)}, u32[]{:S(2)}) collective-permute-start(bf16[2,128,256]{2,1,0:T(8,128)(2,1)S(1)} %pad_maximum_fusion.11), channel_id=1, source_target_pairs={{0,8},{2,10},{4,12},{6,14},{8,0},{10,2},{12,4},{14,6},{16,24},{18,... | collective-permute-start | bytes 393224 | tf_op jit(solution)/shard_map/ppermute | solution.py:315
  150.5 6.8 %collective-permute-start.11 = (bf16[2,128,256]{2,1,0:T(8,128)(2,1)S(1)}, bf16[2,128,256]{2,1,0:T(8,128)(2,1)S(1)}, u32[]{:S(2)}, u32[]{:S(2)}) collective-permute-start(bf16[2,128,256]{2,1,0:T(8,128)(2,1)S(1)} %pad_maximum_fusion.10), channel_id=1, source_target_pairs={{0,8},{2,10},{4,12},{6,14},{8,0},{10,2},{12,4},{14,6},{16,24},{18,... | collective-permute-start | bytes 393224 | tf_op jit(solution)/shard_map/ppermute | solution.py:315
  153.3 7.9 %collective-permute-start.36 = (bf16[2,256,256]{2,1,0:T(8,128)(2,1)S(1)}, bf16[2,256,256]{2,1,0:T(8,128)(2,1)S(1)}, u32[]{:S(2)}, u32[]{:S(2)}) collective-permute-start(bf16[2,256,256]{2,1,0:T(8,128)(2,1)S(1)} %pad_maximum_fusion.8), channel_id=1, source_target_pairs={{0,4},{2,6},{4,0},{6,2},{8,12},{10,14},{12,8},{14,10},{16,20},{18,... | collective-permute-start | bytes 786440 | tf_op jit(solution)/shard_map/ppermute | solution.py:315
  155.7 60.4 %collective-permute-start.44 = (bf16[512,256]{1,0:T(8,128)(2,1)S(1)}, bf16[512,256]{1,0:T(8,128)(2,1)}, u32[]{:S(2)}, u32[]{:S(2)}) collective-permute-start(bf16[512,256]{1,0:T(8,128)(2,1)S(1)} %get-tuple-element.71), channel_id=1, source_target_pairs={{0,1},{1,0},{2,3},{3,2},{4,5},{5,4},{6,7},{7,6},{8,9},{9,8},{10,11... | collective-permute-start | bytes 786440 | tf_op jit(solution)/shard_map/ppermute | solution.py:310
  157.3 17.5 %collective-permute-start.28 = (bf16[2,256,256]{2,1,0:T(8,128)(2,1)S(1)}, bf16[2,256,256]{2,1,0:T(8,128)(2,1)S(1)}, u32[]{:S(2)}, u32[]{:S(2)}) collective-permute-start(bf16[2,256,256]{2,1,0:T(8,128)(2,1)S(1)} %pad_maximum_fusion.7), channel_id=1, source_target_pairs={{0,4},{2,6},{4,0},{6,2},{8,12},{10,14},{12,8},{14,10},{16,20},{18,... | collective-permute-start | bytes 786440 | tf_op jit(solution)/shard_map/ppermute | solution.py:315
  161.2 15.2 %collective-permute-start.20 = (bf16[2,256,256]{2,1,0:T(8,128)(2,1)S(1)}, bf16[2,256,256]{2,1,0:T(8,128)(2,1)S(1)}, u32[]{:S(2)}, u32[]{:S(2)}) collective-permute-start(bf16[2,256,256]{2,1,0:T(8,128)(2,1)S(1)} %pad_maximum_fusion.6), channel_id=1, source_target_pairs={{0,4},{2,6},{4,0},{6,2},{8,12},{10,14},{12,8},{14,10},{16,20},{18,... | collective-permute-start | bytes 786440 | tf_op jit(solution)/shard_map/ppermute | solution.py:315
  162.1 12.7 %copy-start.9 = (bf16[2,512,256]{2,1,0:T(8,128)(2,1)}, bf16[2,512,256]{2,1,0:T(8,128)(2,1)S(1)}, u32[]{:S(2)}) copy-start(bf16[2,512,256]{2,1,0:T(8,128)(2,1)S(1)} %pad_maximum_fusion.4.refs_4_) | copy-start | bytes 1572868
  162.1 14.5 %collective-permute-start.12 = (bf16[2,256,256]{2,1,0:T(8,128)(2,1)S(1)}, bf16[2,256,256]{2,1,0:T(8,128)(2,1)}, u32[]{:S(2)}, u32[]{:S(2)}) collective-permute-start(bf16[2,256,256]{2,1,0:T(8,128)(2,1)S(1)} %pad_maximum_fusion.5), channel_id=1, source_target_pairs={{0,4},{2,6},{4,0},{6,2},{8,12},{10,14},{12,8},{14,10},{16,20},{18,... | collective-permute-start | bytes 786440 | tf_op jit(solution)/shard_map/ppermute | solution.py:315
  163.3 14.8 %collective-permute-start.37 = (bf16[2,512,256]{2,1,0:T(8,128)(2,1)S(1)}, bf16[2,512,256]{2,1,0:T(8,128)(2,1)}, u32[]{:S(2)}, u32[]{:S(2)}) collective-permute-start(bf16[2,512,256]{2,1,0:T(8,128)(2,1)S(1)} %pad_maximum_fusion.4.refs_4_), channel_id=1, source_target_pairs={{0,2},{2,0},{4,6},{6,4},{8,10},{10,8},{12,14},{14,12},{16,18},{18,... | collective-permute-start | bytes 1572872 | tf_op jit(solution)/shard_map/ppermute | solution.py:315
  174.8 42.0 %collective-permute-start.43 = (bf16[512,512]{1,0:T(8,128)(2,1)}, bf16[512,512]{1,0:T(8,128)(2,1)}, u32[]{:S(2)}, u32[]{:S(2)}) collective-permute-start(bf16[512,512]{1,0:T(8,128)(2,1)} %in0_ref.7), channel_id=1, source_target_pairs={{0,1},{1,0},{2,3},{3,2},{4,5},{5,4},{6,7},{7,6},{8,9},{9,8},{10,11... | collective-permute-start | bytes 1572872 | tf_op jit(solution)/shard_map/ppermute | solution.py:310
  176.4 9.6 %copy-start.10 = (bf16[2,512,256]{2,1,0:T(8,128)(2,1)}, bf16[2,512,256]{2,1,0:T(8,128)(2,1)S(1)}, u32[]{:S(2)}) copy-start(bf16[2,512,256]{2,1,0:T(8,128)(2,1)S(1)} %pad_maximum_fusion.3.refs_4_) | copy-start | bytes 1572868
  176.4 9.6 %collective-permute-start.29 = (bf16[2,512,256]{2,1,0:T(8,128)(2,1)S(1)}, bf16[2,512,256]{2,1,0:T(8,128)(2,1)}, u32[]{:S(2)}, u32[]{:S(2)}) collective-permute-start(bf16[2,512,256]{2,1,0:T(8,128)(2,1)S(1)} %pad_maximum_fusion.3.refs_4_), channel_id=1, source_target_pairs={{0,2},{2,0},{4,6},{6,4},{8,10},{10,8},{12,14},{14,12},{16,18},{18,... | collective-permute-start | bytes 1572872 | tf_op jit(solution)/shard_map/ppermute | solution.py:315
  176.5 9.4 %copy-start.11 = (bf16[2,512,256]{2,1,0:T(8,128)(2,1)}, bf16[2,512,256]{2,1,0:T(8,128)(2,1)S(1)}, u32[]{:S(2)}) copy-start(bf16[2,512,256]{2,1,0:T(8,128)(2,1)S(1)} %pad_maximum_fusion.2.refs_4_) | copy-start | bytes 1572868
  176.6 17.1 %collective-permute-start.21 = (bf16[2,512,256]{2,1,0:T(8,128)(2,1)S(1)}, bf16[2,512,256]{2,1,0:T(8,128)(2,1)}, u32[]{:S(2)}, u32[]{:S(2)}) collective-permute-start(bf16[2,512,256]{2,1,0:T(8,128)(2,1)S(1)} %pad_maximum_fusion.2.refs_4_), channel_id=1, source_target_pairs={{0,2},{2,0},{4,6},{6,4},{8,10},{10,8},{12,14},{14,12},{16,18},{18,... | collective-permute-start | bytes 1572872 | tf_op jit(solution)/shard_map/ppermute | solution.py:315
  178.1 7.9 %copy-start.2 = (bf16[2,512,256]{2,1,0:T(8,128)(2,1)}, bf16[2,512,256]{2,1,0:T(8,128)(2,1)S(1)}, u32[]{:S(2)}) copy-start(bf16[2,512,256]{2,1,0:T(8,128)(2,1)S(1)} %pad_maximum_fusion.1.refs_4_) | copy-start | bytes 1572868
  178.1 23.2 %collective-permute-start.13 = (bf16[2,512,256]{2,1,0:T(8,128)(2,1)S(1)}, bf16[2,512,256]{2,1,0:T(8,128)(2,1)S(1)}, u32[]{:S(2)}, u32[]{:S(2)}) collective-permute-start(bf16[2,512,256]{2,1,0:T(8,128)(2,1)S(1)} %pad_maximum_fusion.1.refs_4_), channel_id=1, source_target_pairs={{0,2},{2,0},{4,6},{6,4},{8,10},{10,8},{12,14},{14,12},{16,18},{18,... | collective-permute-start | bytes 1572872 | tf_op jit(solution)/shard_map/ppermute | solution.py:315
  202.1 6.4 %copy-start.17 = (f32[512]{0:T(512)S(1)}, f32[512]{0:T(512)}, u32[]{:S(2)}) copy-start(f32[512]{0:T(512)} %param.20) | copy-start | bytes 6148
  207.1 9.7 %collective-permute-start.42 = (bf16[512,256]{1,0:T(8,128)(2,1)}, bf16[512,256]{1,0:T(8,128)(2,1)S(1)}, u32[]{:S(2)}, u32[]{:S(2)}) collective-permute-start(bf16[512,256]{1,0:T(8,128)(2,1)} %get-tuple-element.60), channel_id=1, source_target_pairs={{0,1},{1,0},{2,3},{3,2},{4,5},{5,4},{6,7},{7,6},{8,9},{9,8},{10,11... | collective-permute-start | bytes 786440 | tf_op jit(solution)/shard_map/ppermute | solution.py:310
  209.1 13.0 %collective-permute-start.45 = (bf16[512,256]{1,0:T(8,128)(2,1)}, bf16[512,256]{1,0:T(8,128)(2,1)S(1)}, u32[]{:S(2)}, u32[]{:S(2)}) collective-permute-start(bf16[512,256]{1,0:T(8,128)(2,1)} %get-tuple-element.61), channel_id=1, source_target_pairs={{0,1},{1,0},{2,3},{3,2},{4,5},{5,4},{6,7},{7,6},{8,9},{9,8},{10,11... | collective-permute-start | bytes 786440 | tf_op jit(solution)/shard_map/ppermute | solution.py:310
  214.7 13.1 %collective-permute-start.46 = (bf16[512,256]{1,0:T(8,128)(2,1)}, bf16[512,256]{1,0:T(8,128)(2,1)S(1)}, u32[]{:S(2)}, u32[]{:S(2)}) collective-permute-start(bf16[512,256]{1,0:T(8,128)(2,1)} %get-tuple-element.63), channel_id=1, source_target_pairs={{0,1},{1,0},{2,3},{3,2},{4,5},{5,4},{6,7},{7,6},{8,9},{9,8},{10,11... | collective-permute-start | bytes 786440 | tf_op jit(solution)/shard_map/ppermute | solution.py:310
  216.1 16.7 %collective-permute-start.47 = (bf16[512,256]{1,0:T(8,128)(2,1)}, bf16[512,256]{1,0:T(8,128)(2,1)S(1)}, u32[]{:S(2)}, u32[]{:S(2)}) collective-permute-start(bf16[512,256]{1,0:T(8,128)(2,1)} %get-tuple-element.64), channel_id=1, source_target_pairs={{0,1},{1,0},{2,3},{3,2},{4,5},{5,4},{6,7},{7,6},{8,9},{9,8},{10,11... | collective-permute-start | bytes 786440 | tf_op jit(solution)/shard_map/ppermute | solution.py:310
  232.3 5.1 %copy-start.13 = (bf16[512,256]{1,0:T(8,128)(2,1)S(1)}, bf16[512,256]{1,0:T(8,128)(2,1)}, u32[]{:S(2)}) copy-start(bf16[512,256]{1,0:T(8,128)(2,1)} %mlp.5) | copy-start | bytes 786436
  232.3 5.1 %copy-start.14 = (bf16[512,256]{1,0:T(8,128)(2,1)S(1)}, bf16[512,256]{1,0:T(8,128)(2,1)}, u32[]{:S(2)}) copy-start(bf16[512,256]{1,0:T(8,128)(2,1)} %mlp.6) | copy-start | bytes 786436
  233.5 5.9 %copy-start.1 = (f32[4,512]{1,0:T(4,128)S(1)}, f32[4,512]{1,0:T(4,128)}, u32[]{:S(2)}) copy-start(f32[4,512]{1,0:T(4,128)} %param.19) | copy-start | bytes 24580
  (11 other events, 17.4 us)

commit v2 on v1

v2 whole, which is shorter than its diff:
```python
import functools
import math

import jax
import jax.numpy as jnp
from jax import lax
from jax.experimental import pallas as pl
from jax.experimental.pallas import tpu as pltpu
from jax.sharding import PartitionSpec as P

EPS = 1e-06
HW = 2
CHUNKS = 2
TILE = 256
FORWARD_ROWS = 128

SCALE = 8.0**0.25
SIN_QUARTER = [SCALE * c for c in (1.5707884677838282, -0.6457119641929367, 0.07766728844449011)]
COS_QUARTER = [
    SCALE * c for c in (0.9999999724196053, -1.2336970139164884, 0.2535986397412255, -0.02040833859268099)
]


def horner(x, coefs):
    value = jnp.float32(coefs[-1])
    for coef in coefs[-2::-1]:
        value = value * x + jnp.float32(coef)
    return value


def cos_sin_turns(turns):
    rest = turns - jnp.round(turns)
    square = rest * rest
    sin_quarter = horner(square, SIN_QUARTER) * rest
    cos_quarter = horner(square, COS_QUARTER)
    sin_half = sin_quarter * cos_quarter
    cos_half = jnp.float32(math.sqrt(2.0)) - sin_quarter * sin_quarter
    return jnp.float32(1.0) - sin_half * sin_half, sin_half * cos_half


def forward_body(
    start, first, block_rows, places, waves_ref, own_pos, other_pos, own_ref, other_ref,
    cos_ref, sin_ref, sum_ref, lhs, rhs, turns,
):
    rows = lhs.shape[0]
    step = pl.program_id(0)
    sums = [None, None]
    atom_rows = own_ref.shape[0]

    @pl.when(step == 0)
    def _():
        for number, ref in enumerate((own_pos, other_pos)):
            high, middle, low = thirds(ref[...])
            rhs[:, number * atom_rows : (number + 1) * atom_rows] = jnp.concatenate(
                [high, middle, high, low, high, middle], axis=0
            ).astype(jnp.bfloat16)

    for part in range(rows // block_rows):
        number = (first + step * (rows // block_rows) + part) ^ places[0]
        at = pl.multiple_of(places[1] + start + number * block_rows, block_rows)
        lhs[part * block_rows : (part + 1) * block_rows, :] = waves_ref[pl.ds(at, block_rows), :]

    blocks = [(ref, base) for ref in (own_ref, other_ref) for base in range(0, atom_rows, TILE)]

    def phase(block):
        turns[block % 3] = jnp.dot(
            lhs[...], rhs[:, block * TILE : (block + 1) * TILE], preferred_element_type=jnp.float32
        )

    def fill(block):
        for strip in range(rows // 16):
            at = slice(strip * 16, strip * 16 + 16)
            cos_part, sin_part = cos_sin_turns(turns[block % 3, at, :])
            cos_ref[at, block * TILE : (block + 1) * TILE] = cos_part.astype(jnp.bfloat16)
            sin_ref[at, block * TILE : (block + 1) * TILE] = sin_part.astype(jnp.bfloat16)

    def multiply(block):
        feats_ref, base = blocks[block]
        feats = feats_ref[base : base + TILE, :]
        at = slice(block * TILE, (block + 1) * TILE)
        for which, ref in enumerate((cos_ref, sin_ref)):
            term = jnp.dot(ref[:, at], feats, preferred_element_type=jnp.float32)
            sums[which] = term if sums[which] is None else sums[which] + term

    phase(0)
    for block in range(len(blocks)):
        if block + 1 < len(blocks):
            phase(block + 1)
        fill(block)
        if block > 0:
            multiply(block - 1)
    multiply(len(blocks) - 1)
    for which in range(2):
        sum_ref[which] = sums[which].astype(sum_ref.dtype)


def forward(places, waves, positions, feats, start, position, count, block_rows, dtype):
    depth = waves.shape[1]
    atom_rows, width = feats[0].shape
    tile = min(FORWARD_ROWS, count)
    trig = jax.ShapeDtypeStruct((count, 2 * atom_rows), jnp.bfloat16)
    return pl.pallas_call(
        functools.partial(forward_body, start, position // block_rows, block_rows),
        grid_spec=pltpu.PrefetchScalarGridSpec(
            num_scalar_prefetch=1,
            grid=(count // tile,),
            in_specs=[
                pl.BlockSpec(array.shape, lambda k, *_: (0, 0))
                for array in (waves, *positions, *feats)
            ],
            out_specs=[
                pl.BlockSpec((tile, 2 * atom_rows), lambda k, *_: (k, 0)),
                pl.BlockSpec((tile, 2 * atom_rows), lambda k, *_: (k, 0)),
                pl.BlockSpec((2, tile, width), lambda k, *_: (0, k, 0)),
            ],
            scratch_shapes=[
                pltpu.VMEM((tile, depth), jnp.bfloat16),
                pltpu.VMEM((depth, 2 * atom_rows), jnp.bfloat16),
                pltpu.VMEM((3, tile, TILE), jnp.float32),
            ],
        ),
        out_shape=[trig, trig, jax.ShapeDtypeStruct((2, count, width), dtype)],
        cost_estimate=pl.CostEstimate(
            flops=18 * count * atom_rows * width,
            transcendentals=0,
            bytes_accessed=8 * count * atom_rows,
        ),
        name="structure",
    )(places, waves, *positions, *feats)


def near_body(base, places, scales, row_ref, left_ref, masked_ref, right_ref, feats_ref, mix_ref, out_ref, wide, kernels, partners):
    cells_per_step = kernels.shape[0]
    cap = wide.shape[1]
    step = pl.program_id(0)
    kinds = mix_ref.shape[0]
    count = places.shape[1]
    halo = left_ref.shape[0]
    inner = masked_ref.shape[0]

    @pl.when(step == 0)
    def _():
        wide[0:halo] = left_ref[...]
        wide[halo : halo + inner] = masked_ref[...]
        wide[halo + inner :] = right_ref[...]

    for part in range(cells_per_step):
        cell = base + step * cells_per_step + part
        col = jnp.transpose(row_ref[cell + halo])
        for which in range(count):
            place = places[cell, which]
            row = row_ref[place]
            squared = None
            for axis in range(3):
                gap = col[:, axis : axis + 1] - row[axis : axis + 1, :]
                squared = gap * gap if squared is None else squared + gap * gap
            for kind in range(kinds):
                kernels[part, kind * cap : (kind + 1) * cap, which * cap : (which + 1) * cap] = (
                    jnp.exp2(scales[kind] * squared).astype(jnp.bfloat16)
                )
            partners[part, which * cap : (which + 1) * cap, :] = wide[place]
        total = jnp.dot(kernels[part], partners[part], preferred_element_type=jnp.float32)
        at = slice(part * cap, (part + 1) * cap)
        near = feats_ref[at, :].astype(jnp.float32)
        for kind in range(kinds):
            near = near + total[kind * cap : (kind + 1) * cap, :] * mix_ref[kind : kind + 1, :]
        out_ref[at, :] = near


def near_part(base, cells, places, scales, rows, left, masked, right, feats, mix):
    count = places.shape[1]
    cap, width = masked.shape[1:]
    kinds = mix.shape[0]
    per = min(8, cells)
    offset = base // per
    whole3 = lambda a: pl.BlockSpec(a.shape, lambda c, *_: (0, 0, 0))
    return pl.pallas_call(
        functools.partial(near_body, base),
        grid_spec=pltpu.PrefetchScalarGridSpec(
            num_scalar_prefetch=2,
            grid=(cells // per,),
            in_specs=[
                whole3(rows),
                whole3(left),
                whole3(masked),
                whole3(right),
                pl.BlockSpec((per * cap, width), lambda c, *_: (c + offset, 0)),
                pl.BlockSpec(mix.shape, lambda c, *_: (0, 0)),
            ],
            out_specs=pl.BlockSpec((per * cap, width), lambda c, *_: (c, 0)),
            scratch_shapes=[
                pltpu.VMEM((rows.shape[0], cap, width), jnp.bfloat16),
                pltpu.VMEM((per, kinds * cap, count * cap), jnp.bfloat16),
                pltpu.VMEM((per, count * cap, width), jnp.bfloat16),
            ],
        ),
        out_shape=jax.ShapeDtypeStruct((cells * cap, width), jnp.float32),
        cost_estimate=pl.CostEstimate(
            flops=8 * cells * cap * cap * count * width * kinds,
            transcendentals=0,
            bytes_accessed=8 * cells * cap * width,
        ),
        name="near",
    )(places, scales, rows, left, masked, right, feats, mix)


def backward_body(has_acc, has_came, *refs):
    trig, filts, rest = refs[:4], refs[4:6], list(refs[6:])
    contract = (((0,), (0,)), ((), ()))
    total = rest.pop(0)[...] if has_acc else None
    if has_came:
        total = total + rest.pop(0)[...].astype(jnp.float32)
    for half in range(2):
        for which in range(2):
            term = lax.dot_general(
                trig[2 * half + which][...],
                filts[half][which],
                contract,
                preferred_element_type=jnp.float32,
            )
            total = term if total is None else total + term
    for ref in rest:
        ref[...] = total.astype(ref.dtype)


def backward(trig, filts, first, count, tile, acc, came, dtypes):
    rows = trig[0].shape[0]
    width = filts[0].shape[2]
    at = first // tile
    args, specs = [], []
    for array in (acc, came):
        if array is not None:
            array, offset = array
            args.append(array)
            specs.append(pl.BlockSpec((tile, width), lambda i, offset=offset: (i + offset, 0)))
    return pl.pallas_call(
        functools.partial(backward_body, acc is not None, came is not None),
        grid=(count // tile,),
        in_specs=[pl.BlockSpec((rows, tile), lambda i: (0, i + at))] * 4
        + [pl.BlockSpec(filts[0].shape, lambda i: (0, 0, 0))] * 2
        + specs,
        out_specs=[pl.BlockSpec((tile, width), lambda i: (i, 0))] * len(dtypes),
        out_shape=[jax.ShapeDtypeStruct((count, width), dtype) for dtype in dtypes],
        cost_estimate=pl.CostEstimate(
            flops=16 * rows * count * width,
            transcendentals=0,
            bytes_accessed=8 * rows * count + 8 * count * width,
        ),
        name="messages",
    )(*trig, *filts, *args)


def mlp_body(side, own_ref, other_ref, gain_ref, in0_ref, in1_ref, out0_ref, out1_ref, *refs):
    result_ref = refs[-1]
    width = own_ref.shape[1]
    mine = side[0]
    own = own_ref[...]
    own_wide = own.astype(jnp.bfloat16).astype(jnp.float32)
    other = other_ref[...].astype(jnp.float32)
    mean = (
        jnp.sum(own_wide * own_wide, axis=1, keepdims=True)
        + jnp.sum(other * other, axis=1, keepdims=True)
    ) / (2 * width)
    scale = lax.rsqrt(mean + EPS)
    normed_own = (own_wide * scale * gain_ref[pl.ds(mine, 1), :]).astype(jnp.bfloat16)
    normed_other = (other * scale * gain_ref[pl.ds(1 - mine, 1), :]).astype(jnp.bfloat16)
    at_own = pl.ds(pl.multiple_of(mine * width, width), width)
    at_other = pl.ds(pl.multiple_of((1 - mine) * width, width), width)
    total = own
    for in_ref, out_ref in ((in0_ref, out0_ref), (in1_ref, out1_ref)):
        value = jnp.dot(normed_own, in_ref[at_own, :], preferred_element_type=jnp.float32)
        value = value + jnp.dot(
            normed_other, in_ref[at_other, :], preferred_element_type=jnp.float32
        )
        half = jnp.float32(0.5) * value
        hidden = (half * jnp.tanh(half) + half).astype(jnp.bfloat16)
        total = total + jnp.dot(hidden, out_ref[...], preferred_element_type=jnp.float32)
    result_ref[...] = total.astype(jnp.bfloat16)


def mlp(side, own, own_at, other, gains, weights, result, first, total_rows):
    rows, width = other.shape
    offset, own_offset = first // rows, own_at // rows
    args = [] if result is None else [result]
    return pl.pallas_call(
        mlp_body,
        grid_spec=pltpu.PrefetchScalarGridSpec(
            num_scalar_prefetch=1,
            grid=(1,),
            in_specs=[
                pl.BlockSpec((rows, width), lambda i, *_: (own_offset, 0)),
                pl.BlockSpec((rows, width), lambda i, *_: (0, 0)),
                pl.BlockSpec(gains.shape, lambda i, *_: (0, 0)),
            ]
            + [pl.BlockSpec(weight.shape, lambda i, *_: (0, 0)) for weight in weights]
            + [pl.BlockSpec(memory_space=pl.ANY)] * len(args),
            out_specs=pl.BlockSpec((rows, width), lambda i, *_: (offset, 0)),
        ),
        out_shape=jax.ShapeDtypeStruct((total_rows, width), jnp.bfloat16),
        input_output_aliases={8: 0} if args else {},
        cost_estimate=pl.CostEstimate(
            flops=2 * rows * width * weights[0].shape[1] * 12,
            transcendentals=0,
            bytes_accessed=8 * rows * width,
        ),
        name="mlp",
    )(side, own, other, gains, *weights, *args)


def thirds(values):
    def rounded(v):
        return v.astype(jnp.bfloat16).astype(jnp.float32)

    high = rounded(values)
    middle = rounded(values - high)
    return high, middle, values - high - middle


def swap(value):
    return lax.ppermute(value, "waves", [(0, 1), (1, 0)])


def across(value, bit):
    count = lax.axis_size("cells")
    return lax.ppermute(value, "cells", [(i, i ^ bit) for i in range(count)])


def shards(
    features,
    positions,
    occupancy,
    neighbours,
    wavevectors,
    filters,
    falloffs,
    mixing,
    norm_gain,
    in_weight,
    out_weight,
):
    devices = lax.axis_size("cells")
    bits = [1 << b for b in range(devices.bit_length() - 1)]
    core_bit, ring_bits = bits[0], bits[1:]
    group = devices // 2
    cell_count = occupancy.shape[0]
    atom_rows, width = features.shape
    capacity = atom_rows // cell_count
    wave_rows = wavevectors.shape[1]
    all_waves = 2 * wave_rows
    own_waves = wave_rows // 2
    chunk_rows = own_waves // CHUNKS
    block_rows = chunk_rows // group
    length = jnp.float32(devices * cell_count)
    place = lax.axis_index("cells").astype(jnp.int32)
    side = lax.axis_index("waves").astype(jnp.int32)
    core = place & core_bit

    live = (jnp.arange(capacity, dtype=jnp.int32)[None, :] < occupancy[:, None]).reshape(atom_rows, 1)
    masked = jnp.where(live, features, jnp.zeros_like(features))
    atoms = jnp.pad(positions, ((0, 5), (0, 0)))

    pair_feats = (masked, across(masked, core_bit))
    pair_atoms = (atoms, across(atoms, core_bit))

    reverse = jnp.int32(0)
    for index, bit in enumerate(reversed(ring_bits)):
        reverse = reverse | jnp.where((place & bit) != 0, 1 << index, 0).astype(jnp.int32)
    places_of_waves = jnp.stack([reverse, core * own_waves])

    def wave_operand(waves):
        padded = jnp.pad(waves * jnp.float32(1.0 / (2.0 * math.pi)), ((0, 5), (0, 0)))
        high = lax.reduce_precision(padded, 8, 7)
        middle = lax.reduce_precision(padded - high, 8, 7)
        low = padded - high - middle
        return jnp.concatenate([high, high, middle, high, low, middle], axis=0).T.astype(jnp.bfloat16)

    other_waves = swap(wavevectors)

    to_right = [(i, (i + 1) % devices) for i in range(devices)]
    to_left = [((i + 1) % devices, i) for i in range(devices)]
    edge = HW * capacity
    left_feats = lax.ppermute(masked[atom_rows - edge :], "cells", to_right)
    right_feats = lax.ppermute(masked[:edge], "cells", to_left)
    left_pos = lax.ppermute(positions[:, atom_rows - edge :], "cells", to_right)
    right_pos = lax.ppermute(positions[:, :edge], "cells", to_left)
    count = jnp.full((8, 128), jnp.sum(occupancy).astype(jnp.float32))
    for bit in bits:
        count = count + across(count, bit)
    count = count[0:1, 0:1]

    def filter_part(chunk, whose):
        row = core * own_waves + chunk * chunk_rows + reverse * block_rows
        return lax.dynamic_slice(filters, (row, whose * width), (block_rows, width))

    own_filters = [filter_part(chunk, side) for chunk in range(CHUNKS)]
    sent_filters = jnp.stack([filter_part(chunk, 1 - side) for chunk in range(CHUNKS)])
    other_filters = swap(sent_filters)

    in_other = swap(in_weight)
    hidden_rows = out_weight.shape[0]
    out_own = lax.dynamic_slice(out_weight, (0, side * width), (hidden_rows, width))
    out_other = swap(lax.dynamic_slice(out_weight, (0, (1 - side) * width), (hidden_rows, width)))

    factor = lax.rsqrt(count) * jnp.float32(1.0 / math.sqrt(all_waves))

    trig, totals = [], []
    number = 0
    for waves, rows_of_filter in ((wavevectors, own_filters), (other_waves, other_filters)):
        operand = wave_operand(waves)
        for chunk in range(CHUNKS):
            half = chunk_rows // 2
            cos_far, sin_far, send = forward(
                places_of_waves, operand, pair_atoms, pair_feats, chunk * chunk_rows, half, half, block_rows, jnp.bfloat16
            )
            cos_near, sin_near, keep = forward(
                places_of_waves, operand, pair_atoms, pair_feats, chunk * chunk_rows, 0, half, block_rows, jnp.float32
            )
            trig.append((cos_near, sin_near, cos_far, sin_far))
            for index, bit in enumerate(ring_bits):
                summed = keep + across(send, bit).astype(jnp.float32)
                if index + 1 < len(ring_bits):
                    half = summed.shape[1] // 2
                    keep, send = summed[:, :half], summed[:, half:].astype(jnp.bfloat16)
            filt = (summed * rows_of_filter[chunk][None] * factor[None]).astype(jnp.bfloat16)
            for index, bit in enumerate(reversed(ring_bits)):
                came = across(filt, bit)
                if index + 1 < len(ring_bits):
                    filt = jnp.concatenate([filt, came], axis=1)
            totals.append((filt, came))
            number += 1

    shift_left = jnp.where(place == 0, length, 0.0).astype(jnp.float32)
    shift_right = jnp.where(place == devices - 1, length, 0.0).astype(jnp.float32)
    first = jnp.array([[1.0], [0.0], [0.0]], jnp.float32)
    wide_pos = jnp.concatenate(
        [left_pos - first * shift_left, positions, right_pos + first * shift_right], axis=1
    )
    rows = jnp.pad(wide_pos, ((0, 5), (0, 0))).reshape(8, cell_count + 2 * HW, capacity).transpose(1, 0, 2)
    places = jnp.arange(cell_count, dtype=jnp.int32)[:, None] + HW + neighbours
    mix = lax.dynamic_slice(mixing, (0, side * width), (mixing.shape[0], width))
    half_cells = cell_count // 2
    half_rows = atom_rows // 2
    own = []
    for half in range(2):
        own.append(
            near_part(
                half * half_cells,
                half_cells,
                places,
                falloffs * jnp.float32(-1.0 / math.log(2.0)),
                rows,
                left_feats.reshape(HW, capacity, width),
                masked.reshape(cell_count, capacity, width),
                right_feats.reshape(HW, capacity, width),
                features,
                mix,
            )
        )

    f32, bf16 = jnp.float32, jnp.bfloat16
    other = None
    tile = half_rows
    mine = None
    for number in range(len(trig) - 1):
        (other,) = backward(
            trig[number], totals[number], atom_rows, atom_rows, tile,
            None if other is None else (other, 0), None, (f32,),
        )
        if mine is None:
            mine = [
                backward(
                    trig[number], totals[number], half * half_rows, half_rows, half_rows,
                    (own[half], 0), None, (f32,),
                )[0]
                for half in range(2)
            ]
            mine = [(mine[0], 0), (mine[1], 0)]
        else:
            mine = [
                (
                    backward(
                        trig[number], totals[number], half * half_rows, half_rows, half_rows,
                        mine[half], None, (f32,),
                    )[0],
                    0,
                )
                for half in range(2)
            ]
    came = []
    for half in range(2):
        (send,) = backward(
            trig[-1], totals[-1], atom_rows + half * half_rows, half_rows, half_rows,
            (other, half), None, (bf16,),
        )
        came.append(across(send, core_bit))
    gains = norm_gain.reshape(2, width)
    weights = (in_weight, in_other, out_own, out_other)
    result = None
    for half in range(2):
        part, send = backward(
            trig[-1], totals[-1], half * half_rows, half_rows, half_rows,
            mine[half], (came[half], 0), (f32, bf16),
        )
        pieces = 1 if half == 0 else 2
        piece_rows = half_rows // pieces
        for piece in range(pieces):
            arrived = swap(send[piece * piece_rows : (piece + 1) * piece_rows])
            result = mlp(
                side.reshape(1), part, piece * piece_rows, arrived, gains, weights, result,
                half * half_rows + piece * piece_rows, atom_rows,
            )
    return result


def solution(mesh):
    placed = (
        P("cells", "waves"),
        P(None, "cells"),
        P("cells"),
        P("cells", None),
        P(None, "waves"),
        P("waves", None),
        P(),
        P(),
        P(),
        P(None, "waves"),
        P("waves", None),
    )

    return jax.shard_map(
        shards, mesh=mesh, in_specs=placed, out_specs=P("cells", "waves"), check_vma=False
    )
```

time: 240 us -> 248 us (1.033); the launches traced: 239 us -> 244 us
  Pallas kernels: 113 us -> 137 us
  waiting for transfers between devices: 62.1 us -> 48.1 us
  starting transfers between devices: 39.2 us -> 34.8 us
  other arithmetic: 10.7 us -> 6.98 us
    pallas_call x14 -> x23, Pallas kernels: 98 us -> 125 us  [the longest x8 61.5 us: forward(): pl.pallas_call(functools.partial(forward_body, start, position // block_r...]
    ppermute x36 -> x32, waiting for transfers between devices: 59.7 us -> 43.1 us  [across(): return lax.ppermute(value, 'cells', [(i, i ^ bit) for i in range(count)])]
    ppermute x1, waiting for transfers between devices: 0.01 us -> 3.54 us  [shards(): left_feats = lax.ppermute(masked[atom_rows - edge:], 'cells', to_right)]
    ppermute x1, starting transfers between devices: 3.29 us -> 0.01 us  [shards(): right_feats = lax.ppermute(masked[:edge], 'cells', to_left)]
    pallas_call x4 -> x3, Pallas kernels: 15.4 us -> 12.2 us  [mlp(): pl.pallas_call(mlp_body, grid_spec=pltpu.PrefetchScalarGridSpec(num_scala...]
    unnamed x55 -> x65, local copies, waits for them, and re-layouts: 4.76 us -> 6.69 us
    ppermute x8 -> x7, starting transfers between devices: 10.8 us -> 8.91 us  [swap(): return lax.ppermute(value, 'waves', [(0, 1), (1, 0)])]
    ppermute x36 -> x32, starting transfers between devices: 20.8 us -> 19.9 us  [across(): return lax.ppermute(value, 'cells', [(i, i ^ bit) for i in range(count)])]
  transfers between devices with their start and end apart: 48 -> 43, of which waited for: 25 -> 23; matrix products, arithmetic and copies ran while one was open for 7% -> 6% of each run, Pallas kernels for 46% -> 55%
where the time goes in v2:
time: 248 us; the launch traced here: 244 us
  Pallas kernels  137 us (55%)
  waiting for transfers between devices  48.1 us (19%)
  starting transfers between devices  34.8 us (14%)
  local copies, waits for them, and re-layouts  14.2 us (6%)
  other arithmetic  6.98 us (3%)
    pallas_call x8, Pallas kernels, forward(): pl.pallas_call(functools.partial(forward_body, start, position // block_r...  61.5 us
    pallas_call x13, Pallas kernels, backward(): pl.pallas_call(functools.partial(backward_body, acc is not None, came is...  52.5 us
    ppermute x32, waiting for transfers between devices, across(): return lax.ppermute(value, 'cells', [(i, i ^ bit) for i in range(count)])  43.1 us
    ppermute x32, starting transfers between devices, across(): return lax.ppermute(value, 'cells', [(i, i ^ bit) for i in range(count)])  19.9 us
    pallas_call x3, Pallas kernels, mlp(): pl.pallas_call(mlp_body, grid_spec=pltpu.PrefetchScalarGridSpec(num_scala...  12.2 us
    pallas_call x2, Pallas kernels, near_part(): pl.pallas_call(functools.partial(near_body, base), grid_spec=pltpu.Prefet...  11.1 us
    ppermute x7, starting transfers between devices, swap(): return lax.ppermute(value, 'waves', [(0, 1), (1, 0)])  8.91 us
    unnamed x65, local copies, waits for them, and re-layouts  6.69 us
  transfers between devices with their start and end apart: 43, of which 23 were waited for; matrix products, arithmetic and copies ran while one was open for 6% of the time, Pallas kernels for 55%

profile of v2, /device:TPU:0, one launch (start us, length us, event | category | flops | bytes accessed | tf_op | source)
XLA Modules:
  0.0 243.5 jit_solution(5212408760177096676)
XLA Ops:
  1.3 5.0 %collective-permute-start.33 = (f32[3,256]{1,0:T(4,128)S(1)}, f32[3,256]{1,0:T(4,128)S(1)}, u32[]{:S(2)}, u32[]{:S(2)}) collective-permute-start(f32[3,256]{1,0:T(4,128)S(1)} %get-tuple-element.74), channel_id=1, source_target_pairs={{2,0},{4,2},{6,4},{8,6},{10,8},{12,10},{14,12},{16,14},{18,16},{20... | collective-permute-start | bytes 9224 | tf_op jit(solution)/shard_map/ppermute | solution.py:385
  6.3 1.3 reduce_sum.9
  8.3 2.0 collective-permute-start
  11.1 1.5 broadcast_select_fusion.own_ref
  18.0 1.0 copy.19
  19.5 3.5 %collective-permute-done.8 = f32[8,128]{1,0:T(8,128)S(1)} collective-permute-done((f32[8,128]{1,0:T(8,128)S(1)}, f32[8,128]{1,0:T(8,128)S(1)}, u32[]{:S(2)}, u32[]{:S(2)}) %collective-permute-start.8) | collective-permute-done | bytes 4128 | tf_op jit(solution)/shard_map/ppermute | solution.py:325
  23.4 3.3 %collective-permute-done.9 = f32[8,128]{1,0:T(8,128)S(1)} collective-permute-done((f32[8,128]{1,0:T(8,128)S(1)}, f32[8,128]{1,0:T(8,128)S(1)}, u32[]{:S(2)}, u32[]{:S(2)}) %collective-permute-start.9) | collective-permute-done | bytes 4128 | tf_op jit(solution)/shard_map/ppermute | solution.py:325
  26.7 1.2 collective-permute-start.10
  28.6 2.6 %collective-permute-done.10 = f32[8,128]{1,0:T(8,128)S(1)} collective-permute-done((f32[8,128]{1,0:T(8,128)S(1)}, f32[8,128]{1,0:T(8,128)S(1)}, u32[]{:S(2)}, u32[]{:S(2)}) %collective-permute-start.10) | collective-permute-done | bytes 4128 | tf_op jit(solution)/shard_map/ppermute | solution.py:325
  33.2 1.0 copy.18
  34.2 1.9 collective-permute-start.39
  36.1 3.5 %collective-permute-done.34 = bf16[256,256]{1,0:T(8,128)(2,1)S(1)} collective-permute-done((bf16[256,256]{1,0:T(8,128)(2,1)S(1)}, bf16[256,256]{1,0:T(8,128)(2,1)S(1)}, u32[]{:S(2)}, u32[]{:S(2)}) %collective-permute-start.34) | collective-permute-done | bytes 131104 | tf_op jit(solution)/shard_map/ppermute | solution.py:382
  39.7 1.9 collective-permute-start.38
  41.6 5.5 %near.3.refs_6_ = f32[1024,256]{1,0:T(8,128)} custom-call(s32[16,3]{1,0:T(8,128)} %broadcast_add_fusion.places, f32[4]{0:T(128)} %broadcast_multiply_fusion.2.scales, f32[20,8,128]{2,1,0:T(8,128)} %fusion.12.row_ref, bf16[2,128,256]{2,1,0:T(8,128)(2,1)} %bitcast.39, bf16[16,128,256]{2,1,0:T(8,128)(2,1)} %bitcast.27, bf16[2,128,256]{2,1,0:T(8,128)(2,1)} %bitcast.37, ...), custom_call_target="tpu_custom_call" | custom-call | flops 3221225472 | bytes 2097152 | tf_op jit(solution)/shard_map/near/pallas_call | solution.py:177
  47.7 8.1 %structure.15 = (bf16[256,4096]{1,0:T(8,128)(2,1)}, bf16[256,4096]{1,0:T(8,128)(2,1)}, bf16[2,256,256]{2,1,0:T(8,128)(2,1)}) custom-call(s32[2]{0:T(128)} %pad_add_fusion.places, bf16[2048,48]{1,0:T(8,128)(2,1)} %bitcast.29, f32[8,2048]{1,0:T(8,128)} %copy-done.19, f32[8,2048]{1,0:T(8,128)} %copy-done.30, bf16[2048,256]{1,0:T(8,128)(2,1)} %copy-done.10, ...), custom_call_target="tpu_custom_call" | custom-call | flops 2415919104 | bytes 4194304 | tf_op jit(solution)/shard_map/structure/pallas_call | solution.py:102
  55.8 7.5 %structure.13 = (bf16[256,4096]{1,0:T(8,128)(2,1)}, bf16[256,4096]{1,0:T(8,128)(2,1)}, bf16[2,256,256]{2,1,0:T(8,128)(2,1)}) custom-call(s32[2]{0:T(128)} %pad_add_fusion.places, bf16[2048,48]{1,0:T(8,128)(2,1)} %bitcast.30, f32[8,2048]{1,0:T(8,128)} %copy-done.19, f32[8,2048]{1,0:T(8,128)} %copy-done.30, bf16[2048,256]{1,0:T(8,128)(2,1)} %copy-done.10, ...), custom_call_target="tpu_custom_call" | custom-call | flops 2415919104 | bytes 4194304 | tf_op jit(solution)/shard_map/structure/pallas_call | solution.py:102
  63.3 2.0 collective-permute-start.20
  65.4 7.6 %structure.11 = (bf16[256,4096]{1,0:T(8,128)(2,1)}, bf16[256,4096]{1,0:T(8,128)(2,1)}, bf16[2,256,256]{2,1,0:T(8,128)(2,1)}) custom-call(s32[2]{0:T(128)} %pad_add_fusion.places, bf16[2048,48]{1,0:T(8,128)(2,1)} %bitcast.33, f32[8,2048]{1,0:T(8,128)} %copy-done.19, f32[8,2048]{1,0:T(8,128)} %copy-done.30, bf16[2048,256]{1,0:T(8,128)(2,1)} %copy-done.10, ...), custom_call_target="tpu_custom_call" | custom-call | flops 2415919104 | bytes 4194304 | tf_op jit(solution)/shard_map/structure/pallas_call | solution.py:102
  73.0 7.5 %structure.9 = (bf16[256,4096]{1,0:T(8,128)(2,1)}, bf16[256,4096]{1,0:T(8,128)(2,1)}, bf16[2,256,256]{2,1,0:T(8,128)(2,1)}) custom-call(s32[2]{0:T(128)} %pad_add_fusion.places, bf16[2048,48]{1,0:T(8,128)(2,1)} %bitcast.34, f32[8,2048]{1,0:T(8,128)} %copy-done.19, f32[8,2048]{1,0:T(8,128)} %copy-done.30, bf16[2048,256]{1,0:T(8,128)(2,1)} %copy-done.10, ...), custom_call_target="tpu_custom_call" | custom-call | flops 2415919104 | bytes 4194304 | tf_op jit(solution)/shard_map/structure/pallas_call | solution.py:102
  80.5 7.6 %structure.14 = (bf16[256,4096]{1,0:T(8,128)(2,1)}, bf16[256,4096]{1,0:T(8,128)(2,1)}, f32[2,256,256]{2,1,0:T(8,128)}) custom-call(s32[2]{0:T(128)} %pad_add_fusion.places, bf16[2048,48]{1,0:T(8,128)(2,1)} %bitcast.31, f32[8,2048]{1,0:T(8,128)} %copy-done.19, f32[8,2048]{1,0:T(8,128)} %copy-done.30, bf16[2048,256]{1,0:T(8,128)(2,1)} %copy-done.10, ...), custom_call_target="tpu_custom_call" | custom-call | flops 2415919104 | bytes 4194304 | tf_op jit(solution)/shard_map/structure/pallas_call | solution.py:102
  88.1 7.7 %structure.12 = (bf16[256,4096]{1,0:T(8,128)(2,1)}, bf16[256,4096]{1,0:T(8,128)(2,1)}, f32[2,256,256]{2,1,0:T(8,128)}) custom-call(s32[2]{0:T(128)} %pad_add_fusion.places, bf16[2048,48]{1,0:T(8,128)(2,1)} %bitcast.32, f32[8,2048]{1,0:T(8,128)} %copy-done.19, f32[8,2048]{1,0:T(8,128)} %copy-done.30, bf16[2048,256]{1,0:T(8,128)(2,1)} %copy-done.10, ...), custom_call_target="tpu_custom_call" | custom-call | flops 2415919104 | bytes 4194304 | tf_op jit(solution)/shard_map/structure/pallas_call | solution.py:102
  95.8 7.8 %structure.10 = (bf16[256,4096]{1,0:T(8,128)(2,1)}, bf16[256,4096]{1,0:T(8,128)(2,1)}, f32[2,256,256]{2,1,0:T(8,128)}) custom-call(s32[2]{0:T(128)} %pad_add_fusion.places, bf16[2048,48]{1,0:T(8,128)(2,1)} %bitcast.35, f32[8,2048]{1,0:T(8,128)} %copy-done.19, f32[8,2048]{1,0:T(8,128)} %copy-done.30, bf16[2048,256]{1,0:T(8,128)(2,1)} %copy-done.10, ...), custom_call_target="tpu_custom_call" | custom-call | flops 2415919104 | bytes 4194304 | tf_op jit(solution)/shard_map/structure/pallas_call | solution.py:102
  103.6 7.7 %structure.8 = (bf16[256,4096]{1,0:T(8,128)(2,1)}, bf16[256,4096]{1,0:T(8,128)(2,1)}, f32[2,256,256]{2,1,0:T(8,128)}) custom-call(s32[2]{0:T(128)} %pad_add_fusion.places, bf16[2048,48]{1,0:T(8,128)(2,1)} %bitcast.36, f32[8,2048]{1,0:T(8,128)} %copy-done.19, f32[8,2048]{1,0:T(8,128)} %copy-done.30, bf16[2048,256]{1,0:T(8,128)(2,1)} %copy-done.10, ...), custom_call_target="tpu_custom_call" | custom-call | flops 2415919104 | bytes 4194304 | tf_op jit(solution)/shard_map/structure/pallas_call | solution.py:102
  111.3 2.1 collective-permute-start.3
  113.7 2.1 collective-permute-start.21
  115.8 2.1 collective-permute-done.3
  118.0 1.6 collective-permute-done.27
  120.2 1.6 collective-permute-done.21
  121.8 1.4 collective-permute-done.15
  123.1 1.6 collective-permute-start.22
  126.2 4.2 %collective-permute-done.28 = bf16[2,64,256]{2,1,0:T(8,128)(2,1)S(1)} collective-permute-done((bf16[2,64,256]{2,1,0:T(8,128)(2,1)S(1)}, bf16[2,64,256]{2,1,0:T(8,128)(2,1)S(1)}, u32[]{:S(2)}, u32[]{:S(2)}) %collective-permute-start.28) | collective-permute-done | bytes 65568 | tf_op jit(solution)/shard_map/ppermute | solution.py:325
  130.4 2.8 %collective-permute-done.22 = bf16[2,64,256]{2,1,0:T(8,128)(2,1)S(1)} collective-permute-done((bf16[2,64,256]{2,1,0:T(8,128)(2,1)S(1)}, bf16[2,64,256]{2,1,0:T(8,128)(2,1)S(1)}, u32[]{:S(2)}, u32[]{:S(2)}) %collective-permute-start.22) | collective-permute-done | bytes 65568 | tf_op jit(solution)/shard_map/ppermute | solution.py:325
  133.5 1.9 collective-permute-done.16
  136.3 1.9 collective-permute-done.5
  138.4 2.5 %collective-permute-done.29 = bf16[2,64,256]{2,1,0:T(8,128)(2,1)S(1)} collective-permute-done((bf16[2,64,256]{2,1,0:T(8,128)(2,1)S(1)}, bf16[2,64,256]{2,1,0:T(8,128)(2,1)S(1)}, u32[]{:S(2)}, u32[]{:S(2)}) %collective-permute-start.29) | collective-permute-done | bytes 65568 | tf_op jit(solution)/shard_map/ppermute | solution.py:325
  141.9 1.7 collective-permute-done.17
  143.7 2.6 %collective-permute-done.11 = bf16[2,64,256]{2,1,0:T(8,128)(2,1)S(1)} collective-permute-done((bf16[2,64,256]{2,1,0:T(8,128)(2,1)S(1)}, bf16[2,64,256]{2,1,0:T(8,128)(2,1)S(1)}, u32[]{:S(2)}, u32[]{:S(2)}) %collective-permute-start.11) | collective-permute-done | bytes 65568 | tf_op jit(solution)/shard_map/ppermute | solution.py:325
  146.4 2.3 collective-permute-done.30
  149.0 1.2 collective-permute-done.24
  150.2 1.7 collective-permute-start.31
  151.9 1.4 collective-permute-start.25
  153.6 1.1 collective-permute-start.19
  154.7 4.7 %collective-permute-done.31.refs_5_ = bf16[2,256,256]{2,1,0:T(8,128)(2,1)S(1)} collective-permute-done((bf16[2,256,256]{2,1,0:T(8,128)(2,1)S(1)}, bf16[2,256,256]{2,1,0:T(8,128)(2,1)S(1)}, u32[]{:S(2)}, u32[]{:S(2)}) %collective-permute-start.31) | collective-permute-done | bytes 262176 | tf_op jit(solution)/shard_map/ppermute | solution.py:325
  159.4 1.7 collective-permute-start.13
  161.1 4.5 %messages.16.refs_6_ = f32[2048,256]{1,0:T(8,128)} custom-call(bf16[256,4096]{1,0:T(8,128)(2,1)} %get-tuple-element.51.refs_0_, bf16[256,4096]{1,0:T(8,128)(2,1)} %get-tuple-element.52.refs_1_, bf16[256,4096]{1,0:T(8,128)(2,1)} %get-tuple-element.53.refs_2_, bf16[256,4096]{1,0:T(8,128)(2,1)} %get-tuple-element.54.refs_3_, bf16[2,256,256]{2,1,0:T(8,128)(2,1)} %copy-done.6, ...), custom_call_target="tpu_custom_call" | custom-call | flops 2147483648 | bytes 8388608 | tf_op jit(solution)/shard_map/messages/pallas_call | solution.py:236
  166.3 4.9 %messages.17.refs_6_ = f32[2048,256]{1,0:T(8,128)} custom-call(bf16[256,4096]{1,0:T(8,128)(2,1)} %get-tuple-element.45.refs_0_, bf16[256,4096]{1,0:T(8,128)(2,1)} %get-tuple-element.46.refs_1_, bf16[256,4096]{1,0:T(8,128)(2,1)} %get-tuple-element.47.refs_2_, bf16[256,4096]{1,0:T(8,128)(2,1)} %get-tuple-element.48.refs_3_, bf16[2,256,256]{2,1,0:T(8,128)(2,1)} %copy-done.4, ...), custom_call_target="tpu_custom_call" | custom-call | flops 2147483648 | bytes 8388608 | tf_op jit(solution)/shard_map/messages/pallas_call | solution.py:236
  171.9 5.1 %messages.18.refs_6_ = f32[2048,256]{1,0:T(8,128)} custom-call(bf16[256,4096]{1,0:T(8,128)(2,1)} %get-tuple-element.39.refs_0_, bf16[256,4096]{1,0:T(8,128)(2,1)} %get-tuple-element.40.refs_1_, bf16[256,4096]{1,0:T(8,128)(2,1)} %get-tuple-element.41.refs_2_, bf16[256,4096]{1,0:T(8,128)(2,1)} %get-tuple-element.42.refs_3_, bf16[2,256,256]{2,1,0:T(8,128)(2,1)} %copy-done.5, ...), custom_call_target="tpu_custom_call" | custom-call | flops 2147483648 | bytes 8388608 | tf_op jit(solution)/shard_map/messages/pallas_call | solution.py:236
  177.7 3.6 %messages.24 = bf16[1024,256]{1,0:T(8,128)(2,1)} custom-call(bf16[256,4096]{1,0:T(8,128)(2,1)} %get-tuple-element.33.refs_0_, bf16[256,4096]{1,0:T(8,128)(2,1)} %get-tuple-element.34.refs_1_, bf16[256,4096]{1,0:T(8,128)(2,1)} %get-tuple-element.35.refs_2_, bf16[256,4096]{1,0:T(8,128)(2,1)} %get-tuple-element.36.refs_3_, bf16[2,256,256]{2,1,0:T(8,128)(2,1)} %copy-done.2, ...), custom_call_target="tpu_custom_call" | custom-call | flops 1073741824 | bytes 4194304 | tf_op jit(solution)/shard_map/messages/pallas_call | solution.py:236
  181.3 5.6 %near.2.refs_6_ = f32[1024,256]{1,0:T(8,128)} custom-call(s32[16,3]{1,0:T(8,128)} %broadcast_add_fusion.places, f32[4]{0:T(128)} %broadcast_multiply_fusion.2.scales, f32[20,8,128]{2,1,0:T(8,128)} %fusion.12.row_ref, bf16[2,128,256]{2,1,0:T(8,128)(2,1)} %bitcast.40, bf16[16,128,256]{2,1,0:T(8,128)(2,1)} %bitcast.28, bf16[2,128,256]{2,1,0:T(8,128)(2,1)} %bitcast.38, ...), custom_call_target="tpu_custom_call" | custom-call | flops 3221225472 | bytes 2097152 | tf_op jit(solution)/shard_map/near/pallas_call | solution.py:177
  186.9 3.6 %messages.19 = bf16[1024,256]{1,0:T(8,128)(2,1)} custom-call(bf16[256,4096]{1,0:T(8,128)(2,1)} %get-tuple-element.33.refs_0_, bf16[256,4096]{1,0:T(8,128)(2,1)} %get-tuple-element.34.refs_1_, bf16[256,4096]{1,0:T(8,128)(2,1)} %get-tuple-element.35.refs_2_, bf16[256,4096]{1,0:T(8,128)(2,1)} %get-tuple-element.36.refs_3_, bf16[2,256,256]{2,1,0:T(8,128)(2,1)} %copy-done.2, ...), custom_call_target="tpu_custom_call" | custom-call | flops 1073741824 | bytes 4194304 | tf_op jit(solution)/shard_map/messages/pallas_call | solution.py:236
  191.0 3.8 %messages.21.refs_6_ = f32[1024,256]{1,0:T(8,128)} custom-call(bf16[256,4096]{1,0:T(8,128)(2,1)} %get-tuple-element.51.refs_0_, bf16[256,4096]{1,0:T(8,128)(2,1)} %get-tuple-element.52.refs_1_, bf16[256,4096]{1,0:T(8,128)(2,1)} %get-tuple-element.53.refs_2_, bf16[256,4096]{1,0:T(8,128)(2,1)} %get-tuple-element.54.refs_3_, bf16[2,256,256]{2,1,0:T(8,128)(2,1)} %copy-done.6, ...), custom_call_target="tpu_custom_call" | custom-call | flops 1073741824 | bytes 4194304 | tf_op jit(solution)/shard_map/messages/pallas_call | solution.py:236
  194.8 3.8 %messages.13.refs_6_ = f32[1024,256]{1,0:T(8,128)} custom-call(bf16[256,4096]{1,0:T(8,128)(2,1)} %get-tuple-element.51.refs_0_, bf16[256,4096]{1,0:T(8,128)(2,1)} %get-tuple-element.52.refs_1_, bf16[256,4096]{1,0:T(8,128)(2,1)} %get-tuple-element.53.refs_2_, bf16[256,4096]{1,0:T(8,128)(2,1)} %get-tuple-element.54.refs_3_, bf16[2,256,256]{2,1,0:T(8,128)(2,1)} %copy-done.6, ...), custom_call_target="tpu_custom_call" | custom-call | flops 1073741824 | bytes 4194304 | tf_op jit(solution)/shard_map/messages/pallas_call | solution.py:236
  198.5 3.8 %messages.22.refs_6_ = f32[1024,256]{1,0:T(8,128)} custom-call(bf16[256,4096]{1,0:T(8,128)(2,1)} %get-tuple-element.45.refs_0_, bf16[256,4096]{1,0:T(8,128)(2,1)} %get-tuple-element.46.refs_1_, bf16[256,4096]{1,0:T(8,128)(2,1)} %get-tuple-element.47.refs_2_, bf16[256,4096]{1,0:T(8,128)(2,1)} %get-tuple-element.48.refs_3_, bf16[2,256,256]{2,1,0:T(8,128)(2,1)} %copy-done.4, ...), custom_call_target="tpu_custom_call" | custom-call | flops 1073741824 | bytes 4194304 | tf_op jit(solution)/shard_map/messages/pallas_call | solution.py:236
  202.3 3.8 %messages.23.refs_6_ = f32[1024,256]{1,0:T(8,128)} custom-call(bf16[256,4096]{1,0:T(8,128)(2,1)} %get-tuple-element.39.refs_0_, bf16[256,4096]{1,0:T(8,128)(2,1)} %get-tuple-element.40.refs_1_, bf16[256,4096]{1,0:T(8,128)(2,1)} %get-tuple-element.41.refs_2_, bf16[256,4096]{1,0:T(8,128)(2,1)} %get-tuple-element.42.refs_3_, bf16[2,256,256]{2,1,0:T(8,128)(2,1)} %copy-done.5, ...), custom_call_target="tpu_custom_call" | custom-call | flops 1073741824 | bytes 4194304 | tf_op jit(solution)/shard_map/messages/pallas_call | solution.py:236
  206.9 4.1 %messages.25 = (f32[1024,256]{1,0:T(8,128)}, bf16[1024,256]{1,0:T(8,128)(2,1)}) custom-call(bf16[256,4096]{1,0:T(8,128)(2,1)} %get-tuple-element.33.refs_0_, bf16[256,4096]{1,0:T(8,128)(2,1)} %get-tuple-element.34.refs_1_, bf16[256,4096]{1,0:T(8,128)(2,1)} %get-tuple-element.35.refs_2_, bf16[256,4096]{1,0:T(8,128)(2,1)} %get-tuple-element.36.refs_3_, ...), custom_call_target="tpu_custom_call" | custom-call | flops 1073741824 | bytes 4194304 | tf_op jit(solution)/shard_map/messages/pallas_call | solution.py:236
  211.9 3.8 %messages.14.refs_6_ = f32[1024,256]{1,0:T(8,128)} custom-call(bf16[256,4096]{1,0:T(8,128)(2,1)} %get-tuple-element.45.refs_0_, bf16[256,4096]{1,0:T(8,128)(2,1)} %get-tuple-element.46.refs_1_, bf16[256,4096]{1,0:T(8,128)(2,1)} %get-tuple-element.47.refs_2_, bf16[256,4096]{1,0:T(8,128)(2,1)} %get-tuple-element.48.refs_3_, bf16[2,256,256]{2,1,0:T(8,128)(2,1)} %copy-done.4, ...), custom_call_target="tpu_custom_call" | custom-call | flops 1073741824 | bytes 4194304 | tf_op jit(solution)/shard_map/messages/pallas_call | solution.py:236
  215.7 3.8 %messages.15.refs_6_ = f32[1024,256]{1,0:T(8,128)} custom-call(bf16[256,4096]{1,0:T(8,128)(2,1)} %get-tuple-element.39.refs_0_, bf16[256,4096]{1,0:T(8,128)(2,1)} %get-tuple-element.40.refs_1_, bf16[256,4096]{1,0:T(8,128)(2,1)} %get-tuple-element.41.refs_2_, bf16[256,4096]{1,0:T(8,128)(2,1)} %get-tuple-element.42.refs_3_, bf16[2,256,256]{2,1,0:T(8,128)(2,1)} %copy-done.5, ...), custom_call_target="tpu_custom_call" | custom-call | flops 1073741824 | bytes 4194304 | tf_op jit(solution)/shard_map/messages/pallas_call | solution.py:236
  220.2 4.1 %messages.20 = (f32[1024,256]{1,0:T(8,128)}, bf16[1024,256]{1,0:T(8,128)(2,1)}) custom-call(bf16[256,4096]{1,0:T(8,128)(2,1)} %get-tuple-element.33.refs_0_, bf16[256,4096]{1,0:T(8,128)(2,1)} %get-tuple-element.34.refs_1_, bf16[256,4096]{1,0:T(8,128)(2,1)} %get-tuple-element.35.refs_2_, bf16[256,4096]{1,0:T(8,128)(2,1)} %get-tuple-element.36.refs_3_, ...), custom_call_target="tpu_custom_call" | custom-call | flops 1073741824 | bytes 4194304 | tf_op jit(solution)/shard_map/messages/pallas_call | solution.py:236
  224.3 1.1 fusion.20
  225.4 1.2 collective-permute-start.40
  228.3 5.1 %mlp.3.refs_0_ = bf16[2048,256]{1,0:T(8,128)(2,1)} custom-call(s32[1]{0:T(128)} %bitcast.side, f32[1024,256]{1,0:T(8,128)} %get-tuple-element.59.own_ref, bf16[1024,256]{1,0:T(8,128)(2,1)} %copy-done.25, f32[2,256]{1,0:T(2,128)} %reshape.52.gain_ref, bf16[512,512]{1,0:T(8,128)(2,1)} %in0_ref.5, bf16[512,512]{1,0:T(8,128)(2,1)} %collective-permute-done.38.in1_ref, ...), custom_call_target="tpu_custom_call" | custom-call | flops 3221225472 | bytes 2097152 | tf_op jit(solution)/shard_map/mlp/pallas_call | solution.py:285
  233.4 1.3 collective-permute-done.40.other_ref
  235.3 3.6 %mlp.4.refs_0_ = bf16[2048,256]{1,0:T(8,128)(2,1)} custom-call(s32[1]{0:T(128)} %bitcast.side, f32[1024,256]{1,0:T(8,128)} %get-tuple-element.57.own_ref, bf16[512,256]{1,0:T(8,128)(2,1)} %copy-done.27, f32[2,256]{1,0:T(2,128)} %reshape.52.gain_ref, bf16[512,512]{1,0:T(8,128)(2,1)} %in0_ref.5, ...), custom_call_target="tpu_custom_call", output_to_operand_aliasing={{}: (8, {})} | custom-call | flops 1610612736 | bytes 1048576 | tf_op jit(solution)/shard_map/mlp/pallas_call | solution.py:285
  239.7 3.6 %mlp.5 = bf16[2048,256]{1,0:T(8,128)(2,1)} custom-call(s32[1]{0:T(128)} %bitcast.side, f32[1024,256]{1,0:T(8,128)} %get-tuple-element.57.own_ref, bf16[512,256]{1,0:T(8,128)(2,1)} %copy-done.26, f32[2,256]{1,0:T(2,128)} %reshape.52.gain_ref, bf16[512,512]{1,0:T(8,128)(2,1)} %in0_ref.5, ...), custom_call_target="tpu_custom_call", output_to_operand_aliasing={{}: (8, {})} | custom-call | flops 1610612736 | bytes 1048576 | tf_op jit(solution)/shard_map/mlp/pallas_call | solution.py:285
  (184 shorter events, 24.7 us)
Async XLA Ops:
  0.0 13.7 %copy-start = (f32[4,512]{1,0:T(4,128)S(1)}, f32[4,512]{1,0:T(4,128)}, u32[]{:S(2)}) copy-start(f32[4,512]{1,0:T(4,128)} %param.19) | copy-start | bytes 24580
  0.0 12.8 %copy-start.20 = (f32[3,2048]{1,0:T(4,128)S(1)}, f32[3,2048]{1,0:T(4,128)}, u32[]{:S(2)}) copy-start(f32[3,2048]{1,0:T(4,128)} %param.16) | copy-start | bytes 73732
  0.0 12.9 %copy-start.31 = (f32[4]{0:T(128)S(1)}, f32[4]{0:T(128)}, u32[]{:S(2)}) copy-start(f32[4]{0:T(128)} %param.18) | copy-start | bytes 52
  0.0 13.5 %copy-start.21 = (s32[16,3]{0,1:T(4,128)S(1)}, s32[16,3]{0,1:T(4,128)}, u32[]{:S(2)}) copy-start(s32[16,3]{0,1:T(4,128)} %param.15) | copy-start | bytes 580
  0.0 15.0 %copy-start.13 = (bf16[512,512]{1,0:T(8,128)(2,1)S(1)}, bf16[512,512]{1,0:T(8,128)(2,1)}, u32[]{:S(2)}) copy-start(bf16[512,512]{1,0:T(8,128)(2,1)} %param.22) | copy-start | bytes 1572868
  0.8 18.6 %collective-permute-start.32 = (f32[3,256]{1,0:T(4,128)S(1)}, f32[3,256]{1,0:T(4,128)S(1)}, u32[]{:S(2)}, u32[]{:S(2)}) collective-permute-start(f32[3,256]{1,0:T(4,128)S(1)} %get-tuple-element.73), channel_id=1, source_target_pairs={{0,2},{2,4},{4,6},{6,8},{8,10},{10,12},{12,14},{14,16},{16,18},{18... | collective-permute-start | bytes 9224 | tf_op jit(solution)/shard_map/ppermute | solution.py:384
  1.3 21.8 %collective-permute-start.33 = (f32[3,256]{1,0:T(4,128)S(1)}, f32[3,256]{1,0:T(4,128)S(1)}, u32[]{:S(2)}, u32[]{:S(2)}) collective-permute-start(f32[3,256]{1,0:T(4,128)S(1)} %get-tuple-element.74), channel_id=1, source_target_pairs={{2,0},{4,2},{6,4},{8,6},{10,8},{12,10},{14,12},{16,14},{18,16},{20... | collective-permute-start | bytes 9224 | tf_op jit(solution)/shard_map/ppermute | solution.py:385
  8.2 10.8 %collective-permute-start.7 = (f32[8,128]{1,0:T(8,128)S(1)}, f32[8,128]{1,0:T(8,128)S(1)}, u32[]{:S(2)}, u32[]{:S(2)}) collective-permute-start(f32[8,128]{1,0:T(8,128)S(1)} %broadcast_in_dim.14), channel_id=1, source_target_pairs={{0,2},{2,0},{4,6},{6,4},{8,10},{10,8},{12,14},{14,12},{16,18},{18,... | collective-permute-start | bytes 12296 | tf_op jit(solution)/shard_map/ppermute | solution.py:325
  8.3 24.2 %collective-permute-start = (f32[3,2048]{1,0:T(4,128)}, f32[3,2048]{1,0:T(4,128)S(1)}, u32[]{:S(2)}, u32[]{:S(2)}) collective-permute-start(f32[3,2048]{1,0:T(4,128)} %param.16), channel_id=1, source_target_pairs={{0,1},{1,0},{2,3},{3,2},{4,5},{5,4},{6,7},{7,6},{8,9},{9,8},{10,11... | collective-permute-start | bytes 73736 | tf_op jit(solution)/shard_map/ppermute | solution.py:320
  11.0 5.6 %copy-start.23 = (f32[3,1]{0,1:T(1,128)S(1)}, f32[3,1]{0,1:T(1,128)}, u32[]{:S(2)}) copy-start(f32[3,1]{0,1:T(1,128)} %constant.46.clone) | copy-start | bytes 40
  11.0 6.3 %copy-start.18 = (f32[3,2048]{1,0:T(4,128)S(1)}, f32[3,2048]{1,0:T(4,128)}, u32[]{:S(2)}) copy-start(f32[3,2048]{1,0:T(4,128)} %param.13) | copy-start | bytes 73732
  11.0 6.3 %copy-start.22 = (f32[512]{0:T(512)S(1)}, f32[512]{0:T(512)}, u32[]{:S(2)}) copy-start(f32[512]{0:T(512)} %param.20) | copy-start | bytes 6148
  12.6 20.6 %copy-start.10 = (bf16[2048,256]{1,0:T(8,128)(2,1)}, bf16[2048,256]{1,0:T(8,128)(2,1)S(1)}, u32[]{:S(2)}) copy-start(bf16[2048,256]{1,0:T(8,128)(2,1)S(1)} %broadcast_select_fusion.own_ref) | copy-start | bytes 3145732
  12.6 34.5 %collective-permute-start.2 = (bf16[2048,256]{1,0:T(8,128)(2,1)S(1)}, bf16[2048,256]{1,0:T(8,128)(2,1)}, u32[]{:S(2)}, u32[]{:S(2)}) collective-permute-start(bf16[2048,256]{1,0:T(8,128)(2,1)S(1)} %broadcast_select_fusion.own_ref), channel_id=1, source_target_pairs={{0,2},{2,0},{4,6},{6,4},{8,10},{10,8},{12,14},{14,12},{16,18},{18,... | collective-permute-start | bytes 3145736 | tf_op jit(solution)/shard_map/ppermute | solution.py:325
  13.6 26.0 %copy-start.24 = (bf16[512,512]{1,0:T(8,128)(2,1)S(1)}, bf16[512,512]{1,0:T(8,128)(2,1)}, u32[]{:S(2)}) copy-start(bf16[512,512]{1,0:T(8,128)(2,1)} %in0_ref.5) | copy-start | bytes 1572868
  17.4 29.7 %copy-start.19 = (f32[8,2048]{1,0:T(8,128)}, f32[8,2048]{1,0:T(8,128)S(1)}, u32[]{:S(2)}) copy-start(f32[8,2048]{1,0:T(8,128)S(1)} %pad.15.own_pos) | copy-start | bytes 196612
  19.1 28.0 %collective-permute-start.1 = (f32[8,2048]{1,0:T(8,128)S(1)}, f32[8,2048]{1,0:T(8,128)S(1)}, u32[]{:S(2)}, u32[]{:S(2)}) collective-permute-start(f32[8,2048]{1,0:T(8,128)S(1)} %pad.15.own_pos), channel_id=1, source_target_pairs={{0,2},{2,0},{4,6},{6,4},{8,10},{10,8},{12,14},{14,12},{16,18},{18,... | collective-permute-start | bytes 196616 | tf_op jit(solution)/shard_map/ppermute | solution.py:325
  19.4 3.6 %collective-permute-start.8 = (f32[8,128]{1,0:T(8,128)S(1)}, f32[8,128]{1,0:T(8,128)S(1)}, u32[]{:S(2)}, u32[]{:S(2)}) collective-permute-start(f32[8,128]{1,0:T(8,128)S(1)} %broadcast_add_fusion.2), channel_id=1, source_target_pairs={{0,4},{2,6},{4,0},{6,2},{8,12},{10,14},{12,8},{14,10},{16,20},{18,... | collective-permute-start | bytes 12296 | tf_op jit(solution)/shard_map/ppermute | solution.py:325
  23.0 24.1 %collective-permute-start.6 = (f32[2,64,256]{2,1,0:T(8,128)S(1)}, f32[2,64,256]{2,1,0:T(8,128)S(1)}, u32[]{:S(2)}, u32[]{:S(2)}) collective-permute-start(f32[2,64,256]{2,1,0:T(8,128)S(1)} %pad_maximum_fusion.4), channel_id=1, source_target_pairs={{0,1},{1,0},{2,3},{3,2},{4,5},{5,4},{6,7},{7,6},{8,9},{9,8},{10,11... | collective-permute-start | bytes 393224 | tf_op jit(solution)/shard_map/ppermute | solution.py:320
  23.1 3.6 %collective-permute-start.9 = (f32[8,128]{1,0:T(8,128)S(1)}, f32[8,128]{1,0:T(8,128)S(1)}, u32[]{:S(2)}, u32[]{:S(2)}) collective-permute-start(f32[8,128]{1,0:T(8,128)S(1)} %fusion.22), channel_id=1, source_target_pairs={{0,8},{2,10},{4,12},{6,14},{8,0},{10,2},{12,4},{14,6},{16,24},{18,... | collective-permute-start | bytes 12296 | tf_op jit(solution)/shard_map/ppermute | solution.py:325
  26.7 4.5 %collective-permute-start.10 = (f32[8,128]{1,0:T(8,128)S(1)}, f32[8,128]{1,0:T(8,128)S(1)}, u32[]{:S(2)}, u32[]{:S(2)}) collective-permute-start(f32[8,128]{1,0:T(8,128)S(1)} %add.124), channel_id=1, source_target_pairs={{0,16},{2,18},{4,20},{6,22},{8,24},{10,26},{12,28},{14,30},{16,0},... | collective-permute-start | bytes 12296 | tf_op jit(solution)/shard_map/ppermute | solution.py:325
  31.2 3.0 %collective-permute-start.35 = (bf16[256,256]{1,0:T(8,128)(2,1)S(1)}, bf16[256,256]{1,0:T(8,128)(2,1)S(1)}, u32[]{:S(2)}, u32[]{:S(2)}) collective-permute-start(bf16[256,256]{1,0:T(8,128)(2,1)S(1)} %get-tuple-element.65), channel_id=1, source_target_pairs={{2,0},{4,2},{6,4},{8,6},{10,8},{12,10},{14,12},{16,14},{18,16},{20... | collective-permute-start | bytes 393224 | tf_op jit(solution)/shard_map/ppermute | solution.py:383
  32.5 7.1 %collective-permute-start.34 = (bf16[256,256]{1,0:T(8,128)(2,1)S(1)}, bf16[256,256]{1,0:T(8,128)(2,1)S(1)}, u32[]{:S(2)}, u32[]{:S(2)}) collective-permute-start(bf16[256,256]{1,0:T(8,128)(2,1)S(1)} %get-tuple-element.66), channel_id=1, source_target_pairs={{0,2},{2,4},{4,6},{6,8},{8,10},{10,12},{12,14},{14,16},{16,18},{18... | collective-permute-start | bytes 393224 | tf_op jit(solution)/shard_map/ppermute | solution.py:382
  34.2 7.4 %copy-start.28 = (bf16[256,256]{1,0:T(8,128)(2,1)}, bf16[256,256]{1,0:T(8,128)(2,1)S(1)}, u32[]{:S(2)}) copy-start(bf16[256,256]{1,0:T(8,128)(2,1)S(1)} %collective-permute-done.35) | copy-start | bytes 393220
  34.2 193.3 %collective-permute-start.39 = (bf16[512,256]{1,0:T(8,128)(2,1)S(1)}, bf16[512,256]{1,0:T(8,128)(2,1)}, u32[]{:S(2)}, u32[]{:S(2)}) collective-permute-start(bf16[512,256]{1,0:T(8,128)(2,1)S(1)} %get-tuple-element.69), channel_id=1, source_target_pairs={{0,1},{1,0},{2,3},{3,2},{4,5},{5,4},{6,7},{7,6},{8,9},{9,8},{10,11... | collective-permute-start | bytes 786440 | tf_op jit(solution)/shard_map/ppermute | solution.py:320
  39.7 187.8 %collective-permute-start.38 = (bf16[512,512]{1,0:T(8,128)(2,1)S(1)}, bf16[512,512]{1,0:T(8,128)(2,1)}, u32[]{:S(2)}, u32[]{:S(2)}) collective-permute-start(bf16[512,512]{1,0:T(8,128)(2,1)S(1)} %copy-done.24), channel_id=1, source_target_pairs={{0,1},{1,0},{2,3},{3,2},{4,5},{5,4},{6,7},{7,6},{8,9},{9,8},{10,11... | collective-permute-start | bytes 1572872 | tf_op jit(solution)/shard_map/ppermute | solution.py:320
  55.8 55.5 %collective-permute-start.26 = (bf16[2,256,256]{2,1,0:T(8,128)(2,1)}, bf16[2,256,256]{2,1,0:T(8,128)(2,1)S(1)}, u32[]{:S(2)}, u32[]{:S(2)}) collective-permute-start(bf16[2,256,256]{2,1,0:T(8,128)(2,1)} %get-tuple-element.56), channel_id=1, source_target_pairs={{0,4},{2,6},{4,0},{6,2},{8,12},{10,14},{12,8},{14,10},{16,20},{18,... | collective-permute-start | bytes 786440 | tf_op jit(solution)/shard_map/ppermute | solution.py:325
  63.3 50.1 %collective-permute-start.20 = (bf16[2,256,256]{2,1,0:T(8,128)(2,1)}, bf16[2,256,256]{2,1,0:T(8,128)(2,1)S(1)}, u32[]{:S(2)}, u32[]{:S(2)}) collective-permute-start(bf16[2,256,256]{2,1,0:T(8,128)(2,1)} %get-tuple-element.50), channel_id=1, source_target_pairs={{0,4},{2,6},{4,0},{6,2},{8,12},{10,14},{12,8},{14,10},{16,20},{18,... | collective-permute-start | bytes 786440 | tf_op jit(solution)/shard_map/ppermute | solution.py:325
  72.9 40.7 %collective-permute-start.14 = (bf16[2,256,256]{2,1,0:T(8,128)(2,1)}, bf16[2,256,256]{2,1,0:T(8,128)(2,1)S(1)}, u32[]{:S(2)}, u32[]{:S(2)}) collective-permute-start(bf16[2,256,256]{2,1,0:T(8,128)(2,1)} %get-tuple-element.44), channel_id=1, source_target_pairs={{0,4},{2,6},{4,0},{6,2},{8,12},{10,14},{12,8},{14,10},{16,20},{18,... | collective-permute-start | bytes 786440 | tf_op jit(solution)/shard_map/ppermute | solution.py:325
  103.6 9.8 %copy-start.17 = (f32[2,256,256]{2,1,0:T(8,128)S(1)}, f32[2,256,256]{2,1,0:T(8,128)}, u32[]{:S(2)}) copy-start(f32[2,256,256]{2,1,0:T(8,128)} %get-tuple-element.55) | copy-start | bytes 1572868
  103.6 10.0 %copy-start.16 = (f32[2,256,256]{2,1,0:T(8,128)S(1)}, f32[2,256,256]{2,1,0:T(8,128)}, u32[]{:S(2)}) copy-start(f32[2,256,256]{2,1,0:T(8,128)} %get-tuple-element.49) | copy-start | bytes 1572868
  111.3 4.4 %copy-start.15 = (f32[2,256,256]{2,1,0:T(8,128)S(1)}, f32[2,256,256]{2,1,0:T(8,128)}, u32[]{:S(2)}) copy-start(f32[2,256,256]{2,1,0:T(8,128)} %get-tuple-element.43) | copy-start | bytes 1572868
  111.3 6.6 %collective-permute-start.3 = (bf16[2,256,256]{2,1,0:T(8,128)(2,1)}, bf16[2,256,256]{2,1,0:T(8,128)(2,1)S(1)}, u32[]{:S(2)}, u32[]{:S(2)}) collective-permute-start(bf16[2,256,256]{2,1,0:T(8,128)(2,1)} %get-tuple-element.38), channel_id=1, source_target_pairs={{0,4},{2,6},{4,0},{6,2},{8,12},{10,14},{12,8},{14,10},{16,20},{18,... | collective-permute-start | bytes 786440 | tf_op jit(solution)/shard_map/ppermute | solution.py:325
  113.4 4.6 %copy-start.14 = (f32[2,256,256]{2,1,0:T(8,128)S(1)}, f32[2,256,256]{2,1,0:T(8,128)}, u32[]{:S(2)}) copy-start(f32[2,256,256]{2,1,0:T(8,128)} %get-tuple-element.37) | copy-start | bytes 1572868
  113.5 6.2 %collective-permute-start.27 = (bf16[2,128,256]{2,1,0:T(8,128)(2,1)S(1)}, bf16[2,128,256]{2,1,0:T(8,128)(2,1)S(1)}, u32[]{:S(2)}, u32[]{:S(2)}) collective-permute-start(bf16[2,128,256]{2,1,0:T(8,128)(2,1)S(1)} %slice.170), channel_id=1, source_target_pairs={{0,8},{2,10},{4,12},{6,14},{8,0},{10,2},{12,4},{14,6},{16,24},{18,... | collective-permute-start | bytes 393224 | tf_op jit(solution)/shard_map/ppermute | solution.py:325
  113.7 8.1 %collective-permute-start.21 = (bf16[2,128,256]{2,1,0:T(8,128)(2,1)S(1)}, bf16[2,128,256]{2,1,0:T(8,128)(2,1)S(1)}, u32[]{:S(2)}, u32[]{:S(2)}) collective-permute-start(bf16[2,128,256]{2,1,0:T(8,128)(2,1)S(1)} %slice.171), channel_id=1, source_target_pairs={{0,8},{2,10},{4,12},{6,14},{8,0},{10,2},{12,4},{14,6},{16,24},{18,... | collective-permute-start | bytes 393224 | tf_op jit(solution)/shard_map/ppermute | solution.py:325
  117.9 5.2 %collective-permute-start.15 = (bf16[2,128,256]{2,1,0:T(8,128)(2,1)S(1)}, bf16[2,128,256]{2,1,0:T(8,128)(2,1)S(1)}, u32[]{:S(2)}, u32[]{:S(2)}) collective-permute-start(bf16[2,128,256]{2,1,0:T(8,128)(2,1)S(1)} %slice.172), channel_id=1, source_target_pairs={{0,8},{2,10},{4,12},{6,14},{8,0},{10,2},{12,4},{14,6},{16,24},{18,... | collective-permute-start | bytes 393224 | tf_op jit(solution)/shard_map/ppermute | solution.py:325
  119.6 5.7 %collective-permute-start.4 = (bf16[2,128,256]{2,1,0:T(8,128)(2,1)S(1)}, bf16[2,128,256]{2,1,0:T(8,128)(2,1)S(1)}, u32[]{:S(2)}, u32[]{:S(2)}) collective-permute-start(bf16[2,128,256]{2,1,0:T(8,128)(2,1)S(1)} %slice.173), channel_id=1, source_target_pairs={{0,8},{2,10},{4,12},{6,14},{8,0},{10,2},{12,4},{14,6},{16,24},{18,... | collective-permute-start | bytes 393224 | tf_op jit(solution)/shard_map/ppermute | solution.py:325
  121.7 8.7 %collective-permute-start.28 = (bf16[2,64,256]{2,1,0:T(8,128)(2,1)S(1)}, bf16[2,64,256]{2,1,0:T(8,128)(2,1)S(1)}, u32[]{:S(2)}, u32[]{:S(2)}) collective-permute-start(bf16[2,64,256]{2,1,0:T(8,128)(2,1)S(1)} %slice.174), channel_id=1, source_target_pairs={{0,16},{2,18},{4,20},{6,22},{8,24},{10,26},{12,28},{14,30},{16,0},... | collective-permute-start | bytes 196616 | tf_op jit(solution)/shard_map/ppermute | solution.py:325
  123.1 10.1 %collective-permute-start.22 = (bf16[2,64,256]{2,1,0:T(8,128)(2,1)S(1)}, bf16[2,64,256]{2,1,0:T(8,128)(2,1)S(1)}, u32[]{:S(2)}, u32[]{:S(2)}) collective-permute-start(bf16[2,64,256]{2,1,0:T(8,128)(2,1)S(1)} %slice.175), channel_id=1, source_target_pairs={{0,16},{2,18},{4,20},{6,22},{8,24},{10,26},{12,28},{14,30},{16,0},... | collective-permute-start | bytes 196616 | tf_op jit(solution)/shard_map/ppermute | solution.py:325
  125.3 10.0 %collective-permute-start.16 = (bf16[2,64,256]{2,1,0:T(8,128)(2,1)S(1)}, bf16[2,64,256]{2,1,0:T(8,128)(2,1)S(1)}, u32[]{:S(2)}, u32[]{:S(2)}) collective-permute-start(bf16[2,64,256]{2,1,0:T(8,128)(2,1)S(1)} %slice.176), channel_id=1, source_target_pairs={{0,16},{2,18},{4,20},{6,22},{8,24},{10,26},{12,28},{14,30},{16,0},... | collective-permute-start | bytes 196616 | tf_op jit(solution)/shard_map/ppermute | solution.py:325
  130.4 7.7 %collective-permute-start.5 = (bf16[2,64,256]{2,1,0:T(8,128)(2,1)S(1)}, bf16[2,64,256]{2,1,0:T(8,128)(2,1)S(1)}, u32[]{:S(2)}, u32[]{:S(2)}) collective-permute-start(bf16[2,64,256]{2,1,0:T(8,128)(2,1)S(1)} %slice.177), channel_id=1, source_target_pairs={{0,16},{2,18},{4,20},{6,22},{8,24},{10,26},{12,28},{14,30},{16,0},... | collective-permute-start | bytes 196616 | tf_op jit(solution)/shard_map/ppermute | solution.py:325
  133.2 7.7 %collective-permute-start.29 = (bf16[2,64,256]{2,1,0:T(8,128)(2,1)S(1)}, bf16[2,64,256]{2,1,0:T(8,128)(2,1)S(1)}, u32[]{:S(2)}, u32[]{:S(2)}) collective-permute-start(bf16[2,64,256]{2,1,0:T(8,128)(2,1)S(1)} %fusion.2), channel_id=1, source_target_pairs={{0,16},{2,18},{4,20},{6,22},{8,24},{10,26},{12,28},{14,30},{16,0},... | collective-permute-start | bytes 196616 | tf_op jit(solution)/shard_map/ppermute | solution.py:325
  135.3 6.3 %collective-permute-start.23 = (bf16[2,64,256]{2,1,0:T(8,128)(2,1)S(1)}, bf16[2,64,256]{2,1,0:T(8,128)(2,1)S(1)}, u32[]{:S(2)}, u32[]{:S(2)}) collective-permute-start(bf16[2,64,256]{2,1,0:T(8,128)(2,1)S(1)} %fusion.5), channel_id=1, source_target_pairs={{0,16},{2,18},{4,20},{6,22},{8,24},{10,26},{12,28},{14,30},{16,0},... | collective-permute-start | bytes 196616 | tf_op jit(solution)/shard_map/ppermute | solution.py:325
  138.1 5.5 %collective-permute-start.17 = (bf16[2,64,256]{2,1,0:T(8,128)(2,1)S(1)}, bf16[2,64,256]{2,1,0:T(8,128)(2,1)S(1)}, u32[]{:S(2)}, u32[]{:S(2)}) collective-permute-start(bf16[2,64,256]{2,1,0:T(8,128)(2,1)S(1)} %fusion.8), channel_id=1, source_target_pairs={{0,16},{2,18},{4,20},{6,22},{8,24},{10,26},{12,28},{14,30},{16,0},... | collective-permute-start | bytes 196616 | tf_op jit(solution)/shard_map/ppermute | solution.py:325
  140.9 5.5 %collective-permute-start.11 = (bf16[2,64,256]{2,1,0:T(8,128)(2,1)S(1)}, bf16[2,64,256]{2,1,0:T(8,128)(2,1)S(1)}, u32[]{:S(2)}, u32[]{:S(2)}) collective-permute-start(bf16[2,64,256]{2,1,0:T(8,128)(2,1)S(1)} %fusion.11), channel_id=1, source_target_pairs={{0,16},{2,18},{4,20},{6,22},{8,24},{10,26},{12,28},{14,30},{16,0},... | collective-permute-start | bytes 196616 | tf_op jit(solution)/shard_map/ppermute | solution.py:325
  141.6 7.1 %collective-permute-start.30 = (bf16[2,128,256]{2,1,0:T(8,128)(2,1)S(1)}, bf16[2,128,256]{2,1,0:T(8,128)(2,1)S(1)}, u32[]{:S(2)}, u32[]{:S(2)}) collective-permute-start(bf16[2,128,256]{2,1,0:T(8,128)(2,1)S(1)} %pad_maximum_fusion.8), channel_id=1, source_target_pairs={{0,8},{2,10},{4,12},{6,14},{8,0},{10,2},{12,4},{14,6},{16,24},{18,... | collective-permute-start | bytes 393224 | tf_op jit(solution)/shard_map/ppermute | solution.py:325
  143.6 6.6 %collective-permute-start.24 = (bf16[2,128,256]{2,1,0:T(8,128)(2,1)S(1)}, bf16[2,128,256]{2,1,0:T(8,128)(2,1)S(1)}, u32[]{:S(2)}, u32[]{:S(2)}) collective-permute-start(bf16[2,128,256]{2,1,0:T(8,128)(2,1)S(1)} %pad_maximum_fusion.7), channel_id=1, source_target_pairs={{0,8},{2,10},{4,12},{6,14},{8,0},{10,2},{12,4},{14,6},{16,24},{18,... | collective-permute-start | bytes 393224 | tf_op jit(solution)/shard_map/ppermute | solution.py:325
  146.4 5.5 %collective-permute-start.18 = (bf16[2,128,256]{2,1,0:T(8,128)(2,1)S(1)}, bf16[2,128,256]{2,1,0:T(8,128)(2,1)S(1)}, u32[]{:S(2)}, u32[]{:S(2)}) collective-permute-start(bf16[2,128,256]{2,1,0:T(8,128)(2,1)S(1)} %pad_maximum_fusion.6), channel_id=1, source_target_pairs={{0,8},{2,10},{4,12},{6,14},{8,0},{10,2},{12,4},{14,6},{16,24},{18,... | collective-permute-start | bytes 393224 | tf_op jit(solution)/shard_map/ppermute | solution.py:325
  148.7 5.0 %collective-permute-start.12 = (bf16[2,128,256]{2,1,0:T(8,128)(2,1)S(1)}, bf16[2,128,256]{2,1,0:T(8,128)(2,1)S(1)}, u32[]{:S(2)}, u32[]{:S(2)}) collective-permute-start(bf16[2,128,256]{2,1,0:T(8,128)(2,1)S(1)} %pad_maximum_fusion.5), channel_id=1, source_target_pairs={{0,8},{2,10},{4,12},{6,14},{8,0},{10,2},{12,4},{14,6},{16,24},{18,... | collective-permute-start | bytes 393224 | tf_op jit(solution)/shard_map/ppermute | solution.py:325
  149.0 12.1 %copy-start.6 = (bf16[2,256,256]{2,1,0:T(8,128)(2,1)}, bf16[2,256,256]{2,1,0:T(8,128)(2,1)S(1)}, u32[]{:S(2)}) copy-start(bf16[2,256,256]{2,1,0:T(8,128)(2,1)S(1)} %pad_maximum_fusion.3.refs_4_) | copy-start | bytes 786436
  150.2 9.2 %collective-permute-start.31 = (bf16[2,256,256]{2,1,0:T(8,128)(2,1)S(1)}, bf16[2,256,256]{2,1,0:T(8,128)(2,1)S(1)}, u32[]{:S(2)}, u32[]{:S(2)}) collective-permute-start(bf16[2,256,256]{2,1,0:T(8,128)(2,1)S(1)} %pad_maximum_fusion.3.refs_4_), channel_id=1, source_target_pairs={{0,4},{2,6},{4,0},{6,2},{8,12},{10,14},{12,8},{14,10},{16,20},{18,... | collective-permute-start | bytes 786440 | tf_op jit(solution)/shard_map/ppermute | solution.py:325
  151.9 13.6 %copy-start.4 = (bf16[2,256,256]{2,1,0:T(8,128)(2,1)}, bf16[2,256,256]{2,1,0:T(8,128)(2,1)S(1)}, u32[]{:S(2)}) copy-start(bf16[2,256,256]{2,1,0:T(8,128)(2,1)S(1)} %pad_maximum_fusion.2.refs_4_) | copy-start | bytes 786436
  151.9 13.6 %collective-permute-start.25 = (bf16[2,256,256]{2,1,0:T(8,128)(2,1)S(1)}, bf16[2,256,256]{2,1,0:T(8,128)(2,1)S(1)}, u32[]{:S(2)}, u32[]{:S(2)}) collective-permute-start(bf16[2,256,256]{2,1,0:T(8,128)(2,1)S(1)} %pad_maximum_fusion.2.refs_4_), channel_id=1, source_target_pairs={{0,4},{2,6},{4,0},{6,2},{8,12},{10,14},{12,8},{14,10},{16,20},{18,... | collective-permute-start | bytes 786440 | tf_op jit(solution)/shard_map/ppermute | solution.py:325
  153.3 12.2 %copy-start.5 = (bf16[2,256,256]{2,1,0:T(8,128)(2,1)}, bf16[2,256,256]{2,1,0:T(8,128)(2,1)S(1)}, u32[]{:S(2)}) copy-start(bf16[2,256,256]{2,1,0:T(8,128)(2,1)S(1)} %pad_maximum_fusion.1.refs_4_) | copy-start | bytes 786436
  153.6 17.5 %collective-permute-start.19 = (bf16[2,256,256]{2,1,0:T(8,128)(2,1)S(1)}, bf16[2,256,256]{2,1,0:T(8,128)(2,1)S(1)}, u32[]{:S(2)}, u32[]{:S(2)}) collective-permute-start(bf16[2,256,256]{2,1,0:T(8,128)(2,1)S(1)} %pad_maximum_fusion.1.refs_4_), channel_id=1, source_target_pairs={{0,4},{2,6},{4,0},{6,2},{8,12},{10,14},{12,8},{14,10},{16,20},{18,... | collective-permute-start | bytes 786440 | tf_op jit(solution)/shard_map/ppermute | solution.py:325
  154.7 10.8 %copy-start.2 = (bf16[2,256,256]{2,1,0:T(8,128)(2,1)}, bf16[2,256,256]{2,1,0:T(8,128)(2,1)S(1)}, u32[]{:S(2)}) copy-start(bf16[2,256,256]{2,1,0:T(8,128)(2,1)S(1)} %pad_maximum_fusion.refs_4_) | copy-start | bytes 786436
  159.4 17.6 %collective-permute-start.13 = (bf16[2,256,256]{2,1,0:T(8,128)(2,1)S(1)}, bf16[2,256,256]{2,1,0:T(8,128)(2,1)S(1)}, u32[]{:S(2)}, u32[]{:S(2)}) collective-permute-start(bf16[2,256,256]{2,1,0:T(8,128)(2,1)S(1)} %pad_maximum_fusion.refs_4_), channel_id=1, source_target_pairs={{0,4},{2,6},{4,0},{6,2},{8,12},{10,14},{12,8},{14,10},{16,20},{18,... | collective-permute-start | bytes 786440 | tf_op jit(solution)/shard_map/ppermute | solution.py:325
  181.3 24.8 %collective-permute-start.41 = (bf16[1024,256]{1,0:T(8,128)(2,1)}, bf16[1024,256]{1,0:T(8,128)(2,1)S(1)}, u32[]{:S(2)}, u32[]{:S(2)}) collective-permute-start(bf16[1024,256]{1,0:T(8,128)(2,1)} %messages.24), channel_id=1, source_target_pairs={{0,2},{2,0},{4,6},{6,4},{8,10},{10,8},{12,14},{14,12},{16,18},{18,... | collective-permute-start | bytes 1572872 | tf_op jit(solution)/shard_map/ppermute | solution.py:325
  190.5 29.0 %collective-permute-start.36 = (bf16[1024,256]{1,0:T(8,128)(2,1)}, bf16[1024,256]{1,0:T(8,128)(2,1)S(1)}, u32[]{:S(2)}, u32[]{:S(2)}) collective-permute-start(bf16[1024,256]{1,0:T(8,128)(2,1)} %messages.19), channel_id=1, source_target_pairs={{0,2},{2,0},{4,6},{6,4},{8,10},{10,8},{12,14},{14,12},{16,18},{18,... | collective-permute-start | bytes 1572872 | tf_op jit(solution)/shard_map/ppermute | solution.py:325
  211.0 16.5 %collective-permute-start.42 = (bf16[1024,256]{1,0:T(8,128)(2,1)}, bf16[1024,256]{1,0:T(8,128)(2,1)S(1)}, u32[]{:S(2)}, u32[]{:S(2)}) collective-permute-start(bf16[1024,256]{1,0:T(8,128)(2,1)} %get-tuple-element.60), channel_id=1, source_target_pairs={{0,1},{1,0},{2,3},{3,2},{4,5},{5,4},{6,7},{7,6},{8,9},{9,8},{10,11... | collective-permute-start | bytes 1572872 | tf_op jit(solution)/shard_map/ppermute | solution.py:320
  225.4 9.2 %collective-permute-start.40 = (bf16[512,256]{1,0:T(8,128)(2,1)S(1)}, bf16[512,256]{1,0:T(8,128)(2,1)S(1)}, u32[]{:S(2)}, u32[]{:S(2)}) collective-permute-start(bf16[512,256]{1,0:T(8,128)(2,1)S(1)} %get-tuple-element.67), channel_id=1, source_target_pairs={{0,1},{1,0},{2,3},{3,2},{4,5},{5,4},{6,7},{7,6},{8,9},{9,8},{10,11... | collective-permute-start | bytes 786440 | tf_op jit(solution)/shard_map/ppermute | solution.py:320
  226.6 12.4 %collective-permute-start.37 = (bf16[512,256]{1,0:T(8,128)(2,1)S(1)}, bf16[512,256]{1,0:T(8,128)(2,1)S(1)}, u32[]{:S(2)}, u32[]{:S(2)}) collective-permute-start(bf16[512,256]{1,0:T(8,128)(2,1)S(1)} %get-tuple-element.68), channel_id=1, source_target_pairs={{0,1},{1,0},{2,3},{3,2},{4,5},{5,4},{6,7},{7,6},{8,9},{9,8},{10,11... | collective-permute-start | bytes 786440 | tf_op jit(solution)/shard_map/ppermute | solution.py:320
  235.3 7.9 %copy-start.1 = (f32[4,512]{1,0:T(4,128)S(1)}, f32[4,512]{1,0:T(4,128)}, u32[]{:S(2)}) copy-start(f32[4,512]{1,0:T(4,128)} %param.19) | copy-start | bytes 24580
  (11 other events, 10.2 us)

commit v3 on v2

--- a/solution.py
+++ b/solution.py
@@ -10,37 +10,33 @@
 
 EPS = 1e-06
 HW = 2
-CHUNKS = 2
+SHARES = ((1.0,), (1.0,))
+GROUPS = (1,)
 TILE = 256
-FORWARD_ROWS = 128
-
-SCALE = 8.0**0.25
-SIN_QUARTER = [SCALE * c for c in (1.5707884677838282, -0.6457119641929367, 0.07766728844449011)]
-COS_QUARTER = [
-    SCALE * c for c in (0.9999999724196053, -1.2336970139164884, 0.2535986397412255, -0.02040833859268099)
-]
-
-
-def horner(x, coefs):
-    value = jnp.float32(coefs[-1])
-    for coef in coefs[-2::-1]:
-        value = value * x + jnp.float32(coef)
-    return value
+FORWARD_ROWS = 256
+
+SIN_1, SIN_0, SIN_BY = -8.313817368817206, 20.224572228345814, 12.875426983082301
+COS_ROOT, COS_1, COS_0 = 0.9993568028372194, -11.426868481113639, 49.031109066681445
+COS_BY = -48.99957374784235
+HALF = SIN_BY**2 / 2.0
+WHOLE_COS = (SIN_BY * COS_BY) ** 2 / 8.0
+WHOLE_SIN = SIN_BY**3 * COS_BY / 8.0
 
 
 def cos_sin_turns(turns):
+    f32 = jnp.float32
     rest = turns - jnp.round(turns)
     square = rest * rest
-    sin_quarter = horner(square, SIN_QUARTER) * rest
-    cos_quarter = horner(square, COS_QUARTER)
+    sin_quarter = rest * ((square + f32(SIN_1)) * square + f32(SIN_0))
+    cos_quarter = (square - f32(COS_ROOT)) * ((square + f32(COS_1)) * square + f32(COS_0))
     sin_half = sin_quarter * cos_quarter
-    cos_half = jnp.float32(math.sqrt(2.0)) - sin_quarter * sin_quarter
-    return jnp.float32(1.0) - sin_half * sin_half, sin_half * cos_half
+    cos_half = f32(HALF) - sin_quarter * sin_quarter
+    return f32(WHOLE_COS) - sin_half * sin_half, sin_half * cos_half
 
 
 def forward_body(
     start, first, block_rows, places, waves_ref, own_pos, other_pos, own_ref, other_ref,
-    cos_ref, sin_ref, sum_ref, lhs, rhs, turns,
+    cos_ref, sin_ref, sum_ref, turned, lhs, rhs, turns,
 ):
     rows = lhs.shape[0]
     step = pl.program_id(0)
@@ -50,7 +46,8 @@
     @pl.when(step == 0)
     def _():
         for number, ref in enumerate((own_pos, other_pos)):
-            high, middle, low = thirds(ref[...])
+            keep = lax.broadcasted_iota(jnp.int32, ref.shape, 0) < 3
+            high, middle, low = thirds(jnp.where(keep, ref[...], jnp.float32(0)))
             rhs[:, number * atom_rows : (number + 1) * atom_rows] = jnp.concatenate(
                 [high, middle, high, low, high, middle], axis=0
             ).astype(jnp.bfloat16)
@@ -58,7 +55,9 @@
     for part in range(rows // block_rows):
         number = (first + step * (rows // block_rows) + part) ^ places[0]
         at = pl.multiple_of(places[1] + start + number * block_rows, block_rows)
-        lhs[part * block_rows : (part + 1) * block_rows, :] = waves_ref[pl.ds(at, block_rows), :]
+        turned[part * block_rows : (part + 1) * block_rows, :] = waves_ref[pl.ds(at, block_rows), :]
+    high, middle, low = thirds(turned[...])
+    lhs[...] = jnp.concatenate([high, high, middle, high, low, middle], axis=1).astype(jnp.bfloat16)
 
     blocks = [(ref, base) for ref in (own_ref, other_ref) for base in range(0, atom_rows, TILE)]
 
@@ -114,8 +113,9 @@
                 pl.BlockSpec((2, tile, width), lambda k, *_: (0, k, 0)),
             ],
             scratch_shapes=[
-                pltpu.VMEM((tile, depth), jnp.bfloat16),
-                pltpu.VMEM((depth, 2 * atom_rows), jnp.bfloat16),
+                pltpu.VMEM((tile, depth), jnp.float32),
+                pltpu.VMEM((tile, 6 * depth), jnp.bfloat16),
+                pltpu.VMEM((6 * depth, 2 * atom_rows), jnp.bfloat16),
                 pltpu.VMEM((3, tile, TILE), jnp.float32),
             ],
         ),
@@ -129,7 +129,8 @@
     )(places, waves, *positions, *feats)
 
 
-def near_body(base, places, scales, row_ref, left_ref, masked_ref, right_ref, feats_ref, mix_ref, out_ref, wide, kernels, partners):
+def near_body(base, places, scales, row_ref, left_ref, masked_ref, right_ref, feats_ref, mix_ref, *refs):
+    out_ref, wide, kernels, partners = refs[-4:]
     cells_per_step = kernels.shape[0]
     cap = wide.shape[1]
     step = pl.program_id(0)
@@ -167,12 +168,13 @@
         out_ref[at, :] = near
 
 
-def near_part(base, cells, places, scales, rows, left, masked, right, feats, mix):
+def near_part(base, cells, places, scales, rows, left, masked, right, feats, mix, result):
     count = places.shape[1]
     cap, width = masked.shape[1:]
     kinds = mix.shape[0]
-    per = min(8, cells)
+    per = min(4, cells)
     offset = base // per
+    args = [] if result is None else [result]
     whole3 = lambda a: pl.BlockSpec(a.shape, lambda c, *_: (0, 0, 0))
     return pl.pallas_call(
         functools.partial(near_body, base),
@@ -186,35 +188,38 @@
                 whole3(right),
                 pl.BlockSpec((per * cap, width), lambda c, *_: (c + offset, 0)),
                 pl.BlockSpec(mix.shape, lambda c, *_: (0, 0)),
-            ],
-            out_specs=pl.BlockSpec((per * cap, width), lambda c, *_: (c, 0)),
+            ]
+            + [pl.BlockSpec(memory_space=pl.ANY)] * len(args),
+            out_specs=pl.BlockSpec((per * cap, width), lambda c, *_: (c + offset, 0)),
             scratch_shapes=[
                 pltpu.VMEM((rows.shape[0], cap, width), jnp.bfloat16),
                 pltpu.VMEM((per, kinds * cap, count * cap), jnp.bfloat16),
                 pltpu.VMEM((per, count * cap, width), jnp.bfloat16),
             ],
         ),
-        out_shape=jax.ShapeDtypeStruct((cells * cap, width), jnp.float32),
+        out_shape=jax.ShapeDtypeStruct(feats.shape, jnp.float32),
+        input_output_aliases={8: 0} if args else {},
         cost_estimate=pl.CostEstimate(
             flops=8 * cells * cap * cap * count * width * kinds,
             transcendentals=0,
             bytes_accessed=8 * cells * cap * width,
         ),
         name="near",
-    )(places, scales, rows, left, masked, right, feats, mix)
-
-
-def backward_body(has_acc, has_came, *refs):
-    trig, filts, rest = refs[:4], refs[4:6], list(refs[6:])
+    )(places, scales, rows, left, masked, right, feats, mix, *args)
+
+
+def backward_body(parts, has_acc, has_came, *refs):
+    refs = list(refs)
+    trig, filts, rest = refs[: 2 * parts], refs[2 * parts : 3 * parts], refs[3 * parts :]
     contract = (((0,), (0,)), ((), ()))
     total = rest.pop(0)[...] if has_acc else None
     if has_came:
         total = total + rest.pop(0)[...].astype(jnp.float32)
-    for half in range(2):
+    for part in range(parts):
         for which in range(2):
             term = lax.dot_general(
-                trig[2 * half + which][...],
-                filts[half][which],
+                trig[2 * part + which][...],
+                filts[part][which],
                 contract,
                 preferred_element_type=jnp.float32,
             )
@@ -223,36 +228,40 @@
         ref[...] = total.astype(ref.dtype)
 
 
-def backward(trig, filts, first, count, tile, acc, came, dtypes):
-    rows = trig[0].shape[0]
-    width = filts[0].shape[2]
+def backward(chunks, first, count, tile, acc, came, dtypes):
+    parts = [part for chunk in chunks for part in chunk]
+    width = parts[0][2].shape[2]
     at = first // tile
     args, specs = [], []
     for array in (acc, came):
         if array is not None:
             array, offset = array
             args.append(array)
-            specs.append(pl.BlockSpec((tile, width), lambda i, offset=offset: (i + offset, 0)))
+            specs.append(pl.BlockSpec((tile, width), lambda i, offset=offset // tile: (i + offset, 0)))
+    trig = [array for cos, sin, _ in parts for array in (cos, sin)]
+    filts = [filt for _, _, filt in parts]
+    rows = sum(cos.shape[0] for cos, _, _ in parts)
     return pl.pallas_call(
-        functools.partial(backward_body, acc is not None, came is not None),
+        functools.partial(backward_body, len(parts), acc is not None, came is not None),
         grid=(count // tile,),
-        in_specs=[pl.BlockSpec((rows, tile), lambda i: (0, i + at))] * 4
-        + [pl.BlockSpec(filts[0].shape, lambda i: (0, 0, 0))] * 2
+        in_specs=[pl.BlockSpec((array.shape[0], tile), lambda i: (0, i + at)) for array in trig]
+        + [pl.BlockSpec(filt.shape, lambda i: (0, 0, 0)) for filt in filts]
         + specs,
         out_specs=[pl.BlockSpec((tile, width), lambda i: (i, 0))] * len(dtypes),
         out_shape=[jax.ShapeDtypeStruct((count, width), dtype) for dtype in dtypes],
         cost_estimate=pl.CostEstimate(
-            flops=16 * rows * count * width,
+            flops=8 * rows * count * width,
             transcendentals=0,
-            bytes_accessed=8 * rows * count + 8 * count * width,
+            bytes_accessed=4 * rows * count + 8 * count * width,
         ),
         name="messages",
     )(*trig, *filts, *args)
 
 
-def mlp_body(side, own_ref, other_ref, gain_ref, in0_ref, in1_ref, out0_ref, out1_ref, *refs):
+def mlp_body(side, own_ref, other_ref, gain_ref, in_ref, out_ref, both_ref, *refs):
     result_ref = refs[-1]
     width = own_ref.shape[1]
+    hidden_count = in_ref.shape[1]
     mine = side[0]
     own = own_ref[...]
     own_wide = own.astype(jnp.bfloat16).astype(jnp.float32)
@@ -267,14 +276,19 @@
     at_own = pl.ds(pl.multiple_of(mine * width, width), width)
     at_other = pl.ds(pl.multiple_of((1 - mine) * width, width), width)
     total = own
-    for in_ref, out_ref in ((in0_ref, out0_ref), (in1_ref, out1_ref)):
-        value = jnp.dot(normed_own, in_ref[at_own, :], preferred_element_type=jnp.float32)
+    hidden_columns = slice(0, hidden_count)
+    halves = (
+        (in_ref.at[:, :], out_ref.at[:, :]),
+        (both_ref.at[:, hidden_columns], both_ref.at[:, hidden_count:]),
+    )
+    for in_half, out_half in halves:
+        value = jnp.dot(normed_own, in_half[at_own, :], preferred_element_type=jnp.float32)
         value = value + jnp.dot(
-            normed_other, in_ref[at_other, :], preferred_element_type=jnp.float32
+            normed_other, in_half[at_other, :], preferred_element_type=jnp.float32
         )
         half = jnp.float32(0.5) * value
         hidden = (half * jnp.tanh(half) + half).astype(jnp.bfloat16)
-        total = total + jnp.dot(hidden, out_ref[...], preferred_element_type=jnp.float32)
+        total = total + jnp.dot(hidden, out_half[...], preferred_element_type=jnp.float32)
     result_ref[...] = total.astype(jnp.bfloat16)
 
 
@@ -297,7 +311,7 @@
             out_specs=pl.BlockSpec((rows, width), lambda i, *_: (offset, 0)),
         ),
         out_shape=jax.ShapeDtypeStruct((total_rows, width), jnp.bfloat16),
-        input_output_aliases={8: 0} if args else {},
+        input_output_aliases={7: 0} if args else {},
         cost_estimate=pl.CostEstimate(
             flops=2 * rows * width * weights[0].shape[1] * 12,
             transcendentals=0,
@@ -348,16 +362,17 @@
     wave_rows = wavevectors.shape[1]
     all_waves = 2 * wave_rows
     own_waves = wave_rows // 2
-    chunk_rows = own_waves // CHUNKS
-    block_rows = chunk_rows // group
     length = jnp.float32(devices * cell_count)
     place = lax.axis_index("cells").astype(jnp.int32)
     side = lax.axis_index("waves").astype(jnp.int32)
     core = place & core_bit
 
-    live = (jnp.arange(capacity, dtype=jnp.int32)[None, :] < occupancy[:, None]).reshape(atom_rows, 1)
-    masked = jnp.where(live, features, jnp.zeros_like(features))
-    atoms = jnp.pad(positions, ((0, 5), (0, 0)))
+    live = jnp.arange(capacity, dtype=jnp.int32)[None, :, None] < occupancy[:, None, None]
+    masked = jnp.where(live, features.reshape(cell_count, capacity, width), jnp.bfloat16(0)).reshape(
+        atom_rows, width
+    )
+    filled = jnp.pad(occupancy.astype(jnp.float32)[None, :], ((0, 4), (0, atom_rows - cell_count)))
+    atoms = jnp.concatenate([positions, filled], axis=0)
 
     pair_feats = (masked, across(masked, core_bit))
     pair_atoms = (atoms, across(atoms, core_bit))
@@ -368,11 +383,7 @@
     places_of_waves = jnp.stack([reverse, core * own_waves])
 
     def wave_operand(waves):
-        padded = jnp.pad(waves * jnp.float32(1.0 / (2.0 * math.pi)), ((0, 5), (0, 0)))
-        high = lax.reduce_precision(padded, 8, 7)
-        middle = lax.reduce_precision(padded - high, 8, 7)
-        low = padded - high - middle
-        return jnp.concatenate([high, high, middle, high, low, middle], axis=0).T.astype(jnp.bfloat16)
+        return jnp.pad(waves * jnp.float32(1.0 / (2.0 * math.pi)), ((0, 5), (0, 0))).T
 
     other_waves = swap(wavevectors)
 
@@ -383,51 +394,73 @@
     right_feats = lax.ppermute(masked[:edge], "cells", to_left)
     left_pos = lax.ppermute(positions[:, atom_rows - edge :], "cells", to_right)
     right_pos = lax.ppermute(positions[:, :edge], "cells", to_left)
-    count = jnp.full((8, 128), jnp.sum(occupancy).astype(jnp.float32))
-    for bit in bits:
+    count = jnp.sum(filled[0, :cell_count] + pair_atoms[1][3, :cell_count])
+    count = jnp.full((8, 128), count)
+    for bit in ring_bits:
         count = count + across(count, bit)
     count = count[0:1, 0:1]
 
-    def filter_part(chunk, whose):
-        row = core * own_waves + chunk * chunk_rows + reverse * block_rows
-        return lax.dynamic_slice(filters, (row, whose * width), (block_rows, width))
-
-    own_filters = [filter_part(chunk, side) for chunk in range(CHUNKS)]
-    sent_filters = jnp.stack([filter_part(chunk, 1 - side) for chunk in range(CHUNKS)])
-    other_filters = swap(sent_filters)
-
-    in_other = swap(in_weight)
+    def filter_part(start, rows, whose):
+        row = core * own_waves + start + reverse * (rows // group)
+        return lax.dynamic_slice(filters, (row, whose * width), (rows // group, width))
+
+    unit = 32 * group
+    splits = []
+    for shares in SHARES:
+        begin, pieces_of_half = 0, []
+        for share in shares:
+            rows_of = max(unit, int(own_waves * share) // unit * unit)
+            rows_of = min(rows_of, own_waves - begin)
+            if rows_of > 0:
+                pieces_of_half.append((begin, rows_of))
+            begin += rows_of
+        splits.append(pieces_of_half)
+    own_filters = [filter_part(start, rows, side) for start, rows in splits[0]]
+    sent_filters = jnp.concatenate(
+        [filter_part(start, rows, 1 - side) for start, rows in splits[1]], axis=0
+    )
+    came_filters = swap(sent_filters)
+    other_filters = [
+        came_filters[start // group : (start + rows) // group] for start, rows in splits[1]
+    ]
+
     hidden_rows = out_weight.shape[0]
     out_own = lax.dynamic_slice(out_weight, (0, side * width), (hidden_rows, width))
-    out_other = swap(lax.dynamic_slice(out_weight, (0, (1 - side) * width), (hidden_rows, width)))
+    out_sent = lax.dynamic_slice(out_weight, (0, (1 - side) * width), (hidden_rows, width))
+    both = swap(jnp.concatenate([in_weight, out_sent], axis=1))
 
     factor = lax.rsqrt(count) * jnp.float32(1.0 / math.sqrt(all_waves))
-
-    trig, totals = [], []
-    number = 0
-    for waves, rows_of_filter in ((wavevectors, own_filters), (other_waves, other_filters)):
+    factors = jnp.stack(
+        [factor * jnp.float32(WHOLE_COS**-2), factor * jnp.float32(WHOLE_SIN**-2)]
+    )
+
+    chunks = []
+    for waves, pieces_of_half, filter_rows in (
+        (wavevectors, splits[0], own_filters),
+        (other_waves, splits[1], other_filters),
+    ):
         operand = wave_operand(waves)
-        for chunk in range(CHUNKS):
-            half = chunk_rows // 2
+        for (start, rows_of), rows_of_filter in zip(pieces_of_half, filter_rows):
+            number = len(chunks)
+            scaled = lax.optimization_barrier(rows_of_filter[None] * factors)
+            half = rows_of // 2
             cos_far, sin_far, send = forward(
-                places_of_waves, operand, pair_atoms, pair_feats, chunk * chunk_rows, half, half, block_rows, jnp.bfloat16
+                places_of_waves, operand, pair_atoms, pair_feats, start, half, half, rows_of // group, jnp.bfloat16
             )
             cos_near, sin_near, keep = forward(
-                places_of_waves, operand, pair_atoms, pair_feats, chunk * chunk_rows, 0, half, block_rows, jnp.float32
+                places_of_waves, operand, pair_atoms, pair_feats, start, 0, half, rows_of // group, jnp.float32
             )
-            trig.append((cos_near, sin_near, cos_far, sin_far))
             for index, bit in enumerate(ring_bits):
                 summed = keep + across(send, bit).astype(jnp.float32)
                 if index + 1 < len(ring_bits):
                     half = summed.shape[1] // 2
                     keep, send = summed[:, :half], summed[:, half:].astype(jnp.bfloat16)
-            filt = (summed * rows_of_filter[chunk][None] * factor[None]).astype(jnp.bfloat16)
+            filt = (summed * scaled).astype(jnp.bfloat16)
             for index, bit in enumerate(reversed(ring_bits)):
                 came = across(filt, bit)
                 if index + 1 < len(ring_bits):
                     filt = jnp.concatenate([filt, came], axis=1)
-            totals.append((filt, came))
-            number += 1
+            chunks.append([(cos_near, sin_near, filt), (cos_far, sin_far, came)])
 
     shift_left = jnp.where(place == 0, length, 0.0).astype(jnp.float32)
     shift_right = jnp.where(place == devices - 1, length, 0.0).astype(jnp.float32)
@@ -440,66 +473,47 @@
     mix = lax.dynamic_slice(mixing, (0, side * width), (mixing.shape[0], width))
     half_cells = cell_count // 2
     half_rows = atom_rows // 2
-    own = []
+    mine = None
     for half in range(2):
-        own.append(
-            near_part(
-                half * half_cells,
-                half_cells,
-                places,
-                falloffs * jnp.float32(-1.0 / math.log(2.0)),
-                rows,
-                left_feats.reshape(HW, capacity, width),
-                masked.reshape(cell_count, capacity, width),
-                right_feats.reshape(HW, capacity, width),
-                features,
-                mix,
-            )
+        mine = near_part(
+            half * half_cells,
+            half_cells,
+            places,
+            falloffs * jnp.float32(-1.0 / math.log(2.0)),
+            rows,
+            left_feats.reshape(HW, capacity, width),
+            masked.reshape(cell_count, capacity, width),
+            right_feats.reshape(HW, capacity, width),
+            features,
+            mix,
+            mine,
         )
 
     f32, bf16 = jnp.float32, jnp.bfloat16
     other = None
-    tile = half_rows
-    mine = None
-    for number in range(len(trig) - 1):
+    at = 0
+    for number, size in enumerate(GROUPS):
+        taken = chunks[at : at + size] if number + 1 < len(GROUPS) else chunks[at:-1]
+        at += size
+        if not taken:
+            continue
         (other,) = backward(
-            trig[number], totals[number], atom_rows, atom_rows, tile,
-            None if other is None else (other, 0), None, (f32,),
+            taken, atom_rows, atom_rows, half_rows, None if other is None else (other, 0), None, (f32,)
         )
-        if mine is None:
-            mine = [
-                backward(
-                    trig[number], totals[number], half * half_rows, half_rows, half_rows,
-                    (own[half], 0), None, (f32,),
-                )[0]
-                for half in range(2)
-            ]
-            mine = [(mine[0], 0), (mine[1], 0)]
-        else:
-            mine = [
-                (
-                    backward(
-                        trig[number], totals[number], half * half_rows, half_rows, half_rows,
-                        mine[half], None, (f32,),
-                    )[0],
-                    0,
-                )
-                for half in range(2)
-            ]
+        (mine,) = backward(taken, 0, atom_rows, half_rows, (mine, 0), None, (f32,))
+    last = chunks[-1:]
     came = []
     for half in range(2):
         (send,) = backward(
-            trig[-1], totals[-1], atom_rows + half * half_rows, half_rows, half_rows,
-            (other, half), None, (bf16,),
+            last, atom_rows + half * half_rows, half_rows, half_rows // 2, (other, half * half_rows), None, (bf16,)
         )
         came.append(across(send, core_bit))
     gains = norm_gain.reshape(2, width)
-    weights = (in_weight, in_other, out_own, out_other)
+    weights = (in_weight, out_own, both)
     result = None
     for half in range(2):
         part, send = backward(
-            trig[-1], totals[-1], half * half_rows, half_rows, half_rows,
-            mine[half], (came[half], 0), (f32, bf16),
+            last, half * half_rows, half_rows, half_rows // 2, (mine, half * half_rows), (came[half], 0), (f32, bf16)
         )
         pieces = 1 if half == 0 else 2
         piece_rows = half_rows // pieces

time: 248 us -> 222 us (0.90); the launches traced: 244 us -> 221 us
  Pallas kernels: 137 us -> 102 us
  other arithmetic: 6.98 us -> 14.7 us
  local copies, waits for them, and re-layouts: 14.2 us -> 19.8 us
  starting transfers between devices: 34.8 us -> 29.6 us
  waiting for transfers between devices: 48.1 us -> 53.3 us
    pallas_call x13 -> x6, Pallas kernels: 52.5 us -> 32.5 us  [backward(): pl.pallas_call(functools.partial(backward_body, len(parts), acc is not No...]
    pallas_call x8 -> x4, Pallas kernels: 61.5 us -> 46.5 us  [forward(): pl.pallas_call(functools.partial(forward_body, start, position // block_r...]
    ppermute x32 -> x19, starting transfers between devices: 19.9 us -> 13.4 us  [across(): return lax.ppermute(value, 'cells', [(i, i ^ bit) for i in range(count)])]
    ppermute x7 -> x6, waiting for transfers between devices: 1.41 us -> 5.85 us  [swap(): return lax.ppermute(value, 'waves', [(0, 1), (1, 0)])]
    ppermute x1, starting transfers between devices: 0.01 us -> 4.42 us  [shards(): right_feats = lax.ppermute(masked[:edge], 'cells', to_left)]
    ppermute x32 -> x19, waiting for transfers between devices: 43.1 us -> 47.5 us  [across(): return lax.ppermute(value, 'cells', [(i, i ^ bit) for i in range(count)])]
    ppermute x1, waiting for transfers between devices: 3.54 us -> 0.01 us  [shards(): left_feats = lax.ppermute(masked[atom_rows - edge:], 'cells', to_right)]
    unnamed x65 -> x48, local copies, waits for them, and re-layouts: 6.69 us -> 9.58 us
  transfers between devices with their start and end apart: 43 -> 29, of which waited for: 23 -> 13; matrix products, arithmetic and copies ran while one was open for 6% -> 12% of each run, Pallas kernels for 55% -> 45%
where the time goes in v3:
time: 222 us; the launch traced here: 221 us
  Pallas kernels  102 us (46%)
  waiting for transfers between devices  53.3 us (24%)
  starting transfers between devices  29.6 us (13%)
  local copies, waits for them, and re-layouts  19.8 us (9%)
  other arithmetic  14.7 us (7%)
    ppermute x19, waiting for transfers between devices, across(): return lax.ppermute(value, 'cells', [(i, i ^ bit) for i in range(count)])  47.5 us
    pallas_call x4, Pallas kernels, forward(): pl.pallas_call(functools.partial(forward_body, start, position // block_r...  46.5 us
    pallas_call x6, Pallas kernels, backward(): pl.pallas_call(functools.partial(backward_body, len(parts), acc is not No...  32.5 us
    ppermute x19, starting transfers between devices, across(): return lax.ppermute(value, 'cells', [(i, i ^ bit) for i in range(count)])  13.4 us
    pallas_call x3, Pallas kernels, mlp(): pl.pallas_call(mlp_body, grid_spec=pltpu.PrefetchScalarGridSpec(num_scala...  12 us
    pallas_call x2, Pallas kernels, near_part(): pl.pallas_call(functools.partial(near_body, base), grid_spec=pltpu.Prefet...  11.4 us
    unnamed x48, local copies, waits for them, and re-layouts  9.58 us
    ppermute x6, starting transfers between devices, swap(): return lax.ppermute(value, 'waves', [(0, 1), (1, 0)])  6.27 us
  transfers between devices with their start and end apart: 29, of which 13 were waited for; matrix products, arithmetic and copies ran while one was open for 12% of the time, Pallas kernels for 45%

profile of v3, /device:TPU:0, one launch (start us, length us, event | category | flops | bytes accessed | tf_op | source)
XLA Modules:
  0.0 220.8 jit_solution(1022147444389328230)
XLA Ops:
  0.0 0.8 fusion.11
  1.3 5.0 %collective-permute-start.20 = (f32[3,256]{1,0:T(4,128)S(1)}, f32[3,256]{1,0:T(4,128)S(1)}, u32[]{:S(2)}, u32[]{:S(2)}) collective-permute-start(f32[3,256]{1,0:T(4,128)S(1)} %get-tuple-element.46), channel_id=1, source_target_pairs={{2,0},{4,2},{6,4},{8,6},{10,8},{12,10},{14,12},{16,14},{18,16},{20... | collective-permute-start | bytes 9224 | tf_op jit(solution)/shard_map/ppermute | solution.py:396
  6.3 1.9 collective-permute-start
  8.2 0.7 convert_bitcast_fusion
  8.9 1.4 select_maximum_fusion.2.own_pos
  10.3 1.0 fusion.8
  11.4 0.7 iota_compare_fusion.2
  12.1 1.1 copy.27
  13.3 1.2 broadcast_multiply_fusion.4.scales
  15.1 0.8 copy.29
  15.8 1.8 constant_dynamic-slice_fusion
  17.6 1.5 broadcast_select_fusion.1.masked_ref
  19.2 0.9 copy-done.7
  20.2 1.2 broadcast_select_fusion.own_ref
  21.5 1.0 pad_bitcast_fusion.waves_ref
  22.5 0.7 broadcast_add_fusion.places
  23.8 0.7 pad_add_fusion.places
  24.4 1.9 collective-permute-start.25
  26.4 1.3 fusion.6
  28.5 1.1 copy.24
  29.6 2.4 %collective-permute-done.7 = f32[8,128]{1,0:T(8,128)S(1)} collective-permute-done((f32[8,128]{1,0:T(8,128)S(1)}, f32[8,128]{1,0:T(8,128)S(1)}, u32[]{:S(2)}, u32[]{:S(2)}) %collective-permute-start.7) | collective-permute-done | bytes 4128 | tf_op jit(solution)/shard_map/ppermute | solution.py:339
  32.8 3.5 %collective-permute-done.8 = f32[8,128]{1,0:T(8,128)S(1)} collective-permute-done((f32[8,128]{1,0:T(8,128)S(1)}, f32[8,128]{1,0:T(8,128)S(1)}, u32[]{:S(2)}, u32[]{:S(2)}) %collective-permute-start.8) | collective-permute-done | bytes 4128 | tf_op jit(solution)/shard_map/ppermute | solution.py:339
  37.0 0.9 collective-permute-start.9
  37.8 1.0 pad_bitcast_fusion.1.waves_ref
  38.9 2.7 %collective-permute-done.9 = f32[8,128]{1,0:T(8,128)S(1)} collective-permute-done((f32[8,128]{1,0:T(8,128)S(1)}, f32[8,128]{1,0:T(8,128)S(1)}, u32[]{:S(2)}, u32[]{:S(2)}) %collective-permute-start.9) | collective-permute-done | bytes 4128 | tf_op jit(solution)/shard_map/ppermute | solution.py:339
  43.3 11.6 %structure.7 = (bf16[512,4096]{1,0:T(8,128)(2,1)}, bf16[512,4096]{1,0:T(8,128)(2,1)}, bf16[2,512,256]{2,1,0:T(8,128)(2,1)}) custom-call(s32[2]{0:T(128)} %pad_add_fusion.places, f32[2048,8]{1,0:T(8,128)} %pad_bitcast_fusion.waves_ref, f32[8,2048]{1,0:T(8,128)} %select_maximum_fusion.2.own_pos, f32[8,2048]{1,0:T(8,128)} %collective-permute-done.1.other_pos, ...), custom_call_target="tpu_custom_call" | custom-call | flops 4831838208 | bytes 8388608 | tf_op jit(solution)/shard_map/structure/pallas_call | solution.py:101
  54.9 11.5 %structure.5 = (bf16[512,4096]{1,0:T(8,128)(2,1)}, bf16[512,4096]{1,0:T(8,128)(2,1)}, bf16[2,512,256]{2,1,0:T(8,128)(2,1)}) custom-call(s32[2]{0:T(128)} %pad_add_fusion.places, f32[2048,8]{1,0:T(8,128)} %pad_bitcast_fusion.1.waves_ref, f32[8,2048]{1,0:T(8,128)} %select_maximum_fusion.2.own_pos, f32[8,2048]{1,0:T(8,128)} %collective-permute-done.1.other_pos, ...), custom_call_target="tpu_custom_call" | custom-call | flops 4831838208 | bytes 8388608 | tf_op jit(solution)/shard_map/structure/pallas_call | solution.py:101
  66.4 2.0 collective-permute-start.3
  68.4 11.5 %structure.6 = (bf16[512,4096]{1,0:T(8,128)(2,1)}, bf16[512,4096]{1,0:T(8,128)(2,1)}, f32[2,512,256]{2,1,0:T(8,128)}) custom-call(s32[2]{0:T(128)} %pad_add_fusion.places, f32[2048,8]{1,0:T(8,128)} %pad_bitcast_fusion.waves_ref, f32[8,2048]{1,0:T(8,128)} %select_maximum_fusion.2.own_pos, f32[8,2048]{1,0:T(8,128)} %collective-permute-done.1.other_pos, ...), custom_call_target="tpu_custom_call" | custom-call | flops 4831838208 | bytes 8388608 | tf_op jit(solution)/shard_map/structure/pallas_call | solution.py:101
  79.9 11.9 %structure.4 = (bf16[512,4096]{1,0:T(8,128)(2,1)}, bf16[512,4096]{1,0:T(8,128)(2,1)}, f32[2,512,256]{2,1,0:T(8,128)}) custom-call(s32[2]{0:T(128)} %pad_add_fusion.places, f32[2048,8]{1,0:T(8,128)} %pad_bitcast_fusion.1.waves_ref, f32[8,2048]{1,0:T(8,128)} %select_maximum_fusion.2.own_pos, f32[8,2048]{1,0:T(8,128)} %collective-permute-done.1.other_pos, ...), custom_call_target="tpu_custom_call" | custom-call | flops 4831838208 | bytes 8388608 | tf_op jit(solution)/shard_map/structure/pallas_call | solution.py:101
  92.2 1.3 convert_add_fusion.1
  93.6 2.1 collective-permute-start.4
  95.7 5.6 %collective-permute-done.14 = bf16[2,256,256]{2,1,0:T(8,128)(2,1)S(1)} collective-permute-done((bf16[2,256,256]{2,1,0:T(8,128)(2,1)S(1)}, bf16[2,256,256]{2,1,0:T(8,128)(2,1)S(1)}, u32[]{:S(2)}, u32[]{:S(2)}) %collective-permute-start.14) | collective-permute-done | bytes 262176 | tf_op jit(solution)/shard_map/ppermute | solution.py:339
  101.3 4.4 %collective-permute-start.22 = (bf16[256,256]{1,0:T(8,128)(2,1)S(1)}, bf16[256,256]{1,0:T(8,128)(2,1)S(1)}, u32[]{:S(2)}, u32[]{:S(2)}) collective-permute-start(bf16[256,256]{1,0:T(8,128)(2,1)S(1)} %bitcast.37), channel_id=1, source_target_pairs={{2,0},{4,2},{6,4},{8,6},{10,8},{12,10},{14,12},{16,14},{18,16},{20... | collective-permute-start | bytes 393224 | tf_op jit(solution)/shard_map/ppermute | solution.py:394
  106.1 1.4 collective-permute-start.15
  107.6 6.9 %collective-permute-done.15 = bf16[2,128,256]{2,1,0:T(8,128)(2,1)S(1)} collective-permute-done((bf16[2,128,256]{2,1,0:T(8,128)(2,1)S(1)}, bf16[2,128,256]{2,1,0:T(8,128)(2,1)S(1)}, u32[]{:S(2)}, u32[]{:S(2)}) %collective-permute-start.15) | collective-permute-done | bytes 131104 | tf_op jit(solution)/shard_map/ppermute | solution.py:339
  114.6 9.8 %collective-permute-done.5 = bf16[2,128,256]{2,1,0:T(8,128)(2,1)S(1)} collective-permute-done((bf16[2,128,256]{2,1,0:T(8,128)(2,1)S(1)}, bf16[2,128,256]{2,1,0:T(8,128)(2,1)S(1)}, u32[]{:S(2)}, u32[]{:S(2)}) %collective-permute-start.5) | collective-permute-done | bytes 131104 | tf_op jit(solution)/shard_map/ppermute | solution.py:339
  124.4 7.2 %collective-permute-done.16 = bf16[2,128,256]{2,1,0:T(8,128)(2,1)S(1)} collective-permute-done((bf16[2,128,256]{2,1,0:T(8,128)(2,1)S(1)}, bf16[2,128,256]{2,1,0:T(8,128)(2,1)S(1)}, u32[]{:S(2)}, u32[]{:S(2)}) %collective-permute-start.16) | collective-permute-done | bytes 131104 | tf_op jit(solution)/shard_map/ppermute | solution.py:339
  131.6 3.1 %collective-permute-start.17 = (bf16[2,256,256]{2,1,0:T(8,128)(2,1)S(1)}, bf16[2,256,256]{2,1,0:T(8,128)(2,1)S(1)}, u32[]{:S(2)}, u32[]{:S(2)}) collective-permute-start(bf16[2,256,256]{2,1,0:T(8,128)(2,1)S(1)} %pad_maximum_fusion.4), channel_id=1, source_target_pairs={{0,8},{2,10},{4,12},{6,14},{8,0},{10,2},{12,4},{14,6},{16,24},{18,... | collective-permute-start | bytes 786440 | tf_op jit(solution)/shard_map/ppermute | solution.py:339
  135.5 3.3 %collective-permute-done.10 = bf16[2,128,256]{2,1,0:T(8,128)(2,1)S(1)} collective-permute-done((bf16[2,128,256]{2,1,0:T(8,128)(2,1)S(1)}, bf16[2,128,256]{2,1,0:T(8,128)(2,1)S(1)}, u32[]{:S(2)}, u32[]{:S(2)}) %collective-permute-start.10) | collective-permute-done | bytes 131104 | tf_op jit(solution)/shard_map/ppermute | solution.py:339
  139.1 4.1 %collective-permute-done.17 = bf16[2,256,256]{2,1,0:T(8,128)(2,1)S(1)} collective-permute-done((bf16[2,256,256]{2,1,0:T(8,128)(2,1)S(1)}, bf16[2,256,256]{2,1,0:T(8,128)(2,1)S(1)}, u32[]{:S(2)}, u32[]{:S(2)}) %collective-permute-start.17) | collective-permute-done | bytes 262176 | tf_op jit(solution)/shard_map/ppermute | solution.py:339
  143.3 2.6 %collective-permute-start.18 = (bf16[2,512,256]{2,1,0:T(8,128)(2,1)S(1)}, bf16[2,512,256]{2,1,0:T(8,128)(2,1)S(1)}, u32[]{:S(2)}, u32[]{:S(2)}) collective-permute-start(bf16[2,512,256]{2,1,0:T(8,128)(2,1)S(1)} %pad_maximum_fusion.2.refs_4_), channel_id=1, source_target_pairs={{0,4},{2,6},{4,0},{6,2},{8,12},{10,14},{12,8},{14,10},{16,20},{18,... | collective-permute-start | bytes 1572872 | tf_op jit(solution)/shard_map/ppermute | solution.py:339
  147.1 5.7 %near.2.refs_0_ = f32[2048,256]{1,0:T(8,128)} custom-call(s32[16,3]{1,0:T(8,128)} %broadcast_add_fusion.places, f32[4]{0:T(128)} %broadcast_multiply_fusion.4.scales, f32[20,8,128]{2,1,0:T(8,128)} %fusion.4.row_ref, bf16[2,128,256]{2,1,0:T(8,128)(2,1)} %bitcast.39, bf16[16,128,256]{2,1,0:T(8,128)(2,1)} %copy-done.7, bf16[2,128,256]{2,1,0:T(8,128)(2,1)} %bitcast.41, ...), custom_call_target="tpu_custom_call" | custom-call | flops 3221225472 | bytes 2097152 | tf_op jit(solution)/shard_map/near/pallas_call | solution.py:179
  153.1 5.7 %near.3.refs_6_ = f32[2048,256]{1,0:T(8,128)} custom-call(s32[16,3]{1,0:T(8,128)} %broadcast_add_fusion.places, f32[4]{0:T(128)} %broadcast_multiply_fusion.4.scales, f32[20,8,128]{2,1,0:T(8,128)} %fusion.4.row_ref, bf16[2,128,256]{2,1,0:T(8,128)(2,1)} %bitcast.40, bf16[16,128,256]{2,1,0:T(8,128)(2,1)} %copy-done.7, ...), custom_call_target="tpu_custom_call", output_to_operand_aliasing={{}: (8, {})} | custom-call | flops 3221225472 | bytes 2097152 | tf_op jit(solution)/shard_map/near/pallas_call | solution.py:179
  158.8 0.8 copy-done.6
  159.6 6.5 %messages.7.refs_6_ = f32[2048,256]{1,0:T(8,128)} custom-call(bf16[512,4096]{1,0:T(8,128)(2,1)} %get-tuple-element.27.refs_0_, bf16[512,4096]{1,0:T(8,128)(2,1)} %get-tuple-element.28.refs_1_, bf16[512,4096]{1,0:T(8,128)(2,1)} %get-tuple-element.29.refs_2_, bf16[512,4096]{1,0:T(8,128)(2,1)} %get-tuple-element.30.refs_3_, bf16[2,512,256]{2,1,0:T(8,128)(2,1)} %copy-done.4, ...), custom_call_target="tpu_custom_call" | custom-call | flops 4294967296 | bytes 12582912 | tf_op jit(solution)/shard_map/messages/pallas_call | solution.py:244
  166.1 1.9 collective-permute-done.12.refs_5_
  168.0 0.8 copy-done.3
  168.7 4.6 %messages.10 = bf16[1024,256]{1,0:T(8,128)(2,1)} custom-call(bf16[512,4096]{1,0:T(8,128)(2,1)} %get-tuple-element.21.refs_0_, bf16[512,4096]{1,0:T(8,128)(2,1)} %get-tuple-element.22.refs_1_, bf16[512,4096]{1,0:T(8,128)(2,1)} %get-tuple-element.23.refs_2_, bf16[512,4096]{1,0:T(8,128)(2,1)} %get-tuple-element.24.refs_3_, bf16[2,512,256]{2,1,0:T(8,128)(2,1)} %copy-done.2, ...), custom_call_target="tpu_custom_call" | custom-call | flops 2147483648 | bytes 6291456 | tf_op jit(solution)/shard_map/messages/pallas_call | solution.py:244
  173.3 4.6 %messages.8 = bf16[1024,256]{1,0:T(8,128)(2,1)} custom-call(bf16[512,4096]{1,0:T(8,128)(2,1)} %get-tuple-element.21.refs_0_, bf16[512,4096]{1,0:T(8,128)(2,1)} %get-tuple-element.22.refs_1_, bf16[512,4096]{1,0:T(8,128)(2,1)} %get-tuple-element.23.refs_2_, bf16[512,4096]{1,0:T(8,128)(2,1)} %get-tuple-element.24.refs_3_, bf16[2,512,256]{2,1,0:T(8,128)(2,1)} %copy-done.2, ...), custom_call_target="tpu_custom_call" | custom-call | flops 2147483648 | bytes 6291456 | tf_op jit(solution)/shard_map/messages/pallas_call | solution.py:244
  178.4 7.0 %messages.6.refs_6_ = f32[2048,256]{1,0:T(8,128)} custom-call(bf16[512,4096]{1,0:T(8,128)(2,1)} %get-tuple-element.27.refs_0_, bf16[512,4096]{1,0:T(8,128)(2,1)} %get-tuple-element.28.refs_1_, bf16[512,4096]{1,0:T(8,128)(2,1)} %get-tuple-element.29.refs_2_, bf16[512,4096]{1,0:T(8,128)(2,1)} %get-tuple-element.30.refs_3_, bf16[2,512,256]{2,1,0:T(8,128)(2,1)} %copy-done.4, ...), custom_call_target="tpu_custom_call" | custom-call | flops 4294967296 | bytes 12582912 | tf_op jit(solution)/shard_map/messages/pallas_call | solution.py:244
  185.5 0.8 copy-done.11
  186.3 4.9 %messages.11 = (f32[1024,256]{1,0:T(8,128)}, bf16[1024,256]{1,0:T(8,128)(2,1)}) custom-call(bf16[512,4096]{1,0:T(8,128)(2,1)} %get-tuple-element.21.refs_0_, bf16[512,4096]{1,0:T(8,128)(2,1)} %get-tuple-element.22.refs_1_, bf16[512,4096]{1,0:T(8,128)(2,1)} %get-tuple-element.23.refs_2_, bf16[512,4096]{1,0:T(8,128)(2,1)} %get-tuple-element.24.refs_3_, ...), custom_call_target="tpu_custom_call" | custom-call | flops 2147483648 | bytes 6291456 | tf_op jit(solution)/shard_map/messages/pallas_call | solution.py:244
  191.9 0.8 copy-done.10
  192.7 4.9 %messages.9 = (f32[1024,256]{1,0:T(8,128)}, bf16[1024,256]{1,0:T(8,128)(2,1)}) custom-call(bf16[512,4096]{1,0:T(8,128)(2,1)} %get-tuple-element.21.refs_0_, bf16[512,4096]{1,0:T(8,128)(2,1)} %get-tuple-element.22.refs_1_, bf16[512,4096]{1,0:T(8,128)(2,1)} %get-tuple-element.23.refs_2_, bf16[512,4096]{1,0:T(8,128)(2,1)} %get-tuple-element.24.refs_3_, ...), custom_call_target="tpu_custom_call" | custom-call | flops 2147483648 | bytes 6291456 | tf_op jit(solution)/shard_map/messages/pallas_call | solution.py:244
  197.6 1.1 fusion.10
  198.6 2.0 collective-permute-start.26
  200.7 5.5 %collective-permute-done.28.other_ref = bf16[1024,256]{1,0:T(8,128)(2,1)S(1)} collective-permute-done((bf16[1024,256]{1,0:T(8,128)(2,1)}, bf16[1024,256]{1,0:T(8,128)(2,1)S(1)}, u32[]{:S(2)}, u32[]{:S(2)}) %collective-permute-start.28) | collective-permute-done | bytes 524320 | tf_op jit(solution)/shard_map/ppermute | solution.py:334
  206.2 0.8 copy-done.18
  207.0 4.8 %mlp.3.refs_0_ = bf16[2048,256]{1,0:T(8,128)(2,1)} custom-call(s32[1]{0:T(128)} %bitcast.side, f32[1024,256]{1,0:T(8,128)} %get-tuple-element.35.own_ref, bf16[1024,256]{1,0:T(8,128)(2,1)} %copy-done.18, f32[2,256]{1,0:T(2,128)} %reshape.67.gain_ref, bf16[512,512]{1,0:T(8,128)(2,1)} %in_ref.5, bf16[512,256]{1,0:T(8,128)(2,1)} %get-tuple-element.44.out_ref, ...), custom_call_target="tpu_custom_call" | custom-call | flops 3221225472 | bytes 2097152 | tf_op jit(solution)/shard_map/mlp/pallas_call | solution.py:299
  211.8 0.7 copy-done.20
  212.6 3.6 %mlp.4.refs_0_ = bf16[2048,256]{1,0:T(8,128)(2,1)} custom-call(s32[1]{0:T(128)} %bitcast.side, f32[1024,256]{1,0:T(8,128)} %get-tuple-element.33.own_ref, bf16[512,256]{1,0:T(8,128)(2,1)} %copy-done.20, f32[2,256]{1,0:T(2,128)} %reshape.67.gain_ref, bf16[512,512]{1,0:T(8,128)(2,1)} %in_ref.5, ...), custom_call_target="tpu_custom_call", output_to_operand_aliasing={{}: (7, {})} | custom-call | flops 1610612736 | bytes 1048576 | tf_op jit(solution)/shard_map/mlp/pallas_call | solution.py:299
  216.5 0.7 copy-done.19
  217.2 3.6 %mlp.5 = bf16[2048,256]{1,0:T(8,128)(2,1)} custom-call(s32[1]{0:T(128)} %bitcast.side, f32[1024,256]{1,0:T(8,128)} %get-tuple-element.33.own_ref, bf16[512,256]{1,0:T(8,128)(2,1)} %copy-done.19, f32[2,256]{1,0:T(2,128)} %reshape.67.gain_ref, bf16[512,512]{1,0:T(8,128)(2,1)} %in_ref.5, ...), custom_call_target="tpu_custom_call", output_to_operand_aliasing={{}: (7, {})} | custom-call | flops 1610612736 | bytes 1048576 | tf_op jit(solution)/shard_map/mlp/pallas_call | solution.py:299
  (105 shorter events, 10.8 us)
Async XLA Ops:
  0.0 14.5 %copy-start = (f32[4,512]{1,0:T(4,128)S(1)}, f32[4,512]{1,0:T(4,128)}, u32[]{:S(2)}) copy-start(f32[4,512]{1,0:T(4,128)} %param.19) | copy-start | bytes 24580
  0.0 20.2 %copy-start.5 = (bf16[2048,256]{1,0:T(8,128)(2,1)S(1)}, bf16[2048,256]{1,0:T(8,128)(2,1)}, u32[]{:S(2)}) copy-start(bf16[2048,256]{1,0:T(8,128)(2,1)} %feats_ref.3) | copy-start | bytes 3145732
  0.8 26.9 %collective-permute-start.19 = (f32[3,256]{1,0:T(4,128)S(1)}, f32[3,256]{1,0:T(4,128)S(1)}, u32[]{:S(2)}, u32[]{:S(2)}) collective-permute-start(f32[3,256]{1,0:T(4,128)S(1)} %get-tuple-element.45), channel_id=1, source_target_pairs={{0,2},{2,4},{4,6},{6,8},{8,10},{10,12},{12,14},{14,16},{16,18},{18... | collective-permute-start | bytes 9224 | tf_op jit(solution)/shard_map/ppermute | solution.py:395
  1.3 130.3 %collective-permute-start.20 = (f32[3,256]{1,0:T(4,128)S(1)}, f32[3,256]{1,0:T(4,128)S(1)}, u32[]{:S(2)}, u32[]{:S(2)}) collective-permute-start(f32[3,256]{1,0:T(4,128)S(1)} %get-tuple-element.46), channel_id=1, source_target_pairs={{2,0},{4,2},{6,4},{8,6},{10,8},{12,10},{14,12},{16,14},{18,16},{20... | collective-permute-start | bytes 9224 | tf_op jit(solution)/shard_map/ppermute | solution.py:396
  6.3 22.2 %collective-permute-start = (f32[3,2048]{1,0:T(4,128)}, f32[3,2048]{1,0:T(4,128)}, u32[]{:S(2)}, u32[]{:S(2)}) collective-permute-start(f32[3,2048]{1,0:T(4,128)} %param.16), channel_id=1, source_target_pairs={{0,1},{1,0},{2,3},{3,2},{4,5},{5,4},{6,7},{7,6},{8,9},{9,8},{10,11... | collective-permute-start | bytes 73736 | tf_op jit(solution)/shard_map/ppermute | solution.py:334
  10.3 14.2 %collective-permute-start.1 = (f32[8,2048]{1,0:T(8,128)}, f32[8,2048]{1,0:T(8,128)}, u32[]{:S(2)}, u32[]{:S(2)}) collective-permute-start(f32[8,2048]{1,0:T(8,128)} %select_maximum_fusion.2.own_pos), channel_id=1, source_target_pairs={{0,2},{2,0},{4,6},{6,4},{8,10},{10,8},{12,14},{14,12},{16,18},{18,... | collective-permute-start | bytes 196616 | tf_op jit(solution)/shard_map/ppermute | solution.py:339
  11.2 82.3 %collective-permute-start.6 = (f32[128,256]{1,0:T(8,128)S(1)}, f32[128,256]{1,0:T(8,128)S(1)}, u32[]{:S(2)}, u32[]{:S(2)}) collective-permute-start(f32[128,256]{1,0:T(8,128)S(1)} %get-tuple-element.38), channel_id=1, source_target_pairs={{0,1},{1,0},{2,3},{3,2},{4,5},{5,4},{6,7},{7,6},{8,9},{9,8},{10,11... | collective-permute-start | bytes 393224 | tf_op jit(solution)/shard_map/ppermute | solution.py:334
  17.6 5.6 %copy-start.9 = (bf16[512,512]{1,0:T(8,128)(2,1)S(1)}, bf16[512,512]{1,0:T(8,128)(2,1)}, u32[]{:S(2)}) copy-start(bf16[512,512]{1,0:T(8,128)(2,1)} %in_ref.5) | copy-start | bytes 1572868
  19.1 1.0 copy-start.7
  19.2 4.1 %copy-start.16 = (f32[3,1]{0,1:T(1,128)S(1)}, f32[3,1]{0,1:T(1,128)}, u32[]{:S(2)}) copy-start(f32[3,1]{0,1:T(1,128)} %constant.51.clone) | copy-start | bytes 40
  19.2 7.2 %copy-start.15 = (s32[16]{0:T(128)S(1)}, s32[16]{0:T(128)}, u32[]{:S(2)}) copy-start(s32[16]{0:T(128)} %param.14) | copy-start | bytes 196
  24.4 176.3 %collective-permute-start.25 = (bf16[512,768]{1,0:T(8,128)(2,1)S(1)}, bf16[512,768]{1,0:T(8,128)(2,1)}, u32[]{:S(2)}, u32[]{:S(2)}) collective-permute-start(bf16[512,768]{1,0:T(8,128)(2,1)S(1)} %pad_maximum_fusion), channel_id=1, source_target_pairs={{0,1},{1,0},{2,3},{3,2},{4,5},{5,4},{6,7},{7,6},{8,9},{9,8},{10,11... | collective-permute-start | bytes 2359304 | tf_op jit(solution)/shard_map/ppermute | solution.py:334
  28.3 3.7 %collective-permute-start.7 = (f32[8,128]{1,0:T(8,128)S(1)}, f32[8,128]{1,0:T(8,128)S(1)}, u32[]{:S(2)}, u32[]{:S(2)}) collective-permute-start(f32[8,128]{1,0:T(8,128)S(1)} %broadcast_in_dim.30), channel_id=1, source_target_pairs={{0,4},{2,6},{4,0},{6,2},{8,12},{10,14},{12,8},{14,10},{16,20},{18,... | collective-permute-start | bytes 12296 | tf_op jit(solution)/shard_map/ppermute | solution.py:339
  28.5 14.8 %collective-permute-start.2 = (bf16[2048,256]{1,0:T(8,128)(2,1)}, bf16[2048,256]{1,0:T(8,128)(2,1)}, u32[]{:S(2)}, u32[]{:S(2)}) collective-permute-start(bf16[2048,256]{1,0:T(8,128)(2,1)} %broadcast_select_fusion.own_ref), channel_id=1, source_target_pairs={{0,2},{2,0},{4,6},{6,4},{8,10},{10,8},{12,14},{14,12},{16,18},{18,... | collective-permute-start | bytes 3145736 | tf_op jit(solution)/shard_map/ppermute | solution.py:339
  32.7 3.7 %collective-permute-start.8 = (f32[8,128]{1,0:T(8,128)S(1)}, f32[8,128]{1,0:T(8,128)S(1)}, u32[]{:S(2)}, u32[]{:S(2)}) collective-permute-start(f32[8,128]{1,0:T(8,128)S(1)} %broadcast_add_fusion.2), channel_id=1, source_target_pairs={{0,8},{2,10},{4,12},{6,14},{8,0},{10,2},{12,4},{14,6},{16,24},{18,... | collective-permute-start | bytes 12296 | tf_op jit(solution)/shard_map/ppermute | solution.py:339
  37.0 4.6 %collective-permute-start.9 = (f32[8,128]{1,0:T(8,128)S(1)}, f32[8,128]{1,0:T(8,128)S(1)}, u32[]{:S(2)}, u32[]{:S(2)}) collective-permute-start(f32[8,128]{1,0:T(8,128)S(1)} %fusion.12), channel_id=1, source_target_pairs={{0,16},{2,18},{4,20},{6,22},{8,24},{10,26},{12,28},{14,30},{16,0},... | collective-permute-start | bytes 12296 | tf_op jit(solution)/shard_map/ppermute | solution.py:339
  54.9 37.0 %collective-permute-start.13 = (bf16[2,512,256]{2,1,0:T(8,128)(2,1)}, bf16[2,512,256]{2,1,0:T(8,128)(2,1)S(1)}, u32[]{:S(2)}, u32[]{:S(2)}) collective-permute-start(bf16[2,512,256]{2,1,0:T(8,128)(2,1)} %get-tuple-element.32), channel_id=1, source_target_pairs={{0,4},{2,6},{4,0},{6,2},{8,12},{10,14},{12,8},{14,10},{16,20},{18,... | collective-permute-start | bytes 1572872 | tf_op jit(solution)/shard_map/ppermute | solution.py:339
  66.4 25.7 %collective-permute-start.3 = (bf16[2,512,256]{2,1,0:T(8,128)(2,1)}, bf16[2,512,256]{2,1,0:T(8,128)(2,1)S(1)}, u32[]{:S(2)}, u32[]{:S(2)}) collective-permute-start(bf16[2,512,256]{2,1,0:T(8,128)(2,1)} %get-tuple-element.26), channel_id=1, source_target_pairs={{0,4},{2,6},{4,0},{6,2},{8,12},{10,14},{12,8},{14,10},{16,20},{18,... | collective-permute-start | bytes 1572872 | tf_op jit(solution)/shard_map/ppermute | solution.py:339
  79.9 12.0 %copy-start.8 = (f32[2,512,256]{2,1,0:T(8,128)S(1)}, f32[2,512,256]{2,1,0:T(8,128)}, u32[]{:S(2)}) copy-start(f32[2,512,256]{2,1,0:T(8,128)} %get-tuple-element.31) | copy-start | bytes 3145732
  91.8 3.8 %copy-start.17 = (f32[2]{0:T(128)S(1)}, f32[2]{0:T(128)}, u32[]{:S(2)}) copy-start(f32[2]{0:T(128)} %maximum_bitcast_fusion) | copy-start | bytes 28
  91.8 54.0 %collective-permute-start.21 = (bf16[256,256]{1,0:T(8,128)(2,1)S(1)}, bf16[256,256]{1,0:T(8,128)(2,1)S(1)}, u32[]{:S(2)}, u32[]{:S(2)}) collective-permute-start(bf16[256,256]{1,0:T(8,128)(2,1)S(1)} %bitcast.38), channel_id=1, source_target_pairs={{0,2},{2,4},{4,6},{6,8},{8,10},{10,12},{12,14},{14,16},{16,18},{18... | collective-permute-start | bytes 393224 | tf_op jit(solution)/shard_map/ppermute | solution.py:393
  92.1 9.2 %collective-permute-start.14 = (bf16[2,256,256]{2,1,0:T(8,128)(2,1)S(1)}, bf16[2,256,256]{2,1,0:T(8,128)(2,1)S(1)}, u32[]{:S(2)}, u32[]{:S(2)}) collective-permute-start(bf16[2,256,256]{2,1,0:T(8,128)(2,1)S(1)} %slice.109), channel_id=1, source_target_pairs={{0,8},{2,10},{4,12},{6,14},{8,0},{10,2},{12,4},{14,6},{16,24},{18,... | collective-permute-start | bytes 786440 | tf_op jit(solution)/shard_map/ppermute | solution.py:339
  92.2 42.6 %copy-start.13 = (f32[3]{0:T(128)S(1)}, f32[3]{0:T(128)}, u32[]{:S(2)}) copy-start(f32[3]{0:T(128)} %get-tuple-element.50) | copy-start | bytes 40
  92.2 42.7 %copy-start.12 = (f32[3,2048]{1,0:T(4,128)S(1)}, f32[3,2048]{1,0:T(4,128)}, u32[]{:S(2)}) copy-start(f32[3,2048]{1,0:T(4,128)} %param.13) | copy-start | bytes 73732
  93.6 12.5 %collective-permute-start.4 = (bf16[2,256,256]{2,1,0:T(8,128)(2,1)S(1)}, bf16[2,256,256]{2,1,0:T(8,128)(2,1)S(1)}, u32[]{:S(2)}, u32[]{:S(2)}) collective-permute-start(bf16[2,256,256]{2,1,0:T(8,128)(2,1)S(1)} %slice.110), channel_id=1, source_target_pairs={{0,8},{2,10},{4,12},{6,14},{8,0},{10,2},{12,4},{14,6},{16,24},{18,... | collective-permute-start | bytes 786440 | tf_op jit(solution)/shard_map/ppermute | solution.py:339
  101.3 44.5 %collective-permute-start.22 = (bf16[256,256]{1,0:T(8,128)(2,1)S(1)}, bf16[256,256]{1,0:T(8,128)(2,1)S(1)}, u32[]{:S(2)}, u32[]{:S(2)}) collective-permute-start(bf16[256,256]{1,0:T(8,128)(2,1)S(1)} %bitcast.37), channel_id=1, source_target_pairs={{2,0},{4,2},{6,4},{8,6},{10,8},{12,10},{14,12},{16,14},{18,16},{20... | collective-permute-start | bytes 393224 | tf_op jit(solution)/shard_map/ppermute | solution.py:394
  106.1 8.4 %collective-permute-start.15 = (bf16[2,128,256]{2,1,0:T(8,128)(2,1)S(1)}, bf16[2,128,256]{2,1,0:T(8,128)(2,1)S(1)}, u32[]{:S(2)}, u32[]{:S(2)}) collective-permute-start(bf16[2,128,256]{2,1,0:T(8,128)(2,1)S(1)} %slice.111), channel_id=1, source_target_pairs={{0,16},{2,18},{4,20},{6,22},{8,24},{10,26},{12,28},{14,30},{16,0},... | collective-permute-start | bytes 393224 | tf_op jit(solution)/shard_map/ppermute | solution.py:339
  114.4 9.9 %collective-permute-start.5 = (bf16[2,128,256]{2,1,0:T(8,128)(2,1)S(1)}, bf16[2,128,256]{2,1,0:T(8,128)(2,1)S(1)}, u32[]{:S(2)}, u32[]{:S(2)}) collective-permute-start(bf16[2,128,256]{2,1,0:T(8,128)(2,1)S(1)} %slice.112), channel_id=1, source_target_pairs={{0,16},{2,18},{4,20},{6,22},{8,24},{10,26},{12,28},{14,30},{16,0},... | collective-permute-start | bytes 393224 | tf_op jit(solution)/shard_map/ppermute | solution.py:339
  124.3 7.3 %collective-permute-start.16 = (bf16[2,128,256]{2,1,0:T(8,128)(2,1)S(1)}, bf16[2,128,256]{2,1,0:T(8,128)(2,1)S(1)}, u32[]{:S(2)}, u32[]{:S(2)}) collective-permute-start(bf16[2,128,256]{2,1,0:T(8,128)(2,1)S(1)} %fusion.1), channel_id=1, source_target_pairs={{0,16},{2,18},{4,20},{6,22},{8,24},{10,26},{12,28},{14,30},{16,0},... | collective-permute-start | bytes 393224 | tf_op jit(solution)/shard_map/ppermute | solution.py:339
  131.6 7.2 %collective-permute-start.10 = (bf16[2,128,256]{2,1,0:T(8,128)(2,1)S(1)}, bf16[2,128,256]{2,1,0:T(8,128)(2,1)S(1)}, u32[]{:S(2)}, u32[]{:S(2)}) collective-permute-start(bf16[2,128,256]{2,1,0:T(8,128)(2,1)S(1)} %fusion.3), channel_id=1, source_target_pairs={{0,16},{2,18},{4,20},{6,22},{8,24},{10,26},{12,28},{14,30},{16,0},... | collective-permute-start | bytes 393224 | tf_op jit(solution)/shard_map/ppermute | solution.py:339
  131.6 11.6 %collective-permute-start.17 = (bf16[2,256,256]{2,1,0:T(8,128)(2,1)S(1)}, bf16[2,256,256]{2,1,0:T(8,128)(2,1)S(1)}, u32[]{:S(2)}, u32[]{:S(2)}) collective-permute-start(bf16[2,256,256]{2,1,0:T(8,128)(2,1)S(1)} %pad_maximum_fusion.4), channel_id=1, source_target_pairs={{0,8},{2,10},{4,12},{6,14},{8,0},{10,2},{12,4},{14,6},{16,24},{18,... | collective-permute-start | bytes 786440 | tf_op jit(solution)/shard_map/ppermute | solution.py:339
  138.8 14.0 %collective-permute-start.11 = (bf16[2,256,256]{2,1,0:T(8,128)(2,1)S(1)}, bf16[2,256,256]{2,1,0:T(8,128)(2,1)S(1)}, u32[]{:S(2)}, u32[]{:S(2)}) collective-permute-start(bf16[2,256,256]{2,1,0:T(8,128)(2,1)S(1)} %pad_maximum_fusion.3), channel_id=1, source_target_pairs={{0,8},{2,10},{4,12},{6,14},{8,0},{10,2},{12,4},{14,6},{16,24},{18,... | collective-permute-start | bytes 786440 | tf_op jit(solution)/shard_map/ppermute | solution.py:339
  143.2 9.6 %copy-start.4 = (bf16[2,512,256]{2,1,0:T(8,128)(2,1)}, bf16[2,512,256]{2,1,0:T(8,128)(2,1)S(1)}, u32[]{:S(2)}) copy-start(bf16[2,512,256]{2,1,0:T(8,128)(2,1)S(1)} %pad_maximum_fusion.2.refs_4_) | copy-start | bytes 1572868
  143.3 15.5 %collective-permute-start.18 = (bf16[2,512,256]{2,1,0:T(8,128)(2,1)S(1)}, bf16[2,512,256]{2,1,0:T(8,128)(2,1)S(1)}, u32[]{:S(2)}, u32[]{:S(2)}) collective-permute-start(bf16[2,512,256]{2,1,0:T(8,128)(2,1)S(1)} %pad_maximum_fusion.2.refs_4_), channel_id=1, source_target_pairs={{0,4},{2,6},{4,0},{6,2},{8,12},{10,14},{12,8},{14,10},{16,20},{18,... | collective-permute-start | bytes 1572872 | tf_op jit(solution)/shard_map/ppermute | solution.py:339
  145.8 0.6 copy-start.21
  146.5 0.7 copy-start.22
  152.9 5.9 %copy-start.2 = (bf16[2,512,256]{2,1,0:T(8,128)(2,1)}, bf16[2,512,256]{2,1,0:T(8,128)(2,1)S(1)}, u32[]{:S(2)}) copy-start(bf16[2,512,256]{2,1,0:T(8,128)(2,1)S(1)} %pad_maximum_fusion.1.refs_4_) | copy-start | bytes 1572868
  152.9 15.1 %collective-permute-start.12 = (bf16[2,512,256]{2,1,0:T(8,128)(2,1)S(1)}, bf16[2,512,256]{2,1,0:T(8,128)(2,1)S(1)}, u32[]{:S(2)}, u32[]{:S(2)}) collective-permute-start(bf16[2,512,256]{2,1,0:T(8,128)(2,1)S(1)} %pad_maximum_fusion.1.refs_4_), channel_id=1, source_target_pairs={{0,4},{2,6},{4,0},{6,2},{8,12},{10,14},{12,8},{14,10},{16,20},{18,... | collective-permute-start | bytes 1572872 | tf_op jit(solution)/shard_map/ppermute | solution.py:339
  158.8 0.8 copy-start.6
  168.0 0.8 copy-start.3
  173.3 12.1 %collective-permute-start.27 = (bf16[1024,256]{1,0:T(8,128)(2,1)}, bf16[1024,256]{1,0:T(8,128)(2,1)S(1)}, u32[]{:S(2)}, u32[]{:S(2)}) collective-permute-start(bf16[1024,256]{1,0:T(8,128)(2,1)} %messages.10), channel_id=1, source_target_pairs={{0,2},{2,0},{4,6},{6,4},{8,10},{10,8},{12,14},{14,12},{16,18},{18,... | collective-permute-start | bytes 1572872 | tf_op jit(solution)/shard_map/ppermute | solution.py:339
  177.9 14.0 %collective-permute-start.23 = (bf16[1024,256]{1,0:T(8,128)(2,1)}, bf16[1024,256]{1,0:T(8,128)(2,1)S(1)}, u32[]{:S(2)}, u32[]{:S(2)}) collective-permute-start(bf16[1024,256]{1,0:T(8,128)(2,1)} %messages.8), channel_id=1, source_target_pairs={{0,2},{2,0},{4,6},{6,4},{8,10},{10,8},{12,14},{14,12},{16,18},{18,... | collective-permute-start | bytes 1572872 | tf_op jit(solution)/shard_map/ppermute | solution.py:339
  185.5 5.9 %copy-start.14 = (f32[512]{0:T(512)S(1)}, f32[512]{0:T(512)}, u32[]{:S(2)}) copy-start(f32[512]{0:T(512)} %param.20) | copy-start | bytes 6148
  185.5 0.8 copy-start.11
  191.2 15.0 %collective-permute-start.28 = (bf16[1024,256]{1,0:T(8,128)(2,1)}, bf16[1024,256]{1,0:T(8,128)(2,1)S(1)}, u32[]{:S(2)}, u32[]{:S(2)}) collective-permute-start(bf16[1024,256]{1,0:T(8,128)(2,1)} %get-tuple-element.36), channel_id=1, source_target_pairs={{0,1},{1,0},{2,3},{3,2},{4,5},{5,4},{6,7},{7,6},{8,9},{9,8},{10,11... | collective-permute-start | bytes 1572872 | tf_op jit(solution)/shard_map/ppermute | solution.py:334
  191.9 0.8 copy-start.10
  198.6 13.2 %collective-permute-start.26 = (bf16[512,256]{1,0:T(8,128)(2,1)S(1)}, bf16[512,256]{1,0:T(8,128)(2,1)S(1)}, u32[]{:S(2)}, u32[]{:S(2)}) collective-permute-start(bf16[512,256]{1,0:T(8,128)(2,1)S(1)} %get-tuple-element.41), channel_id=1, source_target_pairs={{0,1},{1,0},{2,3},{3,2},{4,5},{5,4},{6,7},{7,6},{8,9},{9,8},{10,11... | collective-permute-start | bytes 786440 | tf_op jit(solution)/shard_map/ppermute | solution.py:334
  200.6 15.9 %collective-permute-start.24 = (bf16[512,256]{1,0:T(8,128)(2,1)S(1)}, bf16[512,256]{1,0:T(8,128)(2,1)S(1)}, u32[]{:S(2)}, u32[]{:S(2)}) collective-permute-start(bf16[512,256]{1,0:T(8,128)(2,1)S(1)} %get-tuple-element.42), channel_id=1, source_target_pairs={{0,1},{1,0},{2,3},{3,2},{4,5},{5,4},{6,7},{7,6},{8,9},{9,8},{10,11... | collective-permute-start | bytes 786440 | tf_op jit(solution)/shard_map/ppermute | solution.py:334
  206.2 0.8 copy-start.18
  211.8 0.7 copy-start.20
  212.5 8.2 %copy-start.1 = (f32[4,512]{1,0:T(4,128)S(1)}, f32[4,512]{1,0:T(4,128)}, u32[]{:S(2)}) copy-start(f32[4,512]{1,0:T(4,128)} %param.19) | copy-start | bytes 24580
  216.5 0.7 copy-start.19

commit v4 on v3

--- a/solution.py
+++ b/solution.py
@@ -14,6 +14,7 @@
 GROUPS = (1,)
 TILE = 256
 FORWARD_ROWS = 256
+LIMIT = pltpu.CompilerParams(vmem_limit_bytes=16 << 20)
 
 SIN_1, SIN_0, SIN_BY = -8.313817368817206, 20.224572228345814, 12.875426983082301
 COS_ROOT, COS_1, COS_0 = 0.9993568028372194, -11.426868481113639, 49.031109066681445
@@ -36,15 +37,19 @@
 
 def forward_body(
     start, first, block_rows, places, waves_ref, own_pos, other_pos, own_ref, other_ref,
-    cos_ref, sin_ref, sum_ref, turned, lhs, rhs, turns,
+    cos_ref, sin_ref, sum_ref, columns, turned, lhs, rhs, turns,
 ):
     rows = lhs.shape[0]
     step = pl.program_id(0)
     sums = [None, None]
     atom_rows = own_ref.shape[0]
+    here = pl.ds(pl.multiple_of(step * rows, rows), rows)
+    cos_ref, sin_ref = cos_ref.at[here], sin_ref.at[here]
 
     @pl.when(step == 0)
     def _():
+        begin = pl.multiple_of(places[1], columns.shape[0])
+        columns[...] = jnp.transpose(waves_ref[:, pl.ds(begin, columns.shape[0])])
         for number, ref in enumerate((own_pos, other_pos)):
             keep = lax.broadcasted_iota(jnp.int32, ref.shape, 0) < 3
             high, middle, low = thirds(jnp.where(keep, ref[...], jnp.float32(0)))
@@ -54,8 +59,8 @@
 
     for part in range(rows // block_rows):
         number = (first + step * (rows // block_rows) + part) ^ places[0]
-        at = pl.multiple_of(places[1] + start + number * block_rows, block_rows)
-        turned[part * block_rows : (part + 1) * block_rows, :] = waves_ref[pl.ds(at, block_rows), :]
+        at = pl.multiple_of(start + number * block_rows, block_rows)
+        turned[part * block_rows : (part + 1) * block_rows, :] = columns[pl.ds(at, block_rows), :]
     high, middle, low = thirds(turned[...])
     lhs[...] = jnp.concatenate([high, high, middle, high, low, middle], axis=1).astype(jnp.bfloat16)
 
@@ -94,25 +99,26 @@
 
 
 def forward(places, waves, positions, feats, start, position, count, block_rows, dtype):
-    depth = waves.shape[1]
+    depth = waves.shape[0]
     atom_rows, width = feats[0].shape
     tile = min(FORWARD_ROWS, count)
-    trig = jax.ShapeDtypeStruct((count, 2 * atom_rows), jnp.bfloat16)
+    trig = pltpu.VMEM((count, 2 * atom_rows), jnp.bfloat16)
     return pl.pallas_call(
         functools.partial(forward_body, start, position // block_rows, block_rows),
         grid_spec=pltpu.PrefetchScalarGridSpec(
             num_scalar_prefetch=1,
             grid=(count // tile,),
             in_specs=[
-                pl.BlockSpec(array.shape, lambda k, *_: (0, 0))
+                pl.BlockSpec(array.shape, lambda k, *_: (0, 0), pipeline_mode=pl.Buffered(1))
                 for array in (waves, *positions, *feats)
             ],
             out_specs=[
-                pl.BlockSpec((tile, 2 * atom_rows), lambda k, *_: (k, 0)),
-                pl.BlockSpec((tile, 2 * atom_rows), lambda k, *_: (k, 0)),
+                pl.BlockSpec(memory_space=pltpu.VMEM),
+                pl.BlockSpec(memory_space=pltpu.VMEM),
                 pl.BlockSpec((2, tile, width), lambda k, *_: (0, k, 0)),
             ],
             scratch_shapes=[
+                pltpu.VMEM((waves.shape[1] // 2, depth), jnp.float32),
                 pltpu.VMEM((tile, depth), jnp.float32),
                 pltpu.VMEM((tile, 6 * depth), jnp.bfloat16),
                 pltpu.VMEM((6 * depth, 2 * atom_rows), jnp.bfloat16),
@@ -120,6 +126,7 @@
             ],
         ),
         out_shape=[trig, trig, jax.ShapeDtypeStruct((2, count, width), dtype)],
+        compiler_params=LIMIT,
         cost_estimate=pl.CostEstimate(
             flops=18 * count * atom_rows * width,
             transcendentals=0,
@@ -204,21 +211,21 @@
             transcendentals=0,
             bytes_accessed=8 * cells * cap * width,
         ),
+        compiler_params=LIMIT,
         name="near",
     )(places, scales, rows, left, masked, right, feats, mix, *args)
 
 
-def backward_body(parts, has_acc, has_came, *refs):
+def backward_body(parts, first, tile, has_acc, *refs):
     refs = list(refs)
+    here = pl.ds(pl.multiple_of(first + pl.program_id(0) * tile, tile), tile)
     trig, filts, rest = refs[: 2 * parts], refs[2 * parts : 3 * parts], refs[3 * parts :]
     contract = (((0,), (0,)), ((), ()))
     total = rest.pop(0)[...] if has_acc else None
-    if has_came:
-        total = total + rest.pop(0)[...].astype(jnp.float32)
     for part in range(parts):
         for which in range(2):
             term = lax.dot_general(
-                trig[2 * part + which][...],
+                trig[2 * part + which][:, here],
                 filts[part][which],
                 contract,
                 preferred_element_type=jnp.float32,
@@ -228,27 +235,26 @@
         ref[...] = total.astype(ref.dtype)
 
 
-def backward(chunks, first, count, tile, acc, came, dtypes):
+def backward(chunks, first, count, tile, acc, dtype):
     parts = [part for chunk in chunks for part in chunk]
     width = parts[0][2].shape[2]
-    at = first // tile
     args, specs = [], []
-    for array in (acc, came):
-        if array is not None:
-            array, offset = array
-            args.append(array)
-            specs.append(pl.BlockSpec((tile, width), lambda i, offset=offset // tile: (i + offset, 0)))
+    if acc is not None:
+        offset = acc[1] // tile
+        args.append(acc[0])
+        specs.append(pl.BlockSpec((tile, width), lambda i: (i + offset, 0)))
     trig = [array for cos, sin, _ in parts for array in (cos, sin)]
     filts = [filt for _, _, filt in parts]
     rows = sum(cos.shape[0] for cos, _, _ in parts)
     return pl.pallas_call(
-        functools.partial(backward_body, len(parts), acc is not None, came is not None),
+        functools.partial(backward_body, len(parts), first, tile, acc is not None),
         grid=(count // tile,),
-        in_specs=[pl.BlockSpec((array.shape[0], tile), lambda i: (0, i + at)) for array in trig]
+        in_specs=[pl.BlockSpec(memory_space=pltpu.VMEM) for _ in trig]
         + [pl.BlockSpec(filt.shape, lambda i: (0, 0, 0)) for filt in filts]
         + specs,
-        out_specs=[pl.BlockSpec((tile, width), lambda i: (i, 0))] * len(dtypes),
-        out_shape=[jax.ShapeDtypeStruct((count, width), dtype) for dtype in dtypes],
+        out_specs=pl.BlockSpec((tile, width), lambda i: (i, 0)),
+        out_shape=jax.ShapeDtypeStruct((count, width), dtype),
+        compiler_params=LIMIT,
         cost_estimate=pl.CostEstimate(
             flops=8 * rows * count * width,
             transcendentals=0,
@@ -258,12 +264,12 @@
     )(*trig, *filts, *args)
 
 
-def mlp_body(side, own_ref, other_ref, gain_ref, in_ref, out_ref, both_ref, *refs):
+def mlp_body(side, own_ref, came_ref, other_ref, gain_ref, in_ref, out_ref, both_ref, *refs):
     result_ref = refs[-1]
     width = own_ref.shape[1]
     hidden_count = in_ref.shape[1]
     mine = side[0]
-    own = own_ref[...]
+    own = own_ref[...] + came_ref[...].astype(jnp.float32)
     own_wide = own.astype(jnp.bfloat16).astype(jnp.float32)
     other = other_ref[...].astype(jnp.float32)
     mean = (
@@ -271,10 +277,10 @@
         + jnp.sum(other * other, axis=1, keepdims=True)
     ) / (2 * width)
     scale = lax.rsqrt(mean + EPS)
-    normed_own = (own_wide * scale * gain_ref[pl.ds(mine, 1), :]).astype(jnp.bfloat16)
-    normed_other = (other * scale * gain_ref[pl.ds(1 - mine, 1), :]).astype(jnp.bfloat16)
     at_own = pl.ds(pl.multiple_of(mine * width, width), width)
     at_other = pl.ds(pl.multiple_of((1 - mine) * width, width), width)
+    normed_own = (own_wide * scale * gain_ref[:, at_own]).astype(jnp.bfloat16)
+    normed_other = (other * scale * gain_ref[:, at_other]).astype(jnp.bfloat16)
     total = own
     hidden_columns = slice(0, hidden_count)
     halves = (
@@ -292,7 +298,7 @@
     result_ref[...] = total.astype(jnp.bfloat16)
 
 
-def mlp(side, own, own_at, other, gains, weights, result, first, total_rows):
+def mlp(side, own, came, own_at, other, gains, weights, result, first, total_rows):
     rows, width = other.shape
     offset, own_offset = first // rows, own_at // rows
     args = [] if result is None else [result]
@@ -303,6 +309,7 @@
             grid=(1,),
             in_specs=[
                 pl.BlockSpec((rows, width), lambda i, *_: (own_offset, 0)),
+                pl.BlockSpec((rows, width), lambda i, *_: (own_offset, 0)),
                 pl.BlockSpec((rows, width), lambda i, *_: (0, 0)),
                 pl.BlockSpec(gains.shape, lambda i, *_: (0, 0)),
             ]
@@ -311,14 +318,15 @@
             out_specs=pl.BlockSpec((rows, width), lambda i, *_: (offset, 0)),
         ),
         out_shape=jax.ShapeDtypeStruct((total_rows, width), jnp.bfloat16),
-        input_output_aliases={7: 0} if args else {},
+        input_output_aliases={8: 0} if args else {},
         cost_estimate=pl.CostEstimate(
             flops=2 * rows * width * weights[0].shape[1] * 12,
             transcendentals=0,
             bytes_accessed=8 * rows * width,
         ),
+        compiler_params=LIMIT,
         name="mlp",
-    )(side, own, other, gains, *weights, *args)
+    )(side, own, came, other, gains, *weights, *args)
 
 
 def thirds(values):
@@ -383,7 +391,7 @@
     places_of_waves = jnp.stack([reverse, core * own_waves])
 
     def wave_operand(waves):
-        return jnp.pad(waves * jnp.float32(1.0 / (2.0 * math.pi)), ((0, 5), (0, 0))).T
+        return jnp.pad(waves * jnp.float32(1.0 / (2.0 * math.pi)), ((0, 5), (0, 0)))
 
     other_waves = swap(wavevectors)
 
@@ -497,30 +505,26 @@
         at += size
         if not taken:
             continue
-        (other,) = backward(
-            taken, atom_rows, atom_rows, half_rows, None if other is None else (other, 0), None, (f32,)
+        other = backward(
+            taken, atom_rows, atom_rows, half_rows, None if other is None else (other, 0), f32
         )
-        (mine,) = backward(taken, 0, atom_rows, half_rows, (mine, 0), None, (f32,))
+        mine = backward(taken, 0, atom_rows, half_rows, (mine, 0), f32)
     last = chunks[-1:]
-    came = []
-    for half in range(2):
-        (send,) = backward(
-            last, atom_rows + half * half_rows, half_rows, half_rows // 2, (other, half * half_rows), None, (bf16,)
-        )
-        came.append(across(send, core_bit))
-    gains = norm_gain.reshape(2, width)
+    tile = half_rows // 2
+    gains = norm_gain[None, :]
     weights = (in_weight, out_own, both)
     result = None
     for half in range(2):
-        part, send = backward(
-            last, half * half_rows, half_rows, half_rows // 2, (mine, half * half_rows), (came[half], 0), (f32, bf16)
-        )
+        send = backward(last, atom_rows + half * half_rows, half_rows, tile, (other, half * half_rows), bf16)
+        came = across(send, core_bit)
+        part = backward(last, half * half_rows, half_rows, tile, (mine, half * half_rows), f32)
         pieces = 1 if half == 0 else 2
         piece_rows = half_rows // pieces
         for piece in range(pieces):
-            arrived = swap(send[piece * piece_rows : (piece + 1) * piece_rows])
+            rows_of = slice(piece * piece_rows, (piece + 1) * piece_rows)
+            arrived = swap((part[rows_of] + came[rows_of].astype(f32)).astype(bf16))
             result = mlp(
-                side.reshape(1), part, piece * piece_rows, arrived, gains, weights, result,
+                side.reshape(1), part, came, piece * piece_rows, arrived, gains, weights, result,
                 half * half_rows + piece * piece_rows, atom_rows,
             )
     return result

time: 222 us -> 185 us (0.83)
  Pallas kernels: 102 us -> 57 us
  waiting for transfers between devices: 53.3 us -> 81.4 us
  local copies, waits for them, and re-layouts: 19.8 us -> 7.28 us
  other arithmetic: 14.7 us -> 10.7 us
  starting transfers between devices: 29.6 us -> 27 us
    pallas_call x6, Pallas kernels: 32.5 us -> 12.1 us  [backward(): pl.pallas_call(functools.partial(backward_body, len(parts), first, tile,...]
    ppermute x19, waiting for transfers between devices: 47.5 us -> 64.9 us  [across(): return lax.ppermute(value, 'cells', [(i, i ^ bit) for i in range(count)])]
    pallas_call x4, Pallas kernels: 46.5 us -> 31.4 us  [forward(): pl.pallas_call(functools.partial(forward_body, start, position // block_r...]
    ppermute x6, waiting for transfers between devices: 5.85 us -> 16.5 us  [swap(): return lax.ppermute(value, 'waves', [(0, 1), (1, 0)])]
    unnamed x48 -> x31, local copies, waits for them, and re-layouts: 9.58 us -> 3.27 us
    pallas_call x3, Pallas kernels: 12 us -> 7.02 us  [mlp(): pl.pallas_call(mlp_body, grid_spec=pltpu.PrefetchScalarGridSpec(num_scala...]
    pallas_call x2, Pallas kernels: 11.4 us -> 6.53 us  [near_part(): pl.pallas_call(functools.partial(near_body, base), grid_spec=pltpu.Prefet...]
  transfers between devices with their start and end apart: 29 -> 29, of which waited for: 13 -> 15; matrix products, arithmetic and copies ran while one was open for 12% -> 8% of each run, Pallas kernels for 45% -> 30%
where the time goes in v4:
time: 185 us
  waiting for transfers between devices  81.4 us (44%)
  Pallas kernels  57 us (31%)
  starting transfers between devices  27 us (15%)
  other arithmetic  10.7 us (6%)
  local copies, waits for them, and re-layouts  7.28 us (4%)
    ppermute x19, waiting for transfers between devices, across(): return lax.ppermute(value, 'cells', [(i, i ^ bit) for i in range(count)])  64.9 us
    pallas_call x4, Pallas kernels, forward(): pl.pallas_call(functools.partial(forward_body, start, position // block_r...  31.4 us
    ppermute x6, waiting for transfers between devices, swap(): return lax.ppermute(value, 'waves', [(0, 1), (1, 0)])  16.5 us
    pallas_call x6, Pallas kernels, backward(): pl.pallas_call(functools.partial(backward_body, len(parts), first, tile,...  12.1 us
    ppermute x19, starting transfers between devices, across(): return lax.ppermute(value, 'cells', [(i, i ^ bit) for i in range(count)])  11.3 us
    ppermute x6, starting transfers between devices, swap(): return lax.ppermute(value, 'waves', [(0, 1), (1, 0)])  8.31 us
    pallas_call x3, Pallas kernels, mlp(): pl.pallas_call(mlp_body, grid_spec=pltpu.PrefetchScalarGridSpec(num_scala...  7.02 us
    pallas_call x2, Pallas kernels, near_part(): pl.pallas_call(functools.partial(near_body, base), grid_spec=pltpu.Prefet...  6.53 us
  transfers between devices with their start and end apart: 29, of which 15 were waited for; matrix products, arithmetic and copies ran while one was open for 8% of the time, Pallas kernels for 30%

profile of v4, /device:TPU:0, one launch (start us, length us, event | category | flops | bytes accessed | tf_op | source)
XLA Modules:
  0.0 184.5 jit_solution(6688831473704553684)
XLA Ops:
  0.0 3.0 %collective-permute-start = (f32[3,2048]{1,0:T(4,128)}, f32[3,2048]{1,0:T(4,128)S(1)}, u32[]{:S(2)}, u32[]{:S(2)}) collective-permute-start(f32[3,2048]{1,0:T(4,128)} %param.16), channel_id=1, source_target_pairs={{0,1},{1,0},{2,3},{3,2},{4,5},{5,4},{6,7},{7,6},{8,9},{9,8},{10,11... | collective-permute-start | bytes 73736 | tf_op jit(solution)/shard_map/ppermute | solution.py:342
  3.1 0.7 convert_bitcast_fusion
  3.7 0.8 select_maximum_fusion.2.own_pos
  4.6 0.7 iota_compare_fusion.2
  5.3 1.5 broadcast_select_fusion.own_ref
  6.8 0.6 collective-permute-start.2
  7.4 1.0 fusion.10
  8.5 0.7 fusion.12
  9.2 4.6 %collective-permute-start.20 = (f32[3,256]{1,0:T(4,128)S(1)}, f32[3,256]{1,0:T(4,128)S(1)}, u32[]{:S(2)}, u32[]{:S(2)}) collective-permute-start(f32[3,256]{1,0:T(4,128)S(1)} %get-tuple-element.38), channel_id=1, source_target_pairs={{2,0},{4,2},{6,4},{8,6},{10,8},{12,10},{14,12},{16,14},{18,16},{20... | collective-permute-start | bytes 9224 | tf_op jit(solution)/shard_map/ppermute | solution.py:404
  13.8 0.8 broadcast_multiply_fusion.2
  14.6 0.8 copy.17
  15.4 0.7 broadcast_multiply_fusion.4.scales
  16.1 1.5 broadcast_select_fusion.1.masked_ref
  17.6 1.1 constant_dynamic-slice_fusion
  18.9 0.6 fusion.8
  19.5 0.6 broadcast_in_dim.33
  20.3 3.5 %collective-permute-done.7 = f32[8,128]{1,0:T(8,128)S(1)} collective-permute-done((f32[8,128]{1,0:T(8,128)S(1)}, f32[8,128]{1,0:T(8,128)S(1)}, u32[]{:S(2)}, u32[]{:S(2)}) %collective-permute-start.7) | collective-permute-done | bytes 4128 | tf_op jit(solution)/shard_map/ppermute | solution.py:347
  23.8 0.6 broadcast_add_fusion.2
  24.5 3.5 %collective-permute-done.8 = f32[8,128]{1,0:T(8,128)S(1)} collective-permute-done((f32[8,128]{1,0:T(8,128)S(1)}, f32[8,128]{1,0:T(8,128)S(1)}, u32[]{:S(2)}, u32[]{:S(2)}) %collective-permute-start.8) | collective-permute-done | bytes 4128 | tf_op jit(solution)/shard_map/ppermute | solution.py:347
  28.1 0.6 fusion.13
  28.8 4.5 %collective-permute-done.9 = f32[8,128]{1,0:T(8,128)S(1)} collective-permute-done((f32[8,128]{1,0:T(8,128)S(1)}, f32[8,128]{1,0:T(8,128)S(1)}, u32[]{:S(2)}, u32[]{:S(2)}) %collective-permute-start.9) | collective-permute-done | bytes 4128 | tf_op jit(solution)/shard_map/ppermute | solution.py:347
  33.3 0.5 slice.70
  34.5 7.8 %structure.5 = (bf16[512,4096]{1,0:T(8,128)(2,1)S(1)}, bf16[512,4096]{1,0:T(8,128)(2,1)S(1)}, bf16[2,512,256]{2,1,0:T(8,128)(2,1)S(1)}) custom-call(s32[2]{0:T(128)S(1)} %pad_add_fusion.places, f32[8,2048]{1,0:T(8,128)S(1)} %pad.15.waves_ref, f32[8,2048]{1,0:T(8,128)S(1)} %select_maximum_fusion.2.own_pos, f32[8,2048]{1,0:T(8,128)S(1)} %collective-permute-done.1.other_pos, ...), custom_call_target="tpu_custom_call" | custom-call | flops 4831838208 | bytes 8388608 | tf_op jit(solution)/shard_map/structure/pallas_call | solution.py:106
  42.3 0.5 collective-permute-start.3
  42.8 1.2 copy-done.6
  44.0 1.2 copy-done.10
  45.3 7.8 %structure.7 = (bf16[512,4096]{1,0:T(8,128)(2,1)S(1)}, bf16[512,4096]{1,0:T(8,128)(2,1)S(1)}, bf16[2,512,256]{2,1,0:T(8,128)(2,1)S(1)}) custom-call(s32[2]{0:T(128)S(1)} %pad_add_fusion.places, f32[8,2048]{1,0:T(8,128)S(1)} %pad.17.waves_ref, f32[8,2048]{1,0:T(8,128)S(1)} %select_maximum_fusion.2.own_pos, f32[8,2048]{1,0:T(8,128)S(1)} %collective-permute-done.1.other_pos, ...), custom_call_target="tpu_custom_call" | custom-call | flops 4831838208 | bytes 8388608 | tf_op jit(solution)/shard_map/structure/pallas_call | solution.py:106
  53.1 1.6 collective-permute-start.13
  54.7 7.8 %structure.4 = (bf16[512,4096]{1,0:T(8,128)(2,1)S(1)}, bf16[512,4096]{1,0:T(8,128)(2,1)S(1)}, f32[2,512,256]{2,1,0:T(8,128)S(1)}) custom-call(s32[2]{0:T(128)S(1)} %pad_add_fusion.places, f32[8,2048]{1,0:T(8,128)S(1)} %pad.15.waves_ref, f32[8,2048]{1,0:T(8,128)S(1)} %select_maximum_fusion.2.own_pos, f32[8,2048]{1,0:T(8,128)S(1)} %collective-permute-done.1.other_pos, ...), custom_call_target="tpu_custom_call" | custom-call | flops 4831838208 | bytes 8388608 | tf_op jit(solution)/shard_map/structure/pallas_call | solution.py:106
  62.5 8.0 %structure.6 = (bf16[512,4096]{1,0:T(8,128)(2,1)S(1)}, bf16[512,4096]{1,0:T(8,128)(2,1)S(1)}, f32[2,512,256]{2,1,0:T(8,128)S(1)}) custom-call(s32[2]{0:T(128)S(1)} %pad_add_fusion.places, f32[8,2048]{1,0:T(8,128)S(1)} %pad.17.waves_ref, f32[8,2048]{1,0:T(8,128)S(1)} %select_maximum_fusion.2.own_pos, f32[8,2048]{1,0:T(8,128)S(1)} %collective-permute-done.1.other_pos, ...), custom_call_target="tpu_custom_call" | custom-call | flops 4831838208 | bytes 8388608 | tf_op jit(solution)/shard_map/structure/pallas_call | solution.py:106
  70.5 2.8 %collective-permute-start.22 = (bf16[256,256]{1,0:T(8,128)(2,1)S(1)}, bf16[256,256]{1,0:T(8,128)(2,1)S(1)}, u32[]{:S(2)}, u32[]{:S(2)}) collective-permute-start(bf16[256,256]{1,0:T(8,128)(2,1)S(1)} %bitcast.41), channel_id=1, source_target_pairs={{2,0},{4,2},{6,4},{8,6},{10,8},{12,10},{14,12},{16,14},{18,16},{20... | collective-permute-start | bytes 393224 | tf_op jit(solution)/shard_map/ppermute | solution.py:402
  73.7 2.1 %collective-permute-start.4 = (bf16[2,256,256]{2,1,0:T(8,128)(2,1)S(1)}, bf16[2,256,256]{2,1,0:T(8,128)(2,1)S(1)}, u32[]{:S(2)}, u32[]{:S(2)}) collective-permute-start(bf16[2,256,256]{2,1,0:T(8,128)(2,1)S(1)} %slice.130), channel_id=1, source_target_pairs={{0,8},{2,10},{4,12},{6,14},{8,0},{10,2},{12,4},{14,6},{16,24},{18,... | collective-permute-start | bytes 786440 | tf_op jit(solution)/shard_map/ppermute | solution.py:347
  75.8 1.0 broadcast_multiply_fusion
  76.8 5.9 %collective-permute-done.14 = bf16[2,256,256]{2,1,0:T(8,128)(2,1)S(1)} collective-permute-done((bf16[2,256,256]{2,1,0:T(8,128)(2,1)S(1)}, bf16[2,256,256]{2,1,0:T(8,128)(2,1)S(1)}, u32[]{:S(2)}, u32[]{:S(2)}) %collective-permute-start.14) | collective-permute-done | bytes 262176 | tf_op jit(solution)/shard_map/ppermute | solution.py:347
  82.7 1.5 collective-permute-start.25
  84.3 1.5 collective-permute-done.4
  85.8 2.1 %collective-permute-start.15 = (bf16[2,128,256]{2,1,0:T(8,128)(2,1)S(1)}, bf16[2,128,256]{2,1,0:T(8,128)(2,1)S(1)}, u32[]{:S(2)}, u32[]{:S(2)}) collective-permute-start(bf16[2,128,256]{2,1,0:T(8,128)(2,1)S(1)} %slice.131), channel_id=1, source_target_pairs={{0,16},{2,18},{4,20},{6,22},{8,24},{10,26},{12,28},{14,30},{16,0},... | collective-permute-start | bytes 393224 | tf_op jit(solution)/shard_map/ppermute | solution.py:347
  88.0 7.1 %collective-permute-done.15 = bf16[2,128,256]{2,1,0:T(8,128)(2,1)S(1)} collective-permute-done((bf16[2,128,256]{2,1,0:T(8,128)(2,1)S(1)}, bf16[2,128,256]{2,1,0:T(8,128)(2,1)S(1)}, u32[]{:S(2)}, u32[]{:S(2)}) %collective-permute-start.15) | collective-permute-done | bytes 131104 | tf_op jit(solution)/shard_map/ppermute | solution.py:347
  95.2 8.9 %collective-permute-done.5 = bf16[2,128,256]{2,1,0:T(8,128)(2,1)S(1)} collective-permute-done((bf16[2,128,256]{2,1,0:T(8,128)(2,1)S(1)}, bf16[2,128,256]{2,1,0:T(8,128)(2,1)S(1)}, u32[]{:S(2)}, u32[]{:S(2)}) %collective-permute-start.5) | collective-permute-done | bytes 131104 | tf_op jit(solution)/shard_map/ppermute | solution.py:347
  104.2 8.4 %collective-permute-done.16 = bf16[2,128,256]{2,1,0:T(8,128)(2,1)S(1)} collective-permute-done((bf16[2,128,256]{2,1,0:T(8,128)(2,1)S(1)}, bf16[2,128,256]{2,1,0:T(8,128)(2,1)S(1)}, u32[]{:S(2)}, u32[]{:S(2)}) %collective-permute-start.16) | collective-permute-done | bytes 131104 | tf_op jit(solution)/shard_map/ppermute | solution.py:347
  112.6 2.5 %collective-permute-start.17 = (bf16[2,256,256]{2,1,0:T(8,128)(2,1)S(1)}, bf16[2,256,256]{2,1,0:T(8,128)(2,1)S(1)}, u32[]{:S(2)}, u32[]{:S(2)}) collective-permute-start(bf16[2,256,256]{2,1,0:T(8,128)(2,1)S(1)} %pad_maximum_fusion.4), channel_id=1, source_target_pairs={{0,8},{2,10},{4,12},{6,14},{8,0},{10,2},{12,4},{14,6},{16,24},{18,... | collective-permute-start | bytes 786440 | tf_op jit(solution)/shard_map/ppermute | solution.py:347
  115.2 4.4 %collective-permute-done.10 = bf16[2,128,256]{2,1,0:T(8,128)(2,1)S(1)} collective-permute-done((bf16[2,128,256]{2,1,0:T(8,128)(2,1)S(1)}, bf16[2,128,256]{2,1,0:T(8,128)(2,1)S(1)}, u32[]{:S(2)}, u32[]{:S(2)}) %collective-permute-start.10) | collective-permute-done | bytes 131104 | tf_op jit(solution)/shard_map/ppermute | solution.py:347
  119.7 3.9 %collective-permute-done.17 = bf16[2,256,256]{2,1,0:T(8,128)(2,1)S(1)} collective-permute-done((bf16[2,256,256]{2,1,0:T(8,128)(2,1)S(1)}, bf16[2,256,256]{2,1,0:T(8,128)(2,1)S(1)}, u32[]{:S(2)}, u32[]{:S(2)}) %collective-permute-start.17) | collective-permute-done | bytes 262176 | tf_op jit(solution)/shard_map/ppermute | solution.py:347
  123.8 3.3 %near.2.refs_0_ = f32[2048,256]{1,0:T(8,128)S(1)} custom-call(s32[16,3]{1,0:T(8,128)S(1)} %broadcast_add_fusion.places, f32[4]{0:T(128)S(1)} %broadcast_multiply_fusion.4.scales, f32[20,8,128]{2,1,0:T(8,128)S(1)} %fusion.6.row_ref, bf16[2,128,256]{2,1,0:T(8,128)(2,1)S(1)} %bitcast.34, bf16[16,128,256]{2,1,0:T(8,128)(2,1)S(1)} %broadcast_select_fusion.1.masked_ref, ...), custom_call_target="tpu_custom_call" | custom-call | flops 3221225472 | bytes 2097152 | tf_op jit(solution)/shard_map/near/pallas_call | solution.py:186
  127.1 1.3 collective-permute-done.11
  128.4 0.8 collective-permute-start.12
  129.2 3.3 %near.3.refs_6_ = f32[2048,256]{1,0:T(8,128)S(1)} custom-call(s32[16,3]{1,0:T(8,128)S(1)} %broadcast_add_fusion.places, f32[4]{0:T(128)S(1)} %broadcast_multiply_fusion.4.scales, f32[20,8,128]{2,1,0:T(8,128)S(1)} %fusion.6.row_ref, bf16[2,128,256]{2,1,0:T(8,128)(2,1)S(1)} %bitcast.35, ...), custom_call_target="tpu_custom_call", output_to_operand_aliasing={{}: (8, {})} | custom-call | flops 3221225472 | bytes 2097152 | tf_op jit(solution)/shard_map/near/pallas_call | solution.py:186
  132.5 6.1 %collective-permute-done.18.refs_5_ = bf16[2,512,256]{2,1,0:T(8,128)(2,1)S(1)} collective-permute-done((bf16[2,512,256]{2,1,0:T(8,128)(2,1)S(1)}, bf16[2,512,256]{2,1,0:T(8,128)(2,1)S(1)}, u32[]{:S(2)}, u32[]{:S(2)}) %collective-permute-start.18) | collective-permute-done | bytes 524320 | tf_op jit(solution)/shard_map/ppermute | solution.py:347
  138.6 2.7 %messages.8.refs_6_ = f32[2048,256]{1,0:T(8,128)S(1)} custom-call(bf16[512,4096]{1,0:T(8,128)(2,1)S(1)} %get-tuple-element.23.refs_0_, bf16[512,4096]{1,0:T(8,128)(2,1)S(1)} %get-tuple-element.24.refs_1_, bf16[512,4096]{1,0:T(8,128)(2,1)S(1)} %get-tuple-element.25.refs_2_, bf16[512,4096]{1,0:T(8,128)(2,1)S(1)} %get-tuple-element.26.refs_3_, ...), custom_call_target="tpu_custom_call" | custom-call | flops 4294967296 | bytes 12582912 | tf_op jit(solution)/shard_map/messages/pallas_call | solution.py:249
  141.3 5.7 %collective-permute-done.12.refs_5_ = bf16[2,512,256]{2,1,0:T(8,128)(2,1)S(1)} collective-permute-done((bf16[2,512,256]{2,1,0:T(8,128)(2,1)S(1)}, bf16[2,512,256]{2,1,0:T(8,128)(2,1)S(1)}, u32[]{:S(2)}, u32[]{:S(2)}) %collective-permute-start.12) | collective-permute-done | bytes 524320 | tf_op jit(solution)/shard_map/ppermute | solution.py:347
  147.1 1.6 messages.9
  148.8 1.6 messages.11
  150.4 0.5 collective-permute-start.27
  150.9 2.7 %messages.6.refs_6_ = f32[2048,256]{1,0:T(8,128)S(1)} custom-call(bf16[512,4096]{1,0:T(8,128)(2,1)S(1)} %get-tuple-element.23.refs_0_, bf16[512,4096]{1,0:T(8,128)(2,1)S(1)} %copy-done.3, bf16[512,4096]{1,0:T(8,128)(2,1)S(1)} %get-tuple-element.25.refs_2_, bf16[512,4096]{1,0:T(8,128)(2,1)S(1)} %get-tuple-element.26.refs_3_, ...), custom_call_target="tpu_custom_call" | custom-call | flops 4294967296 | bytes 12582912 | tf_op jit(solution)/shard_map/messages/pallas_call | solution.py:249
  153.6 1.6 messages.10.own_ref
  155.4 1.5 collective-permute-start.28
  156.9 1.8 messages.7.own_ref
  158.9 0.6 collective-permute-start.24
  159.5 1.5 collective-permute-start.26
  161.0 9.3 %collective-permute-done.28.other_ref = bf16[1024,256]{1,0:T(8,128)(2,1)S(1)} collective-permute-done((bf16[1024,256]{1,0:T(8,128)(2,1)S(1)}, bf16[1024,256]{1,0:T(8,128)(2,1)S(1)}, u32[]{:S(2)}, u32[]{:S(2)}) %collective-permute-start.28) | collective-permute-done | bytes 524320 | tf_op jit(solution)/shard_map/ppermute | solution.py:342
  170.2 3.0 %mlp.3.refs_0_ = bf16[2048,256]{1,0:T(8,128)(2,1)} custom-call(s32[1]{0:T(128)} %bitcast.side, f32[1024,256]{1,0:T(8,128)S(1)} %messages.10.own_ref, bf16[1024,256]{1,0:T(8,128)(2,1)S(1)} %collective-permute-done.27.came_ref, bf16[1024,256]{1,0:T(8,128)(2,1)S(1)} %collective-permute-done.28.other_ref, f32[1,512]{1,0:T(1,128)S(1)} %bitcast.38, ...), custom_call_target="tpu_custom_call" | custom-call | flops 3221225472 | bytes 2097152 | tf_op jit(solution)/shard_map/mlp/pallas_call | solution.py:305
  173.3 7.3 %collective-permute-done.26.other_ref = bf16[512,256]{1,0:T(8,128)(2,1)S(1)} collective-permute-done((bf16[512,256]{1,0:T(8,128)(2,1)S(1)}, bf16[512,256]{1,0:T(8,128)(2,1)S(1)}, u32[]{:S(2)}, u32[]{:S(2)}) %collective-permute-start.26) | collective-permute-done | bytes 262176 | tf_op jit(solution)/shard_map/ppermute | solution.py:342
  180.5 2.0 %mlp.4.refs_0_ = bf16[2048,256]{1,0:T(8,128)(2,1)} custom-call(s32[1]{0:T(128)} %bitcast.side, f32[1024,256]{1,0:T(8,128)S(1)} %messages.7.own_ref, bf16[1024,256]{1,0:T(8,128)(2,1)S(1)} %collective-permute-done.23.came_ref, bf16[512,256]{1,0:T(8,128)(2,1)S(1)} %collective-permute-done.26.other_ref, ...), custom_call_target="tpu_custom_call", output_to_operand_aliasing={{}: (8, {})} | custom-call | flops 1610612736 | bytes 1048576 | tf_op jit(solution)/shard_map/mlp/pallas_call | solution.py:305
  182.5 2.0 %mlp.5 = bf16[2048,256]{1,0:T(8,128)(2,1)} custom-call(s32[1]{0:T(128)} %bitcast.side, f32[1024,256]{1,0:T(8,128)S(1)} %messages.7.own_ref, bf16[1024,256]{1,0:T(8,128)(2,1)S(1)} %collective-permute-done.23.came_ref, bf16[512,256]{1,0:T(8,128)(2,1)S(1)} %collective-permute-done.24.other_ref, f32[1,512]{1,0:T(1,128)S(1)} %bitcast.40, ...), custom_call_target="tpu_custom_call", output_to_operand_aliasing={{}: (8, {})} | custom-call | flops 1610612736 | bytes 1048576 | tf_op jit(solution)/shard_map/mlp/pallas_call | solution.py:305
  (87 shorter events, 2.3 us)
Async XLA Ops:
  0.0 18.8 %copy-start = (f32[4,512]{1,0:T(4,128)S(1)}, f32[4,512]{1,0:T(4,128)}, u32[]{:S(2)}) copy-start(f32[4,512]{1,0:T(4,128)} %param.19) | copy-start | bytes 24580
  0.0 18.8 %copy-start.14 = (f32[3,1]{0,1:T(1,128)S(1)}, f32[3,1]{0,1:T(1,128)}, u32[]{:S(2)}) copy-start(f32[3,1]{0,1:T(1,128)} %constant.51.clone) | copy-start | bytes 40
  0.0 18.8 %copy-start.13 = (s32[16]{0:T(128)S(1)}, s32[16]{0:T(128)}, u32[]{:S(2)}) copy-start(s32[16]{0:T(128)} %param.14) | copy-start | bytes 196
  0.0 18.7 %copy-start.8 = (bf16[512,512]{1,0:T(8,128)(2,1)S(1)}, bf16[512,512]{1,0:T(8,128)(2,1)}, u32[]{:S(2)}) copy-start(bf16[512,512]{1,0:T(8,128)(2,1)} %in_ref.5) | copy-start | bytes 1572868
  0.0 28.7 %collective-permute-start = (f32[3,2048]{1,0:T(4,128)}, f32[3,2048]{1,0:T(4,128)S(1)}, u32[]{:S(2)}, u32[]{:S(2)}) collective-permute-start(f32[3,2048]{1,0:T(4,128)} %param.16), channel_id=1, source_target_pairs={{0,1},{1,0},{2,3},{3,2},{4,5},{5,4},{6,7},{7,6},{8,9},{9,8},{10,11... | collective-permute-start | bytes 73736 | tf_op jit(solution)/shard_map/ppermute | solution.py:342
  4.5 14.4 %collective-permute-start.1 = (f32[8,2048]{1,0:T(8,128)S(1)}, f32[8,2048]{1,0:T(8,128)S(1)}, u32[]{:S(2)}, u32[]{:S(2)}) collective-permute-start(f32[8,2048]{1,0:T(8,128)S(1)} %select_maximum_fusion.2.own_pos), channel_id=1, source_target_pairs={{0,2},{2,0},{4,6},{6,4},{8,10},{10,8},{12,14},{14,12},{16,18},{18,... | collective-permute-start | bytes 196616 | tf_op jit(solution)/shard_map/ppermute | solution.py:347
  6.8 35.5 %copy-start.5 = (bf16[2048,256]{1,0:T(8,128)(2,1)}, bf16[2048,256]{1,0:T(8,128)(2,1)S(1)}, u32[]{:S(2)}) copy-start(bf16[2048,256]{1,0:T(8,128)(2,1)S(1)} %broadcast_select_fusion.own_ref) | copy-start | bytes 3145732
  6.8 27.7 %collective-permute-start.2 = (bf16[2048,256]{1,0:T(8,128)(2,1)S(1)}, bf16[2048,256]{1,0:T(8,128)(2,1)S(1)}, u32[]{:S(2)}, u32[]{:S(2)}) collective-permute-start(bf16[2048,256]{1,0:T(8,128)(2,1)S(1)} %broadcast_select_fusion.own_ref), channel_id=1, source_target_pairs={{0,2},{2,0},{4,6},{6,4},{8,10},{10,8},{12,14},{14,12},{16,18},{18,... | collective-permute-start | bytes 3145736 | tf_op jit(solution)/shard_map/ppermute | solution.py:347
  8.3 65.4 %collective-permute-start.6 = (f32[128,256]{1,0:T(8,128)S(1)}, f32[128,256]{1,0:T(8,128)}, u32[]{:S(2)}, u32[]{:S(2)}) collective-permute-start(f32[128,256]{1,0:T(8,128)S(1)} %get-tuple-element.30), channel_id=1, source_target_pairs={{0,1},{1,0},{2,3},{3,2},{4,5},{5,4},{6,7},{7,6},{8,9},{9,8},{10,11... | collective-permute-start | bytes 393224 | tf_op jit(solution)/shard_map/ppermute | solution.py:342
  9.2 15.2 %collective-permute-start.20 = (f32[3,256]{1,0:T(4,128)S(1)}, f32[3,256]{1,0:T(4,128)S(1)}, u32[]{:S(2)}, u32[]{:S(2)}) collective-permute-start(f32[3,256]{1,0:T(4,128)S(1)} %get-tuple-element.38), channel_id=1, source_target_pairs={{2,0},{4,2},{6,4},{8,6},{10,8},{12,10},{14,12},{16,14},{18,16},{20... | collective-permute-start | bytes 9224 | tf_op jit(solution)/shard_map/ppermute | solution.py:404
  20.1 3.7 %collective-permute-start.7 = (f32[8,128]{1,0:T(8,128)S(1)}, f32[8,128]{1,0:T(8,128)S(1)}, u32[]{:S(2)}, u32[]{:S(2)}) collective-permute-start(f32[8,128]{1,0:T(8,128)S(1)} %broadcast_in_dim.33), channel_id=1, source_target_pairs={{0,4},{2,6},{4,0},{6,2},{8,12},{10,14},{12,8},{14,10},{16,20},{18,... | collective-permute-start | bytes 12296 | tf_op jit(solution)/shard_map/ppermute | solution.py:347
  23.8 88.8 %collective-permute-start.19 = (f32[3,256]{1,0:T(4,128)S(1)}, f32[3,256]{1,0:T(4,128)S(1)}, u32[]{:S(2)}, u32[]{:S(2)}) collective-permute-start(f32[3,256]{1,0:T(4,128)S(1)} %get-tuple-element.37), channel_id=1, source_target_pairs={{0,2},{2,4},{4,6},{6,8},{8,10},{10,12},{12,14},{14,16},{16,18},{18... | collective-permute-start | bytes 9224 | tf_op jit(solution)/shard_map/ppermute | solution.py:403
  24.4 3.7 %collective-permute-start.8 = (f32[8,128]{1,0:T(8,128)S(1)}, f32[8,128]{1,0:T(8,128)S(1)}, u32[]{:S(2)}, u32[]{:S(2)}) collective-permute-start(f32[8,128]{1,0:T(8,128)S(1)} %broadcast_add_fusion.2), channel_id=1, source_target_pairs={{0,8},{2,10},{4,12},{6,14},{8,0},{10,2},{12,4},{14,6},{16,24},{18,... | collective-permute-start | bytes 12296 | tf_op jit(solution)/shard_map/ppermute | solution.py:347
  28.1 95.7 %collective-permute-start.21 = (bf16[256,256]{1,0:T(8,128)(2,1)S(1)}, bf16[256,256]{1,0:T(8,128)(2,1)S(1)}, u32[]{:S(2)}, u32[]{:S(2)}) collective-permute-start(bf16[256,256]{1,0:T(8,128)(2,1)S(1)} %bitcast.42), channel_id=1, source_target_pairs={{0,2},{2,4},{4,6},{6,8},{8,10},{10,12},{12,14},{14,16},{16,18},{18... | collective-permute-start | bytes 393224 | tf_op jit(solution)/shard_map/ppermute | solution.py:401
  28.7 4.6 %collective-permute-start.9 = (f32[8,128]{1,0:T(8,128)S(1)}, f32[8,128]{1,0:T(8,128)S(1)}, u32[]{:S(2)}, u32[]{:S(2)}) collective-permute-start(f32[8,128]{1,0:T(8,128)S(1)} %fusion.13), channel_id=1, source_target_pairs={{0,16},{2,18},{4,20},{6,22},{8,24},{10,26},{12,28},{14,30},{16,0},... | collective-permute-start | bytes 12296 | tf_op jit(solution)/shard_map/ppermute | solution.py:347
  34.5 7.8 %copy-start.9 = (bf16[2048,256]{1,0:T(8,128)(2,1)}, bf16[2048,256]{1,0:T(8,128)(2,1)S(1)}, u32[]{:S(2)}) copy-start(bf16[2048,256]{1,0:T(8,128)(2,1)S(1)} %collective-permute-done.2.other_ref) | copy-start | bytes 3145732
  42.3 31.1 %collective-permute-start.3 = (bf16[2,512,256]{2,1,0:T(8,128)(2,1)S(1)}, bf16[2,512,256]{2,1,0:T(8,128)(2,1)S(1)}, u32[]{:S(2)}, u32[]{:S(2)}) collective-permute-start(bf16[2,512,256]{2,1,0:T(8,128)(2,1)S(1)} %get-tuple-element.22), channel_id=1, source_target_pairs={{0,4},{2,6},{4,0},{6,2},{8,12},{10,14},{12,8},{14,10},{16,20},{18,... | collective-permute-start | bytes 1572872 | tf_op jit(solution)/shard_map/ppermute | solution.py:347
  42.8 1.2 copy-start.6
  44.0 1.2 copy-start.10
  45.3 9.4 %copy-start.7 = (bf16[2048,256]{1,0:T(8,128)(2,1)S(1)}, bf16[2048,256]{1,0:T(8,128)(2,1)}, u32[]{:S(2)}) copy-start(bf16[2048,256]{1,0:T(8,128)(2,1)} %copy-done.5) | copy-start | bytes 3145732
  53.1 17.4 %collective-permute-start.13 = (bf16[2,512,256]{2,1,0:T(8,128)(2,1)S(1)}, bf16[2,512,256]{2,1,0:T(8,128)(2,1)S(1)}, u32[]{:S(2)}, u32[]{:S(2)}) collective-permute-start(bf16[2,512,256]{2,1,0:T(8,128)(2,1)S(1)} %get-tuple-element.28), channel_id=1, source_target_pairs={{0,4},{2,6},{4,0},{6,2},{8,12},{10,14},{12,8},{14,10},{16,20},{18,... | collective-permute-start | bytes 1572872 | tf_op jit(solution)/shard_map/ppermute | solution.py:347
  70.5 68.1 %copy-start.2 = (bf16[512,4096]{1,0:T(8,128)(2,1)}, bf16[512,4096]{1,0:T(8,128)(2,1)S(1)}, u32[]{:S(2)}) copy-start(bf16[512,4096]{1,0:T(8,128)(2,1)S(1)} %get-tuple-element.24.refs_1_) | copy-start | bytes 12582916
  70.5 53.3 %collective-permute-start.22 = (bf16[256,256]{1,0:T(8,128)(2,1)S(1)}, bf16[256,256]{1,0:T(8,128)(2,1)S(1)}, u32[]{:S(2)}, u32[]{:S(2)}) collective-permute-start(bf16[256,256]{1,0:T(8,128)(2,1)S(1)} %bitcast.41), channel_id=1, source_target_pairs={{2,0},{4,2},{6,4},{8,6},{10,8},{12,10},{14,12},{16,14},{18,16},{20... | collective-permute-start | bytes 393224 | tf_op jit(solution)/shard_map/ppermute | solution.py:402
  73.4 9.2 %collective-permute-start.14 = (bf16[2,256,256]{2,1,0:T(8,128)(2,1)S(1)}, bf16[2,256,256]{2,1,0:T(8,128)(2,1)S(1)}, u32[]{:S(2)}, u32[]{:S(2)}) collective-permute-start(bf16[2,256,256]{2,1,0:T(8,128)(2,1)S(1)} %slice.129), channel_id=1, source_target_pairs={{0,8},{2,10},{4,12},{6,14},{8,0},{10,2},{12,4},{14,6},{16,24},{18,... | collective-permute-start | bytes 786440 | tf_op jit(solution)/shard_map/ppermute | solution.py:347
  73.5 41.7 %copy-start.12 = (f32[3,2048]{1,0:T(4,128)S(1)}, f32[3,2048]{1,0:T(4,128)}, u32[]{:S(2)}) copy-start(f32[3,2048]{1,0:T(4,128)} %param.13) | copy-start | bytes 73732
  73.7 50.1 %copy-start.4 = (bf16[2048,256]{1,0:T(8,128)(2,1)S(1)}, bf16[2048,256]{1,0:T(8,128)(2,1)}, u32[]{:S(2)}) copy-start(bf16[2048,256]{1,0:T(8,128)(2,1)} %feats_ref.3) | copy-start | bytes 3145732
  73.7 12.1 %collective-permute-start.4 = (bf16[2,256,256]{2,1,0:T(8,128)(2,1)S(1)}, bf16[2,256,256]{2,1,0:T(8,128)(2,1)S(1)}, u32[]{:S(2)}, u32[]{:S(2)}) collective-permute-start(bf16[2,256,256]{2,1,0:T(8,128)(2,1)S(1)} %slice.130), channel_id=1, source_target_pairs={{0,8},{2,10},{4,12},{6,14},{8,0},{10,2},{12,4},{14,6},{16,24},{18,... | collective-permute-start | bytes 786440 | tf_op jit(solution)/shard_map/ppermute | solution.py:347
  82.7 78.3 %collective-permute-start.25 = (bf16[512,768]{1,0:T(8,128)(2,1)S(1)}, bf16[512,768]{1,0:T(8,128)(2,1)S(1)}, u32[]{:S(2)}, u32[]{:S(2)}) collective-permute-start(bf16[512,768]{1,0:T(8,128)(2,1)S(1)} %pad_maximum_fusion), channel_id=1, source_target_pairs={{0,1},{1,0},{2,3},{3,2},{4,5},{5,4},{6,7},{7,6},{8,9},{9,8},{10,11... | collective-permute-start | bytes 2359304 | tf_op jit(solution)/shard_map/ppermute | solution.py:342
  85.8 9.3 %collective-permute-start.15 = (bf16[2,128,256]{2,1,0:T(8,128)(2,1)S(1)}, bf16[2,128,256]{2,1,0:T(8,128)(2,1)S(1)}, u32[]{:S(2)}, u32[]{:S(2)}) collective-permute-start(bf16[2,128,256]{2,1,0:T(8,128)(2,1)S(1)} %slice.131), channel_id=1, source_target_pairs={{0,16},{2,18},{4,20},{6,22},{8,24},{10,26},{12,28},{14,30},{16,0},... | collective-permute-start | bytes 393224 | tf_op jit(solution)/shard_map/ppermute | solution.py:347
  95.1 9.0 %collective-permute-start.5 = (bf16[2,128,256]{2,1,0:T(8,128)(2,1)S(1)}, bf16[2,128,256]{2,1,0:T(8,128)(2,1)S(1)}, u32[]{:S(2)}, u32[]{:S(2)}) collective-permute-start(bf16[2,128,256]{2,1,0:T(8,128)(2,1)S(1)} %slice.132), channel_id=1, source_target_pairs={{0,16},{2,18},{4,20},{6,22},{8,24},{10,26},{12,28},{14,30},{16,0},... | collective-permute-start | bytes 393224 | tf_op jit(solution)/shard_map/ppermute | solution.py:347
  104.1 8.5 %collective-permute-start.16 = (bf16[2,128,256]{2,1,0:T(8,128)(2,1)S(1)}, bf16[2,128,256]{2,1,0:T(8,128)(2,1)S(1)}, u32[]{:S(2)}, u32[]{:S(2)}) collective-permute-start(bf16[2,128,256]{2,1,0:T(8,128)(2,1)S(1)} %fusion.3), channel_id=1, source_target_pairs={{0,16},{2,18},{4,20},{6,22},{8,24},{10,26},{12,28},{14,30},{16,0},... | collective-permute-start | bytes 393224 | tf_op jit(solution)/shard_map/ppermute | solution.py:347
  112.6 7.0 %collective-permute-start.10 = (bf16[2,128,256]{2,1,0:T(8,128)(2,1)S(1)}, bf16[2,128,256]{2,1,0:T(8,128)(2,1)S(1)}, u32[]{:S(2)}, u32[]{:S(2)}) collective-permute-start(bf16[2,128,256]{2,1,0:T(8,128)(2,1)S(1)} %fusion.5), channel_id=1, source_target_pairs={{0,16},{2,18},{4,20},{6,22},{8,24},{10,26},{12,28},{14,30},{16,0},... | collective-permute-start | bytes 393224 | tf_op jit(solution)/shard_map/ppermute | solution.py:347
  112.6 11.0 %collective-permute-start.17 = (bf16[2,256,256]{2,1,0:T(8,128)(2,1)S(1)}, bf16[2,256,256]{2,1,0:T(8,128)(2,1)S(1)}, u32[]{:S(2)}, u32[]{:S(2)}) collective-permute-start(bf16[2,256,256]{2,1,0:T(8,128)(2,1)S(1)} %pad_maximum_fusion.4), channel_id=1, source_target_pairs={{0,8},{2,10},{4,12},{6,14},{8,0},{10,2},{12,4},{14,6},{16,24},{18,... | collective-permute-start | bytes 786440 | tf_op jit(solution)/shard_map/ppermute | solution.py:347
  119.7 8.7 %collective-permute-start.11 = (bf16[2,256,256]{2,1,0:T(8,128)(2,1)S(1)}, bf16[2,256,256]{2,1,0:T(8,128)(2,1)S(1)}, u32[]{:S(2)}, u32[]{:S(2)}) collective-permute-start(bf16[2,256,256]{2,1,0:T(8,128)(2,1)S(1)} %pad_maximum_fusion.3), channel_id=1, source_target_pairs={{0,8},{2,10},{4,12},{6,14},{8,0},{10,2},{12,4},{14,6},{16,24},{18,... | collective-permute-start | bytes 786440 | tf_op jit(solution)/shard_map/ppermute | solution.py:347
  123.7 14.9 %collective-permute-start.18 = (bf16[2,512,256]{2,1,0:T(8,128)(2,1)S(1)}, bf16[2,512,256]{2,1,0:T(8,128)(2,1)S(1)}, u32[]{:S(2)}, u32[]{:S(2)}) collective-permute-start(bf16[2,512,256]{2,1,0:T(8,128)(2,1)S(1)} %pad_maximum_fusion.2.refs_4_), channel_id=1, source_target_pairs={{0,4},{2,6},{4,0},{6,2},{8,12},{10,14},{12,8},{14,10},{16,20},{18,... | collective-permute-start | bytes 1572872 | tf_op jit(solution)/shard_map/ppermute | solution.py:347
  128.4 18.7 %collective-permute-start.12 = (bf16[2,512,256]{2,1,0:T(8,128)(2,1)S(1)}, bf16[2,512,256]{2,1,0:T(8,128)(2,1)S(1)}, u32[]{:S(2)}, u32[]{:S(2)}) collective-permute-start(bf16[2,512,256]{2,1,0:T(8,128)(2,1)S(1)} %pad_maximum_fusion.1.refs_4_), channel_id=1, source_target_pairs={{0,4},{2,6},{4,0},{6,2},{8,12},{10,14},{12,8},{14,10},{16,20},{18,... | collective-permute-start | bytes 1572872 | tf_op jit(solution)/shard_map/ppermute | solution.py:347
  148.7 2.3 %copy-start.3 = (bf16[512,4096]{1,0:T(8,128)(2,1)S(1)}, bf16[512,4096]{1,0:T(8,128)(2,1)}, u32[]{:S(2)}) copy-start(bf16[512,4096]{1,0:T(8,128)(2,1)} %copy-done.2) | copy-start | bytes 12582916
  148.7 10.1 %collective-permute-start.23 = (bf16[1024,256]{1,0:T(8,128)(2,1)S(1)}, bf16[1024,256]{1,0:T(8,128)(2,1)S(1)}, u32[]{:S(2)}, u32[]{:S(2)}) collective-permute-start(bf16[1024,256]{1,0:T(8,128)(2,1)S(1)} %messages.9), channel_id=1, source_target_pairs={{0,2},{2,0},{4,6},{6,4},{8,10},{10,8},{12,14},{14,12},{16,18},{18,... | collective-permute-start | bytes 1572872 | tf_op jit(solution)/shard_map/ppermute | solution.py:347
  150.4 4.9 %collective-permute-start.27 = (bf16[1024,256]{1,0:T(8,128)(2,1)S(1)}, bf16[1024,256]{1,0:T(8,128)(2,1)S(1)}, u32[]{:S(2)}, u32[]{:S(2)}) collective-permute-start(bf16[1024,256]{1,0:T(8,128)(2,1)S(1)} %messages.11), channel_id=1, source_target_pairs={{0,2},{2,0},{4,6},{6,4},{8,10},{10,8},{12,14},{14,12},{16,18},{18,... | collective-permute-start | bytes 1572872 | tf_op jit(solution)/shard_map/ppermute | solution.py:347
  155.4 14.9 %copy-start.11 = (f32[512]{0:T(512)S(1)}, f32[512]{0:T(512)}, u32[]{:S(2)}) copy-start(f32[512]{0:T(512)} %param.20) | copy-start | bytes 6148
  155.4 14.9 %collective-permute-start.28 = (bf16[1024,256]{1,0:T(8,128)(2,1)S(1)}, bf16[1024,256]{1,0:T(8,128)(2,1)S(1)}, u32[]{:S(2)}, u32[]{:S(2)}) collective-permute-start(bf16[1024,256]{1,0:T(8,128)(2,1)S(1)} %add_convert_fusion), channel_id=1, source_target_pairs={{0,1},{1,0},{2,3},{3,2},{4,5},{5,4},{6,7},{7,6},{8,9},{9,8},{10,11... | collective-permute-start | bytes 1572872 | tf_op jit(solution)/shard_map/ppermute | solution.py:342
  158.9 23.6 %collective-permute-start.24 = (bf16[512,256]{1,0:T(8,128)(2,1)S(1)}, bf16[512,256]{1,0:T(8,128)(2,1)S(1)}, u32[]{:S(2)}, u32[]{:S(2)}) collective-permute-start(bf16[512,256]{1,0:T(8,128)(2,1)S(1)} %get-tuple-element.32), channel_id=1, source_target_pairs={{0,1},{1,0},{2,3},{3,2},{4,5},{5,4},{6,7},{7,6},{8,9},{9,8},{10,11... | collective-permute-start | bytes 786440 | tf_op jit(solution)/shard_map/ppermute | solution.py:342
  159.5 21.0 %collective-permute-start.26 = (bf16[512,256]{1,0:T(8,128)(2,1)S(1)}, bf16[512,256]{1,0:T(8,128)(2,1)S(1)}, u32[]{:S(2)}, u32[]{:S(2)}) collective-permute-start(bf16[512,256]{1,0:T(8,128)(2,1)S(1)} %get-tuple-element.31), channel_id=1, source_target_pairs={{0,1},{1,0},{2,3},{3,2},{4,5},{5,4},{6,7},{7,6},{8,9},{9,8},{10,11... | collective-permute-start | bytes 786440 | tf_op jit(solution)/shard_map/ppermute | solution.py:342
  180.5 4.0 %copy-start.1 = (f32[4,512]{1,0:T(4,128)S(1)}, f32[4,512]{1,0:T(4,128)}, u32[]{:S(2)}) copy-start(f32[4,512]{1,0:T(4,128)} %param.19) | copy-start | bytes 24580

commit v5 on v4

--- a/solution.py
+++ b/solution.py
@@ -10,11 +10,11 @@
 
 EPS = 1e-06
 HW = 2
-SHARES = ((1.0,), (1.0,))
-GROUPS = (1,)
+SHARES = ((1.0,), (0.5, 0.5))
+GROUPS = (1, 1)
 TILE = 256
 FORWARD_ROWS = 256
-LIMIT = pltpu.CompilerParams(vmem_limit_bytes=16 << 20)
+LIMIT = pltpu.CompilerParams(vmem_limit_bytes=8 << 20)
 
 SIN_1, SIN_0, SIN_BY = -8.313817368817206, 20.224572228345814, 12.875426983082301
 COS_ROOT, COS_1, COS_0 = 0.9993568028372194, -11.426868481113639, 49.031109066681445
@@ -101,7 +101,7 @@
 def forward(places, waves, positions, feats, start, position, count, block_rows, dtype):
     depth = waves.shape[0]
     atom_rows, width = feats[0].shape
-    tile = min(FORWARD_ROWS, count)
+    tile = min(FORWARD_ROWS, count // 2)
     trig = pltpu.VMEM((count, 2 * atom_rows), jnp.bfloat16)
     return pl.pallas_call(
         functools.partial(forward_body, start, position // block_rows, block_rows),
@@ -412,7 +412,7 @@
         row = core * own_waves + start + reverse * (rows // group)
         return lax.dynamic_slice(filters, (row, whose * width), (rows // group, width))
 
-    unit = 32 * group
+    unit = 16 * group
     splits = []
     for shares in SHARES:
         begin, pieces_of_half = 0, []
@@ -518,7 +518,7 @@
         send = backward(last, atom_rows + half * half_rows, half_rows, tile, (other, half * half_rows), bf16)
         came = across(send, core_bit)
         part = backward(last, half * half_rows, half_rows, tile, (mine, half * half_rows), f32)
-        pieces = 1 if half == 0 else 2
+        pieces = 1
         piece_rows = half_rows // pieces
         for piece in range(pieces):
             rows_of = slice(piece * piece_rows, (piece + 1) * piece_rows)

time: 185 us -> 192 us (1.038)
  Pallas kernels: 57 us -> 70.1 us
  waiting for transfers between devices: 81.4 us -> 74.2 us
  starting transfers between devices: 27 us -> 29.5 us
    ppermute x19 -> x25, waiting for transfers between devices: 64.9 us -> 50.5 us  [across(): return lax.ppermute(value, 'cells', [(i, i ^ bit) for i in range(count)])]
    pallas_call x4 -> x6, Pallas kernels: 31.4 us -> 44.3 us  [forward(): pl.pallas_call(functools.partial(forward_body, start, position // block_r...]
    ppermute x19 -> x25, starting transfers between devices: 11.3 us -> 18.2 us  [across(): return lax.ppermute(value, 'cells', [(i, i ^ bit) for i in range(count)])]
    ppermute x1, waiting for transfers between devices: 0.01 us -> 4.94 us  [shards(): left_pos = lax.ppermute(positions[:, atom_rows - edge:], 'cells', to_right)]
    ppermute x1, starting transfers between devices: 2.77 us -> 0.01 us  [shards(): right_feats = lax.ppermute(masked[:edge], 'cells', to_left)]
    ppermute x6 -> x5, waiting for transfers between devices: 16.5 us -> 18.7 us  [swap(): return lax.ppermute(value, 'waves', [(0, 1), (1, 0)])]
    ppermute x6 -> x5, starting transfers between devices: 8.31 us -> 6.85 us  [swap(): return lax.ppermute(value, 'waves', [(0, 1), (1, 0)])]
    pallas_call x6 -> x8, Pallas kernels: 12.1 us -> 13.2 us  [backward(): pl.pallas_call(functools.partial(backward_body, len(parts), first, tile,...]
  transfers between devices with their start and end apart: 29 -> 34, of which waited for: 15 -> 15; matrix products, arithmetic and copies ran while one was open for 8% -> 7% of each run, Pallas kernels for 30% -> 35%
where the time goes in v5:
time: 192 us; the launch traced here: 191 us
  waiting for transfers between devices  74.2 us (39%)
  Pallas kernels  70.1 us (37%)
  starting transfers between devices  29.5 us (15%)
  other arithmetic  9.67 us (5%)
  local copies, waits for them, and re-layouts  6.21 us (3%)
    ppermute x25, waiting for transfers between devices, across(): return lax.ppermute(value, 'cells', [(i, i ^ bit) for i in range(count)])  50.5 us
    pallas_call x6, Pallas kernels, forward(): pl.pallas_call(functools.partial(forward_body, start, position // block_r...  44.3 us
    ppermute x5, waiting for transfers between devices, swap(): return lax.ppermute(value, 'waves', [(0, 1), (1, 0)])  18.7 us
    ppermute x25, starting transfers between devices, across(): return lax.ppermute(value, 'cells', [(i, i ^ bit) for i in range(count)])  18.2 us
    pallas_call x8, Pallas kernels, backward(): pl.pallas_call(functools.partial(backward_body, len(parts), first, tile,...  13.2 us
    ppermute x5, starting transfers between devices, swap(): return lax.ppermute(value, 'waves', [(0, 1), (1, 0)])  6.85 us
    pallas_call x2, Pallas kernels, near_part(): pl.pallas_call(functools.partial(near_body, base), grid_spec=pltpu.Prefet...  6.54 us
    pallas_call x2, Pallas kernels, mlp(): pl.pallas_call(mlp_body, grid_spec=pltpu.PrefetchScalarGridSpec(num_scala...  6.12 us
  transfers between devices with their start and end apart: 34, of which 15 were waited for; matrix products, arithmetic and copies ran while one was open for 7% of the time, Pallas kernels for 35%

profile of v5, /device:TPU:0, one launch (start us, length us, event | category | flops | bytes accessed | tf_op | source)
XLA Modules:
  0.0 191.1 jit_solution(17969365930052526786)
XLA Ops:
  0.0 3.0 %collective-permute-start = (f32[3,2048]{1,0:T(4,128)}, f32[3,2048]{1,0:T(4,128)S(1)}, u32[]{:S(2)}, u32[]{:S(2)}) collective-permute-start(f32[3,2048]{1,0:T(4,128)} %param.16), channel_id=1, source_target_pairs={{0,1},{1,0},{2,3},{3,2},{4,5},{5,4},{6,7},{7,6},{8,9},{9,8},{10,11... | collective-permute-start | bytes 73736 | tf_op jit(solution)/shard_map/ppermute | solution.py:342
  3.1 0.7 convert_bitcast_fusion
  3.7 0.8 select_maximum_fusion.2.own_pos
  4.6 0.7 iota_compare_fusion.2
  5.3 2.3 %broadcast_select_fusion.own_ref = bf16[2048,256]{1,0:T(8,128)(2,1)} fusion(bf16[2048,256]{1,0:T(8,128)(2,1)} %feats_ref.3, pred[2048]{0:T(1024)(128)(4,1)S(1)} %get-tuple-element.52), kind=kLoop, calls=%fused_computation.3 | loop fusion | flops 524288 | bytes 2099200 | tf_op jit(solution)/shard_map/jit(_where)/select_n | solution.py:379
  7.6 0.5 collective-permute-start.2
  8.1 0.9 fusion.10
  9.2 4.4 %collective-permute-start.26 = (f32[3,256]{1,0:T(4,128)S(1)}, f32[3,256]{1,0:T(4,128)S(1)}, u32[]{:S(2)}, u32[]{:S(2)}) collective-permute-start(f32[3,256]{1,0:T(4,128)S(1)} %get-tuple-element.50), channel_id=1, source_target_pairs={{2,0},{4,2},{6,4},{8,6},{10,8},{12,10},{14,12},{16,14},{18,16},{20... | collective-permute-start | bytes 9224 | tf_op jit(solution)/shard_map/ppermute | solution.py:404
  13.7 0.6 broadcast_multiply_fusion.5.scales
  14.3 0.4 broadcast_select_fusion.1.masked_ref
  14.8 1.0 copy-done.3
  15.9 0.9 pad_maximum_fusion
  16.9 0.9 dynamic_slice.20
  18.0 0.7 fusion.8
  18.7 4.9 %collective-permute-done.25 = f32[3,256]{1,0:T(4,128)S(1)} collective-permute-done((f32[3,256]{1,0:T(4,128)S(1)}, f32[3,256]{1,0:T(4,128)S(1)}, u32[]{:S(2)}, u32[]{:S(2)}) %collective-permute-start.25) | collective-permute-done | bytes 3104 | tf_op jit(solution)/shard_map/ppermute | solution.py:403
  23.6 0.6 broadcast_in_dim.34
  24.4 3.5 %collective-permute-done.7 = f32[8,128]{1,0:T(8,128)S(1)} collective-permute-done((f32[8,128]{1,0:T(8,128)S(1)}, f32[8,128]{1,0:T(8,128)S(1)}, u32[]{:S(2)}, u32[]{:S(2)}) %collective-permute-start.7) | collective-permute-done | bytes 4128 | tf_op jit(solution)/shard_map/ppermute | solution.py:347
  27.9 0.6 broadcast_add_fusion.2
  28.6 3.6 %collective-permute-done.8 = f32[8,128]{1,0:T(8,128)S(1)} collective-permute-done((f32[8,128]{1,0:T(8,128)S(1)}, f32[8,128]{1,0:T(8,128)S(1)}, u32[]{:S(2)}, u32[]{:S(2)}) %collective-permute-start.8) | collective-permute-done | bytes 4128 | tf_op jit(solution)/shard_map/ppermute | solution.py:347
  32.2 0.6 fusion.14
  33.0 4.5 %collective-permute-done.9 = f32[8,128]{1,0:T(8,128)S(1)} collective-permute-done((f32[8,128]{1,0:T(8,128)S(1)}, f32[8,128]{1,0:T(8,128)S(1)}, u32[]{:S(2)}, u32[]{:S(2)}) %collective-permute-start.9) | collective-permute-done | bytes 4128 | tf_op jit(solution)/shard_map/ppermute | solution.py:347
  37.4 1.5 collective-permute-start.31
  38.9 0.6 slice.79
  40.5 1.2 copy-done.4
  41.7 0.7 copy-done.11
  42.4 3.3 %near.2.refs_0_ = f32[2048,256]{1,0:T(8,128)S(1)} custom-call(s32[16,3]{1,0:T(8,128)S(1)} %broadcast_add_fusion.places, f32[4]{0:T(128)S(1)} %copy-done.11, f32[20,8,128]{2,1,0:T(8,128)S(1)} %fusion.6.row_ref, bf16[2,128,256]{2,1,0:T(8,128)(2,1)S(1)} %bitcast.34, bf16[16,128,256]{2,1,0:T(8,128)(2,1)S(1)} %copy-done.4, bf16[2,128,256]{2,1,0:T(8,128)(2,1)S(1)} %bitcast.36, ...), custom_call_target="tpu_custom_call" | custom-call | flops 3221225472 | bytes 2097152 | tf_op jit(solution)/shard_map/near/pallas_call | solution.py:186
  45.7 6.4 %structure.7 = (bf16[256,4096]{1,0:T(8,128)(2,1)S(1)}, bf16[256,4096]{1,0:T(8,128)(2,1)S(1)}, bf16[2,256,256]{2,1,0:T(8,128)(2,1)S(1)}) custom-call(s32[2]{0:T(128)S(1)} %pad_add_fusion.places, f32[8,2048]{1,0:T(8,128)S(1)} %pad.15.waves_ref, f32[8,2048]{1,0:T(8,128)S(1)} %select_maximum_fusion.2.own_pos, f32[8,2048]{1,0:T(8,128)S(1)} %copy-done.9, ...), custom_call_target="tpu_custom_call" | custom-call | flops 2415919104 | bytes 4194304 | tf_op jit(solution)/shard_map/structure/pallas_call | solution.py:106
  52.1 6.3 %structure.9 = (bf16[256,4096]{1,0:T(8,128)(2,1)S(1)}, bf16[256,4096]{1,0:T(8,128)(2,1)S(1)}, bf16[2,256,256]{2,1,0:T(8,128)(2,1)S(1)}) custom-call(s32[2]{0:T(128)S(1)} %pad_add_fusion.places, f32[8,2048]{1,0:T(8,128)S(1)} %pad.15.waves_ref, f32[8,2048]{1,0:T(8,128)S(1)} %select_maximum_fusion.2.own_pos, f32[8,2048]{1,0:T(8,128)S(1)} %copy-done.9, ...), custom_call_target="tpu_custom_call" | custom-call | flops 2415919104 | bytes 4194304 | tf_op jit(solution)/shard_map/structure/pallas_call | solution.py:106
  58.5 2.1 %collective-permute-start.13 = (bf16[2,256,256]{2,1,0:T(8,128)(2,1)S(1)}, bf16[2,256,256]{2,1,0:T(8,128)(2,1)S(1)}, u32[]{:S(2)}, u32[]{:S(2)}) collective-permute-start(bf16[2,256,256]{2,1,0:T(8,128)(2,1)S(1)} %get-tuple-element.34), channel_id=1, source_target_pairs={{0,4},{2,6},{4,0},{6,2},{8,12},{10,14},{12,8},{14,10},{16,20},{18,... | collective-permute-start | bytes 786440 | tf_op jit(solution)/shard_map/ppermute | solution.py:347
  60.6 9.3 %structure.11 = (bf16[512,4096]{1,0:T(8,128)(2,1)S(1)}, bf16[512,4096]{1,0:T(8,128)(2,1)S(1)}, bf16[2,512,256]{2,1,0:T(8,128)(2,1)S(1)}) custom-call(s32[2]{0:T(128)S(1)} %pad_add_fusion.places, f32[8,2048]{1,0:T(8,128)S(1)} %pad.17.waves_ref, f32[8,2048]{1,0:T(8,128)S(1)} %select_maximum_fusion.2.own_pos, f32[8,2048]{1,0:T(8,128)S(1)} %copy-done.9, ...), custom_call_target="tpu_custom_call" | custom-call | flops 4831838208 | bytes 8388608 | tf_op jit(solution)/shard_map/structure/pallas_call | solution.py:106
  70.0 9.3 %structure.10 = (bf16[512,4096]{1,0:T(8,128)(2,1)S(1)}, bf16[512,4096]{1,0:T(8,128)(2,1)S(1)}, f32[2,512,256]{2,1,0:T(8,128)S(1)}) custom-call(s32[2]{0:T(128)S(1)} %pad_add_fusion.places, f32[8,2048]{1,0:T(8,128)S(1)} %pad.17.waves_ref, f32[8,2048]{1,0:T(8,128)S(1)} %select_maximum_fusion.2.own_pos, f32[8,2048]{1,0:T(8,128)S(1)} %copy-done.9, ...), custom_call_target="tpu_custom_call" | custom-call | flops 4831838208 | bytes 8388608 | tf_op jit(solution)/shard_map/structure/pallas_call | solution.py:106
  79.3 6.5 %structure.6 = (bf16[256,4096]{1,0:T(8,128)(2,1)S(1)}, bf16[256,4096]{1,0:T(8,128)(2,1)S(1)}, f32[2,256,256]{2,1,0:T(8,128)S(1)}) custom-call(s32[2]{0:T(128)S(1)} %pad_add_fusion.places, f32[8,2048]{1,0:T(8,128)S(1)} %pad.15.waves_ref, f32[8,2048]{1,0:T(8,128)S(1)} %select_maximum_fusion.2.own_pos, f32[8,2048]{1,0:T(8,128)S(1)} %copy-done.9, ...), custom_call_target="tpu_custom_call" | custom-call | flops 2415919104 | bytes 4194304 | tf_op jit(solution)/shard_map/structure/pallas_call | solution.py:106
  85.9 6.4 %structure.8 = (bf16[256,4096]{1,0:T(8,128)(2,1)S(1)}, bf16[256,4096]{1,0:T(8,128)(2,1)S(1)}, f32[2,256,256]{2,1,0:T(8,128)S(1)}) custom-call(s32[2]{0:T(128)S(1)} %pad_add_fusion.places, f32[8,2048]{1,0:T(8,128)S(1)} %pad.15.waves_ref, f32[8,2048]{1,0:T(8,128)S(1)} %select_maximum_fusion.2.own_pos, f32[8,2048]{1,0:T(8,128)S(1)} %copy-done.9, ...), custom_call_target="tpu_custom_call" | custom-call | flops 2415919104 | bytes 4194304 | tf_op jit(solution)/shard_map/structure/pallas_call | solution.py:106
  92.6 2.1 %collective-permute-start.20 = (bf16[2,256,256]{2,1,0:T(8,128)(2,1)S(1)}, bf16[2,256,256]{2,1,0:T(8,128)(2,1)S(1)}, u32[]{:S(2)}, u32[]{:S(2)}) collective-permute-start(bf16[2,256,256]{2,1,0:T(8,128)(2,1)S(1)} %slice.141), channel_id=1, source_target_pairs={{0,8},{2,10},{4,12},{6,14},{8,0},{10,2},{12,4},{14,6},{16,24},{18,... | collective-permute-start | bytes 786440 | tf_op jit(solution)/shard_map/ppermute | solution.py:347
  94.8 4.7 %collective-permute-done.4 = bf16[2,128,256]{2,1,0:T(8,128)(2,1)S(1)} collective-permute-done((bf16[2,128,256]{2,1,0:T(8,128)(2,1)S(1)}, bf16[2,128,256]{2,1,0:T(8,128)(2,1)S(1)}, u32[]{:S(2)}, u32[]{:S(2)}) %collective-permute-start.4) | collective-permute-done | bytes 131104 | tf_op jit(solution)/shard_map/ppermute | solution.py:347
  99.6 4.5 %collective-permute-done.20 = bf16[2,256,256]{2,1,0:T(8,128)(2,1)S(1)} collective-permute-done((bf16[2,256,256]{2,1,0:T(8,128)(2,1)S(1)}, bf16[2,256,256]{2,1,0:T(8,128)(2,1)S(1)}, u32[]{:S(2)}, u32[]{:S(2)}) %collective-permute-start.20) | collective-permute-done | bytes 262176 | tf_op jit(solution)/shard_map/ppermute | solution.py:347
  104.6 2.3 %collective-permute-done.14 = bf16[2,128,256]{2,1,0:T(8,128)(2,1)S(1)} collective-permute-done((bf16[2,128,256]{2,1,0:T(8,128)(2,1)S(1)}, bf16[2,128,256]{2,1,0:T(8,128)(2,1)S(1)}, u32[]{:S(2)}, u32[]{:S(2)}) %collective-permute-start.14) | collective-permute-done | bytes 131104 | tf_op jit(solution)/shard_map/ppermute | solution.py:347
  107.4 7.8 %collective-permute-done.21 = bf16[2,128,256]{2,1,0:T(8,128)(2,1)S(1)} collective-permute-done((bf16[2,128,256]{2,1,0:T(8,128)(2,1)S(1)}, bf16[2,128,256]{2,1,0:T(8,128)(2,1)S(1)}, u32[]{:S(2)}, u32[]{:S(2)}) %collective-permute-start.21) | collective-permute-done | bytes 131104 | tf_op jit(solution)/shard_map/ppermute | solution.py:347
  115.3 3.0 %collective-permute-start.10 = (bf16[2,64,256]{2,1,0:T(8,128)(2,1)S(1)}, bf16[2,64,256]{2,1,0:T(8,128)(2,1)S(1)}, u32[]{:S(2)}, u32[]{:S(2)}) collective-permute-start(bf16[2,64,256]{2,1,0:T(8,128)(2,1)S(1)} %fusion.5), channel_id=1, source_target_pairs={{0,16},{2,18},{4,20},{6,22},{8,24},{10,26},{12,28},{14,30},{16,0},... | collective-permute-start | bytes 196616 | tf_op jit(solution)/shard_map/ppermute | solution.py:347
  118.3 4.4 %collective-permute-done.22 = bf16[2,128,256]{2,1,0:T(8,128)(2,1)S(1)} collective-permute-done((bf16[2,128,256]{2,1,0:T(8,128)(2,1)S(1)}, bf16[2,128,256]{2,1,0:T(8,128)(2,1)S(1)}, u32[]{:S(2)}, u32[]{:S(2)}) %collective-permute-start.22) | collective-permute-done | bytes 131104 | tf_op jit(solution)/shard_map/ppermute | solution.py:347
  122.8 2.4 %collective-permute-start.16 = (bf16[2,64,256]{2,1,0:T(8,128)(2,1)S(1)}, bf16[2,64,256]{2,1,0:T(8,128)(2,1)S(1)}, u32[]{:S(2)}, u32[]{:S(2)}) collective-permute-start(bf16[2,64,256]{2,1,0:T(8,128)(2,1)S(1)} %fusion.3), channel_id=1, source_target_pairs={{0,16},{2,18},{4,20},{6,22},{8,24},{10,26},{12,28},{14,30},{16,0},... | collective-permute-start | bytes 196616 | tf_op jit(solution)/shard_map/ppermute | solution.py:347
  125.3 5.2 %collective-permute-done.16 = bf16[2,64,256]{2,1,0:T(8,128)(2,1)S(1)} collective-permute-done((bf16[2,64,256]{2,1,0:T(8,128)(2,1)S(1)}, bf16[2,64,256]{2,1,0:T(8,128)(2,1)S(1)}, u32[]{:S(2)}, u32[]{:S(2)}) %collective-permute-start.16) | collective-permute-done | bytes 65568 | tf_op jit(solution)/shard_map/ppermute | solution.py:347
  130.5 1.7 collective-permute-start.17
  132.1 0.5 collective-permute-done.23
  132.7 2.1 %collective-permute-start.24 = (bf16[2,512,256]{2,1,0:T(8,128)(2,1)S(1)}, bf16[2,512,256]{2,1,0:T(8,128)(2,1)S(1)}, u32[]{:S(2)}, u32[]{:S(2)}) collective-permute-start(bf16[2,512,256]{2,1,0:T(8,128)(2,1)S(1)} %pad_maximum_fusion.1.refs_4_), channel_id=1, source_target_pairs={{0,4},{2,6},{4,0},{6,2},{8,12},{10,14},{12,8},{14,10},{16,20},{18,... | collective-permute-start | bytes 1572872 | tf_op jit(solution)/shard_map/ppermute | solution.py:347
  134.8 3.3 %near.3.refs_6_ = f32[2048,256]{1,0:T(8,128)S(1)} custom-call(s32[16,3]{1,0:T(8,128)S(1)} %broadcast_add_fusion.places, f32[4]{0:T(128)S(1)} %copy-done.12, f32[20,8,128]{2,1,0:T(8,128)S(1)} %fusion.6.row_ref, bf16[2,128,256]{2,1,0:T(8,128)(2,1)S(1)} %bitcast.35, bf16[16,128,256]{2,1,0:T(8,128)(2,1)S(1)} %copy-done.5, ...), custom_call_target="tpu_custom_call", output_to_operand_aliasing={{}: (8, {})} | custom-call | flops 3221225472 | bytes 2097152 | tf_op jit(solution)/shard_map/near/pallas_call | solution.py:186
  138.2 2.1 %collective-permute-start.18 = (bf16[2,256,256]{2,1,0:T(8,128)(2,1)S(1)}, bf16[2,256,256]{2,1,0:T(8,128)(2,1)S(1)}, u32[]{:S(2)}, u32[]{:S(2)}) collective-permute-start(bf16[2,256,256]{2,1,0:T(8,128)(2,1)S(1)} %pad_maximum_fusion.3.refs_4_), channel_id=1, source_target_pairs={{0,4},{2,6},{4,0},{6,2},{8,12},{10,14},{12,8},{14,10},{16,20},{18,... | collective-permute-start | bytes 786440 | tf_op jit(solution)/shard_map/ppermute | solution.py:347
  140.3 6.8 %collective-permute-done.24.refs_5_ = bf16[2,512,256]{2,1,0:T(8,128)(2,1)S(1)} collective-permute-done((bf16[2,512,256]{2,1,0:T(8,128)(2,1)S(1)}, bf16[2,512,256]{2,1,0:T(8,128)(2,1)S(1)}, u32[]{:S(2)}, u32[]{:S(2)}) %collective-permute-start.24) | collective-permute-done | bytes 524320 | tf_op jit(solution)/shard_map/ppermute | solution.py:347
  147.1 2.8 %messages.11.refs_6_ = f32[2048,256]{1,0:T(8,128)S(1)} custom-call(bf16[512,4096]{1,0:T(8,128)(2,1)S(1)} %get-tuple-element.35.refs_0_, bf16[512,4096]{1,0:T(8,128)(2,1)S(1)} %get-tuple-element.36.refs_1_, bf16[512,4096]{1,0:T(8,128)(2,1)S(1)} %get-tuple-element.37.refs_2_, bf16[512,4096]{1,0:T(8,128)(2,1)S(1)} %get-tuple-element.38.refs_3_, ...), custom_call_target="tpu_custom_call" | custom-call | flops 4294967296 | bytes 12582912 | tf_op jit(solution)/shard_map/messages/pallas_call | solution.py:249
  150.0 2.8 %collective-permute-done.18.refs_5_ = bf16[2,256,256]{2,1,0:T(8,128)(2,1)S(1)} collective-permute-done((bf16[2,256,256]{2,1,0:T(8,128)(2,1)S(1)}, bf16[2,256,256]{2,1,0:T(8,128)(2,1)S(1)}, u32[]{:S(2)}, u32[]{:S(2)}) %collective-permute-start.18) | collective-permute-done | bytes 262176 | tf_op jit(solution)/shard_map/ppermute | solution.py:347
  152.7 1.6 messages.12.refs_6_
  154.4 1.0 messages.13
  155.5 1.0 messages.15
  156.5 0.5 collective-permute-start.32
  157.1 2.8 %messages.8.refs_6_ = f32[2048,256]{1,0:T(8,128)S(1)} custom-call(bf16[512,4096]{1,0:T(8,128)(2,1)S(1)} %get-tuple-element.35.refs_0_, bf16[512,4096]{1,0:T(8,128)(2,1)S(1)} %get-tuple-element.36.refs_1_, bf16[512,4096]{1,0:T(8,128)(2,1)S(1)} %get-tuple-element.37.refs_2_, bf16[512,4096]{1,0:T(8,128)(2,1)S(1)} %get-tuple-element.38.refs_3_, ...), custom_call_target="tpu_custom_call" | custom-call | flops 4294967296 | bytes 12582912 | tf_op jit(solution)/shard_map/messages/pallas_call | solution.py:249
  159.8 1.8 messages.9.refs_6_
  161.7 1.0 messages.14.own_ref
  162.9 0.6 collective-permute-start.33
  163.5 1.0 messages.10.own_ref
  164.7 1.5 collective-permute-start.30
  166.2 11.5 %collective-permute-done.33.other_ref = bf16[1024,256]{1,0:T(8,128)(2,1)S(1)} collective-permute-done((bf16[1024,256]{1,0:T(8,128)(2,1)S(1)}, bf16[1024,256]{1,0:T(8,128)(2,1)S(1)}, u32[]{:S(2)}, u32[]{:S(2)}) %collective-permute-start.33) | collective-permute-done | bytes 524320 | tf_op jit(solution)/shard_map/ppermute | solution.py:342
  177.7 3.1 %mlp.2.refs_0_ = bf16[2048,256]{1,0:T(8,128)(2,1)} custom-call(s32[1]{0:T(128)} %bitcast.side, f32[1024,256]{1,0:T(8,128)S(1)} %messages.14.own_ref, bf16[1024,256]{1,0:T(8,128)(2,1)S(1)} %collective-permute-done.32.came_ref, bf16[1024,256]{1,0:T(8,128)(2,1)S(1)} %collective-permute-done.33.other_ref, f32[1,512]{1,0:T(1,128)S(1)} %bitcast.38, ...), custom_call_target="tpu_custom_call" | custom-call | flops 3221225472 | bytes 2097152 | tf_op jit(solution)/shard_map/mlp/pallas_call | solution.py:305
  180.8 7.2 %collective-permute-done.30.other_ref = bf16[1024,256]{1,0:T(8,128)(2,1)S(1)} collective-permute-done((bf16[1024,256]{1,0:T(8,128)(2,1)S(1)}, bf16[1024,256]{1,0:T(8,128)(2,1)S(1)}, u32[]{:S(2)}, u32[]{:S(2)}) %collective-permute-start.30) | collective-permute-done | bytes 524320 | tf_op jit(solution)/shard_map/ppermute | solution.py:342
  188.0 3.1 %mlp.3 = bf16[2048,256]{1,0:T(8,128)(2,1)} custom-call(s32[1]{0:T(128)} %bitcast.side, f32[1024,256]{1,0:T(8,128)S(1)} %messages.10.own_ref, bf16[1024,256]{1,0:T(8,128)(2,1)S(1)} %collective-permute-done.29.came_ref, bf16[1024,256]{1,0:T(8,128)(2,1)S(1)} %collective-permute-done.30.other_ref, ...), custom_call_target="tpu_custom_call", output_to_operand_aliasing={{}: (8, {})} | custom-call | flops 3221225472 | bytes 2097152 | tf_op jit(solution)/shard_map/mlp/pallas_call | solution.py:305
  (121 shorter events, 3.9 us)
Async XLA Ops:
  0.0 15.7 %copy-start = (f32[4,512]{1,0:T(4,128)S(1)}, f32[4,512]{1,0:T(4,128)}, u32[]{:S(2)}) copy-start(f32[4,512]{1,0:T(4,128)} %param.19) | copy-start | bytes 24580
  0.0 13.5 %copy-start.15 = (f32[3,2048]{1,0:T(4,128)S(1)}, f32[3,2048]{1,0:T(4,128)}, u32[]{:S(2)}) copy-start(f32[3,2048]{1,0:T(4,128)} %param.16) | copy-start | bytes 73732
  0.0 9.1 %copy-start.14 = (f32[3,2048]{1,0:T(4,128)S(1)}, f32[3,2048]{1,0:T(4,128)}, u32[]{:S(2)}) copy-start(f32[3,2048]{1,0:T(4,128)} %param.13) | copy-start | bytes 73732
  0.0 14.2 %copy-start.2 = (bf16[2048,256]{1,0:T(8,128)(2,1)S(1)}, bf16[2048,256]{1,0:T(8,128)(2,1)}, u32[]{:S(2)}) copy-start(bf16[2048,256]{1,0:T(8,128)(2,1)} %feats_ref.3) | copy-start | bytes 3145732
  0.0 13.6 %copy-start.16 = (s32[16,3]{0,1:T(4,128)S(1)}, s32[16,3]{0,1:T(4,128)}, u32[]{:S(2)}) copy-start(s32[16,3]{0,1:T(4,128)} %param.15) | copy-start | bytes 580
  0.0 13.7 %copy-start.19 = (f32[4]{0:T(128)S(1)}, f32[4]{0:T(128)}, u32[]{:S(2)}) copy-start(f32[4]{0:T(128)} %param.18) | copy-start | bytes 52
  0.0 32.8 %collective-permute-start = (f32[3,2048]{1,0:T(4,128)}, f32[3,2048]{1,0:T(4,128)S(1)}, u32[]{:S(2)}, u32[]{:S(2)}) collective-permute-start(f32[3,2048]{1,0:T(4,128)} %param.16), channel_id=1, source_target_pairs={{0,1},{1,0},{2,3},{3,2},{4,5},{5,4},{6,7},{7,6},{8,9},{9,8},{10,11... | collective-permute-start | bytes 73736 | tf_op jit(solution)/shard_map/ppermute | solution.py:342
  4.5 13.4 %collective-permute-start.1 = (f32[8,2048]{1,0:T(8,128)S(1)}, f32[8,2048]{1,0:T(8,128)S(1)}, u32[]{:S(2)}, u32[]{:S(2)}) collective-permute-start(f32[8,2048]{1,0:T(8,128)S(1)} %select_maximum_fusion.2.own_pos), channel_id=1, source_target_pairs={{0,2},{2,0},{4,6},{6,4},{8,10},{10,8},{12,14},{14,12},{16,18},{18,... | collective-permute-start | bytes 196616 | tf_op jit(solution)/shard_map/ppermute | solution.py:347
  7.6 8.2 %copy-start.13 = (bf16[512,512]{1,0:T(8,128)(2,1)S(1)}, bf16[512,512]{1,0:T(8,128)(2,1)}, u32[]{:S(2)}) copy-start(bf16[512,512]{1,0:T(8,128)(2,1)} %param.22) | copy-start | bytes 1572868
  7.6 38.1 %collective-permute-start.2 = (bf16[2048,256]{1,0:T(8,128)(2,1)}, bf16[2048,256]{1,0:T(8,128)(2,1)}, u32[]{:S(2)}, u32[]{:S(2)}) collective-permute-start(bf16[2048,256]{1,0:T(8,128)(2,1)} %broadcast_select_fusion.own_ref), channel_id=1, source_target_pairs={{0,2},{2,0},{4,6},{6,4},{8,10},{10,8},{12,14},{14,12},{16,18},{18,... | collective-permute-start | bytes 3145736 | tf_op jit(solution)/shard_map/ppermute | solution.py:347
  9.0 6.9 %copy-start.6 = (bf16[512,512]{1,0:T(8,128)(2,1)S(1)}, bf16[512,512]{1,0:T(8,128)(2,1)}, u32[]{:S(2)}) copy-start(bf16[512,512]{1,0:T(8,128)(2,1)} %in_ref.3) | copy-start | bytes 1572868
  9.0 31.4 %collective-permute-start.6 = (f32[128,256]{1,0:T(8,128)S(1)}, f32[128,256]{1,0:T(8,128)S(1)}, u32[]{:S(2)}, u32[]{:S(2)}) collective-permute-start(f32[128,256]{1,0:T(8,128)S(1)} %pad_maximum_fusion.5), channel_id=1, source_target_pairs={{0,1},{1,0},{2,3},{3,2},{4,5},{5,4},{6,7},{7,6},{8,9},{9,8},{10,11... | collective-permute-start | bytes 393224 | tf_op jit(solution)/shard_map/ppermute | solution.py:342
  9.2 8.6 %collective-permute-start.26 = (f32[3,256]{1,0:T(4,128)S(1)}, f32[3,256]{1,0:T(4,128)S(1)}, u32[]{:S(2)}, u32[]{:S(2)}) collective-permute-start(f32[3,256]{1,0:T(4,128)S(1)} %get-tuple-element.50), channel_id=1, source_target_pairs={{2,0},{4,2},{6,4},{8,6},{10,8},{12,10},{14,12},{16,14},{18,16},{20... | collective-permute-start | bytes 9224 | tf_op jit(solution)/shard_map/ppermute | solution.py:404
  14.7 2.1 %copy-start.18 = (f32[3,1]{0,1:T(1,128)S(1)}, f32[3,1]{0,1:T(1,128)}, u32[]{:S(2)}) copy-start(f32[3,1]{0,1:T(1,128)} %constant.53.clone) | copy-start | bytes 40
  14.7 3.3 %copy-start.17 = (s32[16]{0:T(128)S(1)}, s32[16]{0:T(128)}, u32[]{:S(2)}) copy-start(s32[16]{0:T(128)} %param.14) | copy-start | bytes 196
  14.7 1.0 copy-start.3
  17.8 5.8 %collective-permute-start.25 = (f32[3,256]{1,0:T(4,128)S(1)}, f32[3,256]{1,0:T(4,128)S(1)}, u32[]{:S(2)}, u32[]{:S(2)}) collective-permute-start(f32[3,256]{1,0:T(4,128)S(1)} %get-tuple-element.49), channel_id=1, source_target_pairs={{0,2},{2,4},{4,6},{6,8},{8,10},{10,12},{12,14},{14,16},{16,18},{18... | collective-permute-start | bytes 9224 | tf_op jit(solution)/shard_map/ppermute | solution.py:403
  18.0 22.6 %copy-start.8 = (f32[8,2048]{1,0:T(8,128)}, f32[8,2048]{1,0:T(8,128)S(1)}, u32[]{:S(2)}) copy-start(f32[8,2048]{1,0:T(8,128)S(1)} %collective-permute-done.1.other_pos) | copy-start | bytes 196612
  18.0 22.5 %collective-permute-start.27 = (bf16[256,256]{1,0:T(8,128)(2,1)S(1)}, bf16[256,256]{1,0:T(8,128)(2,1)S(1)}, u32[]{:S(2)}, u32[]{:S(2)}) collective-permute-start(bf16[256,256]{1,0:T(8,128)(2,1)S(1)} %bitcast.41), channel_id=1, source_target_pairs={{0,2},{2,4},{4,6},{6,8},{8,10},{10,12},{12,14},{14,16},{16,18},{18... | collective-permute-start | bytes 393224 | tf_op jit(solution)/shard_map/ppermute | solution.py:401
  24.2 3.7 %collective-permute-start.7 = (f32[8,128]{1,0:T(8,128)S(1)}, f32[8,128]{1,0:T(8,128)S(1)}, u32[]{:S(2)}, u32[]{:S(2)}) collective-permute-start(f32[8,128]{1,0:T(8,128)S(1)} %broadcast_in_dim.34), channel_id=1, source_target_pairs={{0,4},{2,6},{4,0},{6,2},{8,12},{10,14},{12,8},{14,10},{16,20},{18,... | collective-permute-start | bytes 12296 | tf_op jit(solution)/shard_map/ppermute | solution.py:347
  28.5 3.7 %collective-permute-start.8 = (f32[8,128]{1,0:T(8,128)S(1)}, f32[8,128]{1,0:T(8,128)S(1)}, u32[]{:S(2)}, u32[]{:S(2)}) collective-permute-start(f32[8,128]{1,0:T(8,128)S(1)} %broadcast_add_fusion.2), channel_id=1, source_target_pairs={{0,8},{2,10},{4,12},{6,14},{8,0},{10,2},{12,4},{14,6},{16,24},{18,... | collective-permute-start | bytes 12296 | tf_op jit(solution)/shard_map/ppermute | solution.py:347
  32.2 8.3 %collective-permute-start.28 = (bf16[256,256]{1,0:T(8,128)(2,1)S(1)}, bf16[256,256]{1,0:T(8,128)(2,1)S(1)}, u32[]{:S(2)}, u32[]{:S(2)}) collective-permute-start(bf16[256,256]{1,0:T(8,128)(2,1)S(1)} %bitcast.40), channel_id=1, source_target_pairs={{2,0},{4,2},{6,4},{8,6},{10,8},{12,10},{14,12},{16,14},{18,16},{20... | collective-permute-start | bytes 393224 | tf_op jit(solution)/shard_map/ppermute | solution.py:402
  32.9 4.6 %collective-permute-start.9 = (f32[8,128]{1,0:T(8,128)S(1)}, f32[8,128]{1,0:T(8,128)S(1)}, u32[]{:S(2)}, u32[]{:S(2)}) collective-permute-start(f32[8,128]{1,0:T(8,128)S(1)} %fusion.14), channel_id=1, source_target_pairs={{0,16},{2,18},{4,20},{6,22},{8,24},{10,26},{12,28},{14,30},{16,0},... | collective-permute-start | bytes 12296 | tf_op jit(solution)/shard_map/ppermute | solution.py:347
  37.4 128.8 %collective-permute-start.31 = (bf16[512,768]{1,0:T(8,128)(2,1)}, bf16[512,768]{1,0:T(8,128)(2,1)S(1)}, u32[]{:S(2)}, u32[]{:S(2)}) collective-permute-start(bf16[512,768]{1,0:T(8,128)(2,1)} %pad_maximum_fusion), channel_id=1, source_target_pairs={{0,1},{1,0},{2,3},{3,2},{4,5},{5,4},{6,7},{7,6},{8,9},{9,8},{10,11... | collective-permute-start | bytes 2359304 | tf_op jit(solution)/shard_map/ppermute | solution.py:342
  40.5 1.2 copy-start.4
  41.7 0.7 copy-start.11
  42.4 3.3 %copy-start.9 = (f32[8,2048]{1,0:T(8,128)S(1)}, f32[8,2048]{1,0:T(8,128)}, u32[]{:S(2)}) copy-start(f32[8,2048]{1,0:T(8,128)} %copy-done.8) | copy-start | bytes 196612
  52.1 40.2 %collective-permute-start.3 = (bf16[2,256,256]{2,1,0:T(8,128)(2,1)S(1)}, bf16[2,256,256]{2,1,0:T(8,128)(2,1)S(1)}, u32[]{:S(2)}, u32[]{:S(2)}) collective-permute-start(bf16[2,256,256]{2,1,0:T(8,128)(2,1)S(1)} %get-tuple-element.28), channel_id=1, source_target_pairs={{0,4},{2,6},{4,0},{6,2},{8,12},{10,14},{12,8},{14,10},{16,20},{18,... | collective-permute-start | bytes 786440 | tf_op jit(solution)/shard_map/ppermute | solution.py:347
  58.5 36.2 %collective-permute-start.13 = (bf16[2,256,256]{2,1,0:T(8,128)(2,1)S(1)}, bf16[2,256,256]{2,1,0:T(8,128)(2,1)S(1)}, u32[]{:S(2)}, u32[]{:S(2)}) collective-permute-start(bf16[2,256,256]{2,1,0:T(8,128)(2,1)S(1)} %get-tuple-element.34), channel_id=1, source_target_pairs={{0,4},{2,6},{4,0},{6,2},{8,12},{10,14},{12,8},{14,10},{16,20},{18,... | collective-permute-start | bytes 786440 | tf_op jit(solution)/shard_map/ppermute | solution.py:347
  69.9 22.5 %collective-permute-start.19 = (bf16[2,512,256]{2,1,0:T(8,128)(2,1)S(1)}, bf16[2,512,256]{2,1,0:T(8,128)(2,1)S(1)}, u32[]{:S(2)}, u32[]{:S(2)}) collective-permute-start(bf16[2,512,256]{2,1,0:T(8,128)(2,1)S(1)} %get-tuple-element.40), channel_id=1, source_target_pairs={{0,4},{2,6},{4,0},{6,2},{8,12},{10,14},{12,8},{14,10},{16,20},{18,... | collective-permute-start | bytes 1572872 | tf_op jit(solution)/shard_map/ppermute | solution.py:347
  92.4 7.1 %collective-permute-start.4 = (bf16[2,128,256]{2,1,0:T(8,128)(2,1)S(1)}, bf16[2,128,256]{2,1,0:T(8,128)(2,1)S(1)}, u32[]{:S(2)}, u32[]{:S(2)}) collective-permute-start(bf16[2,128,256]{2,1,0:T(8,128)(2,1)S(1)} %slice.144), channel_id=1, source_target_pairs={{0,8},{2,10},{4,12},{6,14},{8,0},{10,2},{12,4},{14,6},{16,24},{18,... | collective-permute-start | bytes 393224 | tf_op jit(solution)/shard_map/ppermute | solution.py:347
  92.6 11.6 %collective-permute-start.20 = (bf16[2,256,256]{2,1,0:T(8,128)(2,1)S(1)}, bf16[2,256,256]{2,1,0:T(8,128)(2,1)S(1)}, u32[]{:S(2)}, u32[]{:S(2)}) collective-permute-start(bf16[2,256,256]{2,1,0:T(8,128)(2,1)S(1)} %slice.141), channel_id=1, source_target_pairs={{0,8},{2,10},{4,12},{6,14},{8,0},{10,2},{12,4},{14,6},{16,24},{18,... | collective-permute-start | bytes 786440 | tf_op jit(solution)/shard_map/ppermute | solution.py:347
  94.7 12.2 %collective-permute-start.14 = (bf16[2,128,256]{2,1,0:T(8,128)(2,1)S(1)}, bf16[2,128,256]{2,1,0:T(8,128)(2,1)S(1)}, u32[]{:S(2)}, u32[]{:S(2)}) collective-permute-start(bf16[2,128,256]{2,1,0:T(8,128)(2,1)S(1)} %slice.143), channel_id=1, source_target_pairs={{0,8},{2,10},{4,12},{6,14},{8,0},{10,2},{12,4},{14,6},{16,24},{18,... | collective-permute-start | bytes 393224 | tf_op jit(solution)/shard_map/ppermute | solution.py:347
  99.5 15.7 %collective-permute-start.5 = (bf16[2,64,256]{2,1,0:T(8,128)(2,1)S(1)}, bf16[2,64,256]{2,1,0:T(8,128)(2,1)S(1)}, u32[]{:S(2)}, u32[]{:S(2)}) collective-permute-start(bf16[2,64,256]{2,1,0:T(8,128)(2,1)S(1)} %slice.146), channel_id=1, source_target_pairs={{0,16},{2,18},{4,20},{6,22},{8,24},{10,26},{12,28},{14,30},{16,0},... | collective-permute-start | bytes 196616 | tf_op jit(solution)/shard_map/ppermute | solution.py:347
  104.2 30.6 %copy-start.5 = (bf16[16,128,256]{2,1,0:T(8,128)(2,1)S(1)}, bf16[16,128,256]{2,1,0:T(8,128)(2,1)}, u32[]{:S(2)}) copy-start(bf16[16,128,256]{2,1,0:T(8,128)(2,1)} %copy-done.3) | copy-start | bytes 3145732
  104.2 30.6 %copy-start.12 = (f32[4]{0:T(128)S(1)}, f32[4]{0:T(128)}, u32[]{:S(2)}) copy-start(f32[4]{0:T(128)} %broadcast_multiply_fusion.5.scales) | copy-start | bytes 52
  104.2 10.9 %collective-permute-start.21 = (bf16[2,128,256]{2,1,0:T(8,128)(2,1)S(1)}, bf16[2,128,256]{2,1,0:T(8,128)(2,1)S(1)}, u32[]{:S(2)}, u32[]{:S(2)}) collective-permute-start(bf16[2,128,256]{2,1,0:T(8,128)(2,1)S(1)} %slice.142), channel_id=1, source_target_pairs={{0,16},{2,18},{4,20},{6,22},{8,24},{10,26},{12,28},{14,30},{16,0},... | collective-permute-start | bytes 393224 | tf_op jit(solution)/shard_map/ppermute | solution.py:347
  106.9 15.8 %collective-permute-start.15 = (bf16[2,64,256]{2,1,0:T(8,128)(2,1)S(1)}, bf16[2,64,256]{2,1,0:T(8,128)(2,1)S(1)}, u32[]{:S(2)}, u32[]{:S(2)}) collective-permute-start(bf16[2,64,256]{2,1,0:T(8,128)(2,1)S(1)} %slice.145), channel_id=1, source_target_pairs={{0,16},{2,18},{4,20},{6,22},{8,24},{10,26},{12,28},{14,30},{16,0},... | collective-permute-start | bytes 196616 | tf_op jit(solution)/shard_map/ppermute | solution.py:347
  115.2 7.5 %collective-permute-start.22 = (bf16[2,128,256]{2,1,0:T(8,128)(2,1)S(1)}, bf16[2,128,256]{2,1,0:T(8,128)(2,1)S(1)}, u32[]{:S(2)}, u32[]{:S(2)}) collective-permute-start(bf16[2,128,256]{2,1,0:T(8,128)(2,1)S(1)} %fusion.1), channel_id=1, source_target_pairs={{0,16},{2,18},{4,20},{6,22},{8,24},{10,26},{12,28},{14,30},{16,0},... | collective-permute-start | bytes 393224 | tf_op jit(solution)/shard_map/ppermute | solution.py:347
  115.3 9.9 %collective-permute-start.10 = (bf16[2,64,256]{2,1,0:T(8,128)(2,1)S(1)}, bf16[2,64,256]{2,1,0:T(8,128)(2,1)S(1)}, u32[]{:S(2)}, u32[]{:S(2)}) collective-permute-start(bf16[2,64,256]{2,1,0:T(8,128)(2,1)S(1)} %fusion.5), channel_id=1, source_target_pairs={{0,16},{2,18},{4,20},{6,22},{8,24},{10,26},{12,28},{14,30},{16,0},... | collective-permute-start | bytes 196616 | tf_op jit(solution)/shard_map/ppermute | solution.py:347
  122.7 9.9 %collective-permute-start.23 = (bf16[2,256,256]{2,1,0:T(8,128)(2,1)S(1)}, bf16[2,256,256]{2,1,0:T(8,128)(2,1)S(1)}, u32[]{:S(2)}, u32[]{:S(2)}) collective-permute-start(bf16[2,256,256]{2,1,0:T(8,128)(2,1)S(1)} %pad_maximum_fusion.4), channel_id=1, source_target_pairs={{0,8},{2,10},{4,12},{6,14},{8,0},{10,2},{12,4},{14,6},{16,24},{18,... | collective-permute-start | bytes 786440 | tf_op jit(solution)/shard_map/ppermute | solution.py:347
  122.8 7.6 %collective-permute-start.16 = (bf16[2,64,256]{2,1,0:T(8,128)(2,1)S(1)}, bf16[2,64,256]{2,1,0:T(8,128)(2,1)S(1)}, u32[]{:S(2)}, u32[]{:S(2)}) collective-permute-start(bf16[2,64,256]{2,1,0:T(8,128)(2,1)S(1)} %fusion.3), channel_id=1, source_target_pairs={{0,16},{2,18},{4,20},{6,22},{8,24},{10,26},{12,28},{14,30},{16,0},... | collective-permute-start | bytes 196616 | tf_op jit(solution)/shard_map/ppermute | solution.py:347
  125.2 12.9 %collective-permute-start.11 = (bf16[2,128,256]{2,1,0:T(8,128)(2,1)S(1)}, bf16[2,128,256]{2,1,0:T(8,128)(2,1)S(1)}, u32[]{:S(2)}, u32[]{:S(2)}) collective-permute-start(bf16[2,128,256]{2,1,0:T(8,128)(2,1)S(1)} %pad_maximum_fusion.6), channel_id=1, source_target_pairs={{0,8},{2,10},{4,12},{6,14},{8,0},{10,2},{12,4},{14,6},{16,24},{18,... | collective-permute-start | bytes 393224 | tf_op jit(solution)/shard_map/ppermute | solution.py:347
  130.5 7.7 %collective-permute-start.17 = (bf16[2,128,256]{2,1,0:T(8,128)(2,1)S(1)}, bf16[2,128,256]{2,1,0:T(8,128)(2,1)S(1)}, u32[]{:S(2)}, u32[]{:S(2)}) collective-permute-start(bf16[2,128,256]{2,1,0:T(8,128)(2,1)S(1)} %pad_maximum_fusion.7), channel_id=1, source_target_pairs={{0,8},{2,10},{4,12},{6,14},{8,0},{10,2},{12,4},{14,6},{16,24},{18,... | collective-permute-start | bytes 393224 | tf_op jit(solution)/shard_map/ppermute | solution.py:347
  132.7 14.4 %collective-permute-start.24 = (bf16[2,512,256]{2,1,0:T(8,128)(2,1)S(1)}, bf16[2,512,256]{2,1,0:T(8,128)(2,1)S(1)}, u32[]{:S(2)}, u32[]{:S(2)}) collective-permute-start(bf16[2,512,256]{2,1,0:T(8,128)(2,1)S(1)} %pad_maximum_fusion.1.refs_4_), channel_id=1, source_target_pairs={{0,4},{2,6},{4,0},{6,2},{8,12},{10,14},{12,8},{14,10},{16,20},{18,... | collective-permute-start | bytes 1572872 | tf_op jit(solution)/shard_map/ppermute | solution.py:347
  138.1 16.3 %collective-permute-start.12 = (bf16[2,256,256]{2,1,0:T(8,128)(2,1)S(1)}, bf16[2,256,256]{2,1,0:T(8,128)(2,1)S(1)}, u32[]{:S(2)}, u32[]{:S(2)}) collective-permute-start(bf16[2,256,256]{2,1,0:T(8,128)(2,1)S(1)} %pad_maximum_fusion.2.refs_4_), channel_id=1, source_target_pairs={{0,4},{2,6},{4,0},{6,2},{8,12},{10,14},{12,8},{14,10},{16,20},{18,... | collective-permute-start | bytes 786440 | tf_op jit(solution)/shard_map/ppermute | solution.py:347
  138.2 14.5 %collective-permute-start.18 = (bf16[2,256,256]{2,1,0:T(8,128)(2,1)S(1)}, bf16[2,256,256]{2,1,0:T(8,128)(2,1)S(1)}, u32[]{:S(2)}, u32[]{:S(2)}) collective-permute-start(bf16[2,256,256]{2,1,0:T(8,128)(2,1)S(1)} %pad_maximum_fusion.3.refs_4_), channel_id=1, source_target_pairs={{0,4},{2,6},{4,0},{6,2},{8,12},{10,14},{12,8},{14,10},{16,20},{18,... | collective-permute-start | bytes 786440 | tf_op jit(solution)/shard_map/ppermute | solution.py:347
  155.4 9.1 %collective-permute-start.29 = (bf16[1024,256]{1,0:T(8,128)(2,1)S(1)}, bf16[1024,256]{1,0:T(8,128)(2,1)S(1)}, u32[]{:S(2)}, u32[]{:S(2)}) collective-permute-start(bf16[1024,256]{1,0:T(8,128)(2,1)S(1)} %messages.13), channel_id=1, source_target_pairs={{0,2},{2,0},{4,6},{6,4},{8,10},{10,8},{12,14},{14,12},{16,18},{18,... | collective-permute-start | bytes 1572872 | tf_op jit(solution)/shard_map/ppermute | solution.py:347
  156.5 6.2 %collective-permute-start.32 = (bf16[1024,256]{1,0:T(8,128)(2,1)S(1)}, bf16[1024,256]{1,0:T(8,128)(2,1)S(1)}, u32[]{:S(2)}, u32[]{:S(2)}) collective-permute-start(bf16[1024,256]{1,0:T(8,128)(2,1)S(1)} %messages.15), channel_id=1, source_target_pairs={{0,2},{2,0},{4,6},{6,4},{8,10},{10,8},{12,14},{14,12},{16,18},{18,... | collective-permute-start | bytes 1572872 | tf_op jit(solution)/shard_map/ppermute | solution.py:347
  162.9 14.9 %collective-permute-start.33 = (bf16[1024,256]{1,0:T(8,128)(2,1)S(1)}, bf16[1024,256]{1,0:T(8,128)(2,1)S(1)}, u32[]{:S(2)}, u32[]{:S(2)}) collective-permute-start(bf16[1024,256]{1,0:T(8,128)(2,1)S(1)} %add_convert_fusion), channel_id=1, source_target_pairs={{0,1},{1,0},{2,3},{3,2},{4,5},{5,4},{6,7},{7,6},{8,9},{9,8},{10,11... | collective-permute-start | bytes 1572872 | tf_op jit(solution)/shard_map/ppermute | solution.py:342
  164.5 13.2 %copy-start.7 = (bf16[512,512]{1,0:T(8,128)(2,1)S(1)}, bf16[512,512]{1,0:T(8,128)(2,1)}, u32[]{:S(2)}) copy-start(bf16[512,512]{1,0:T(8,128)(2,1)} %in_ref.3) | copy-start | bytes 1572868
  164.5 13.2 %copy-start.10 = (f32[512]{0:T(512)S(1)}, f32[512]{0:T(512)}, u32[]{:S(2)}) copy-start(f32[512]{0:T(512)} %param.20) | copy-start | bytes 6148
  164.7 23.4 %collective-permute-start.30 = (bf16[1024,256]{1,0:T(8,128)(2,1)S(1)}, bf16[1024,256]{1,0:T(8,128)(2,1)S(1)}, u32[]{:S(2)}, u32[]{:S(2)}) collective-permute-start(bf16[1024,256]{1,0:T(8,128)(2,1)S(1)} %add_convert_fusion.1), channel_id=1, source_target_pairs={{0,1},{1,0},{2,3},{3,2},{4,5},{5,4},{6,7},{7,6},{8,9},{9,8},{10,11... | collective-permute-start | bytes 1572872 | tf_op jit(solution)/shard_map/ppermute | solution.py:342
  188.0 3.1 %copy-start.1 = (f32[4,512]{1,0:T(4,128)S(1)}, f32[4,512]{1,0:T(4,128)}, u32[]{:S(2)}) copy-start(f32[4,512]{1,0:T(4,128)} %param.19) | copy-start | bytes 24580
